TPU v7x, 128 devices: a whole 4x4x4 slice. The times are simulated.
128 devices in a mesh: req: 8 (over y, z_hi), mlp: 16 (over z_lo, x, core).
Axes of the slice: x: 4, y: 4, z: 4 (z_hi: 2, z_lo: 2; z = z_hi * 2 + z_lo), core: 2. Of those that a mesh axis runs over, the one named last changes fastest.
Arguments:
- prompt_tokens: bfloat16 [16, 1024, 2048], P('req', None, 'mlp'), may hold values from -6 to 6
- decode_tokens: bfloat16 [32, 2048], P('req', 'mlp'), may hold values from -6 to 6
- prompt_lengths: int32 [16], P('req'), may hold values from 128 to 1024, as said below
- decode_states: float32 [32, 16, 128, 128], P('req', 'mlp'), may hold values from -6 to 6
- w_fio: float32 [2048, 6144], P('req', 'mlp'), may hold values from -0.125 to 0.125
- forget_bias: float32 [2048], P('mlp'), as said below
- head_gain: float32 [2048], P('mlp'), may hold values from 0.1 to 1.9
- w_out: float32 [2048, 2048], P('mlp', 'req'), may hold values from -0.125 to 0.125
- mlp_gain: float32 [2048], replicated, may hold values from 0.1 to 1.9
- w_gu: float32 [2048, 11264], P('req', 'mlp'), may hold values from -0.125 to 0.125
- w_down: float32 [5632, 2048], P('mlp', 'req'), may hold values from -0.078125 to 0.078125
Outputs:
- prompt_out: bfloat16 [16, 1024, 2048], P('req', None, 'mlp')
- decode_out: bfloat16 [32, 2048], P('req', 'mlp')
- prompt_states: float32 [16, 16, 128, 128], P('req', 'mlp')
- decode_next: float32 [32, 16, 128, 128], P('req', 'mlp')
Inputs may be any that keep to these rules, and one draw needn't show every extreme that they name: `prompt_lengths`: slots at or past a prompt's length are padding; one prompt has length 1024 and another 1024 // 8. `forget_bias`: every entry is at least 3 and at most ln(1024) + 1.7.
All inputs are finite; a program needn't handle non-finite values.
Results may differ from a plain program's by a relative error of at most 0.02.
Values may be sent and summed in bfloat16 or wider, within the bound.
No kernel may reach another device: no remote copies, remote signals or barrier semaphores. Data moves between devices by JAX's collectives and lax.ppermute only.
A program may use at most 128 MiB of HBM per device.

v0:
```python
import jax
import jax.numpy as jnp
from jax import lax
from jax.sharding import PartitionSpec as P

BLOCK = 64


epsilon = 1e-05


def add_columns(operand, weights_piece):
    return jnp.dot(operand, weights_piece, preferred_element_type=jnp.float32)


def project_output(source_rows, weights):
    return jnp.dot(
        source_rows,
        lax.all_gather(weights, "req", axis=1, tiled=True),
        preferred_element_type=jnp.float32,
    )


def block_step(carried, forget_block, value_block, query_block, start_row, lengths):
    steps_here = forget_block.shape[1]
    positions = start_row + jnp.arange(steps_here, dtype=jnp.int32)
    alive_mask = (positions[None, :] < lengths[:, None])[:, :, None, None]
    log_forget = jnp.where(alive_mask, jax.nn.log_sigmoid(forget_block), 0.0)
    key_gate = jnp.where(alive_mask, jax.nn.sigmoid(-forget_block), 0.0)
    cumulated = jnp.cumsum(log_forget, axis=1)
    query_tilde = query_block * jnp.exp(cumulated)
    key_tilde = key_gate * jnp.exp(-cumulated)
    scores = jnp.einsum("pthc,pshc->phts", query_tilde, key_tilde, precision=lax.Precision.HIGHEST)
    triangle = jnp.arange(steps_here)[:, None] >= jnp.arange(steps_here)[None, :]
    scores = jnp.where(triangle, scores, 0.0)
    emitted = jnp.einsum("phts,pshv->pthv", scores, value_block, precision=lax.Precision.HIGHEST)
    emitted = emitted + jnp.einsum(
        "pthc,phcv->pthv", query_tilde, carried, precision=lax.Precision.HIGHEST
    )
    emitted = jnp.where(alive_mask, emitted, 0.0)
    last_log = cumulated[:, -1]
    key_decayed = key_gate * jnp.exp(last_log[:, None] - cumulated)
    carried = jnp.exp(last_log)[..., None] * carried + jnp.einsum(
        "pthc,pthv->phcv", key_decayed, value_block, precision=lax.Precision.HIGHEST
    )
    return (carried, emitted)


def on_device(
    prompt_tokens,
    decode_tokens,
    prompt_lengths,
    decode_states,
    w_fio,
    forget_bias,
    head_gain,
    w_out,
    mlp_gain,
    w_gu,
    w_down,
):
    prompts_here, plen, feature_part = prompt_tokens.shape
    heads_here = decode_states.shape[1]
    head_size = decode_states.shape[2]
    prompt_rows = prompts_here * plen
    local_rows = jnp.concatenate(
        [prompt_tokens.reshape(prompt_rows, feature_part), decode_tokens], axis=0
    )
    row_count = local_rows.shape[0]
    x_full = lax.all_gather(local_rows, "mlp", axis=1, tiled=True)
    model_width = x_full.shape[1]
    mixing = add_columns(
        x_full, lax.all_gather(w_fio.astype(jnp.bfloat16), "req", axis=0, tiled=True)
    )
    mixing = mixing.reshape(row_count, heads_here, 3, head_size)
    bias_table = forget_bias.reshape(heads_here, head_size)
    forget_logit = mixing[:, :, 0] + bias_table
    values = mixing[:, :, 1]
    queries = mixing[:, :, 2]
    prompt_forget = forget_logit[:prompt_rows].reshape(prompts_here, plen, heads_here, head_size)
    prompt_values = values[:prompt_rows].reshape(prompts_here, plen, heads_here, head_size)
    prompt_queries = queries[:prompt_rows].reshape(prompts_here, plen, heads_here, head_size)
    start_state = jnp.zeros((prompts_here, heads_here, head_size, head_size), jnp.float32)
    block_total = plen // BLOCK

    def to_blocks(source_array):
        return source_array.reshape(
            prompts_here, block_total, BLOCK, heads_here, head_size
        ).transpose(1, 0, 2, 3, 4)

    def scan_block(carried, inputs):
        forget_block, value_block, query_block, start_row = inputs
        return block_step(
            carried, forget_block, value_block, query_block, start_row, prompt_lengths
        )

    starts = jnp.arange(block_total, dtype=jnp.int32) * BLOCK
    prompt_states, block_outputs = lax.scan(
        scan_block,
        start_state,
        (to_blocks(prompt_forget), to_blocks(prompt_values), to_blocks(prompt_queries), starts),
    )
    prompt_mixed = block_outputs.transpose(1, 0, 2, 3, 4).reshape(
        prompts_here, plen, heads_here, head_size
    )
    decode_logit = forget_logit[prompt_rows:]
    decode_next = (
        jax.nn.sigmoid(decode_logit)[..., None] * decode_states
        + jax.nn.sigmoid(-decode_logit)[..., None] * values[prompt_rows:][:, :, None, :]
    )
    decode_mixed = jnp.einsum(
        "nhcv,nhc->nhv", decode_next, queries[prompt_rows:], precision=lax.Precision.HIGHEST
    )
    mixed_all = jnp.concatenate(
        [prompt_mixed.reshape(prompt_rows, heads_here, head_size), decode_mixed], axis=0
    )
    mean_square = jnp.mean(mixed_all * mixed_all, axis=-1, keepdims=True)
    head_rows = (
        mixed_all * lax.rsqrt(mean_square + epsilon) * head_gain.reshape(heads_here, head_size)
    ).astype(jnp.bfloat16)
    head_rows = head_rows.reshape(row_count, heads_here * head_size)
    offset = lax.axis_index("mlp") * feature_part
    head_terms = project_output(head_rows, w_out.astype(jnp.bfloat16))
    attention = lax.psum_scatter(
        head_terms.astype(jnp.bfloat16), "mlp", scatter_dimension=1, tiled=True
    ).astype(jnp.float32)
    residual = (local_rows.astype(jnp.float32) + attention).astype(jnp.bfloat16)
    residual_wide = residual.astype(jnp.float32)
    square_sum = lax.psum(jnp.sum(residual_wide * residual_wide, axis=1), "mlp")
    row_scale = lax.rsqrt(square_sum / model_width + epsilon)[:, None]
    gain_part = lax.dynamic_slice_in_dim(mlp_gain, offset, feature_part)
    normed_part = (residual_wide * row_scale * gain_part).astype(jnp.bfloat16)
    normed = lax.all_gather(normed_part, "mlp", axis=1, tiled=True)
    gate_up = add_columns(
        normed, lax.all_gather(w_gu.astype(jnp.bfloat16), "req", axis=0, tiled=True)
    )
    hidden_here = w_gu.shape[1] // 2
    hidden = (jax.nn.silu(gate_up[:, :hidden_here]) * gate_up[:, hidden_here:]).astype(jnp.bfloat16)
    down_terms = jnp.dot(
        hidden,
        lax.all_gather(w_down.astype(jnp.bfloat16), "req", axis=1, tiled=True),
        preferred_element_type=jnp.float32,
    )
    down_share = lax.psum_scatter(
        down_terms.astype(jnp.bfloat16), "mlp", scatter_dimension=1, tiled=True
    ).astype(jnp.float32)
    layer_output = (residual_wide + down_share).astype(jnp.bfloat16)
    prompt_out = layer_output[:prompt_rows].reshape(prompts_here, plen, feature_part)
    decode_out = layer_output[prompt_rows:]
    return (prompt_out, decode_out, prompt_states, decode_next)


def solution(mesh):
    placed = (
        P("req", None, "mlp"),
        P("req", "mlp"),
        P("req"),
        P("req", "mlp", None, None),
        P("req", "mlp"),
        P("mlp"),
        P("mlp"),
        P("mlp", "req"),
        P(),
        P("req", "mlp"),
        P("mlp", "req"),
    )
    return jax.shard_map(
        on_device,
        mesh=mesh,
        in_specs=placed,
        out_specs=(
            P("req", None, "mlp"),
            P("req", "mlp"),
            P("req", "mlp", None, None),
            P("req", "mlp", None, None),
        ),
        check_vma=False,
    )
```

profile of v0, /device:TPU:1, one launch (start us, length us, event | category | flops | bytes accessed | tf_op | source)
XLA Modules:
  0.0 634.0 jit_solution(2306237471951861111)
XLA Ops:
  7.2 1.8 convert_element_type.49
  9.1 1.5 pad_maximum_fusion
  10.7 33.1 %all_gather.20 = bf16[128,2048]{1,0:T(8,128)(2,1)} all-gather(bf16[128,256]{1,0:T(8,128)(2,1)S(1)} %convert_element_type.51), channel_id=1, replica_groups=mesh['req'=8,'mlp'=16] {'req'}, dimensions={1}, use_global_device_ids=true | all-gather | bytes 589824 | tf_op jit(solution)/shard_map/all_gather | solution.py:19
  43.8 21.5 %all-gather.8.cloned.1.call-done = bf16[2048,384]{1,0:T(8,128)(2,1)} async-done(((bf16[256,384]{1,0:T(8,128)(2,1)}), bf16[2048,384]{1,0:T(8,128)(2,1)}) %all-gather.8.cloned.1.call-update) | async-done | bytes 1572880 | tf_op jit(solution)/shard_map/all_gather | solution.py:73
  65.3 63.3 %all-gather.6.cloned.1.call-done = bf16[2052,2048]{1,0:T(8,128)(2,1)} async-done(((bf16[2052,128]{1,0:T(8,128)(2,1)}), bf16[2052,2048]{1,0:T(8,128)(2,1)}) %all-gather.6.cloned.1.call-update) | async-done | bytes 8405008 | tf_op jit(solution)/shard_map/all_gather | solution.py:70
  128.6 7.4 %fusion.59 = f32[2052,384]{0,1:T(8,128)S(1)} fusion(bf16[2052,2048]{1,0:T(8,128)(2,1)} %all-gather.6.cloned.1.call-done, bf16[2048,384]{1,0:T(8,128)(2,1)} %all-gather.8.cloned.1.call-done), kind=kOutput, calls=%fused_computation.84 | convolution fusion | flops 3227516928 | bytes 13129728 | tf_op jit(solution)/shard_map/dot_general | solution.py:13
  136.0 1.6 copy-done.3
  138.4 2.2 copy-done.4
  141.9 2.6 copy.47
  144.5 1.3 copy.48
  145.8 108.7 %while.13 = (s32[]{:T(128)}, f32[2,1,128,128]{3,2,0,1:T(8,128)S(1)}, f32[16,2,64,1,128]{4,2,0,1,3:T(8,128)}, s32[16]{0:T(128)S(1)}, s32[2]{0:T(128)S(1)}, /*inde...) while((s32[]{:T(128)}, ...), condition=%wide.region_2.3_spmd.clone, body=%wide.region_0.2_spmd.clone.sunk | while | flops 77050048 | bytes 1596940 | solution.py:98
  147.3 1.2 convolution_select_fusion.2
  149.5 1.7 fusion.93
  151.3 1.3 fusion.91
  154.1 1.2 convolution_select_fusion.2
  156.3 1.7 fusion.93
  158.1 1.3 fusion.91
  160.9 1.2 convolution_select_fusion.2
  163.1 1.7 fusion.93
  164.9 1.3 fusion.91
  167.7 1.2 convolution_select_fusion.2
  169.9 1.7 fusion.93
  171.7 1.3 fusion.91
  174.5 1.2 convolution_select_fusion.2
  176.7 1.7 fusion.93
  178.5 1.3 fusion.91
  181.3 1.2 convolution_select_fusion.2
  183.5 1.7 fusion.93
  185.3 1.3 fusion.91
  190.3 1.7 fusion.93
  192.1 1.3 fusion.91
  197.1 1.7 fusion.93
  198.9 1.3 fusion.91
  203.9 1.7 fusion.93
  205.7 1.3 fusion.91
  210.7 1.7 fusion.93
  212.5 1.3 fusion.91
  217.5 1.7 fusion.93
  219.3 1.3 fusion.91
  224.3 1.7 fusion.93
  226.0 1.3 fusion.91
  231.1 1.7 fusion.93
  232.8 1.3 fusion.91
  237.9 1.7 fusion.93
  239.6 1.3 fusion.91
  244.7 1.7 fusion.93
  246.4 1.3 fusion.91
  251.5 1.7 fusion.93
  253.2 1.3 fusion.91
  255.2 1.6 fusion.49
  256.8 5.6 convolution_convert_fusion.1
  262.5 11.6 %copy.58 = bf16[2052,2048]{0,1:T(8,128)(2,1)} copy(bf16[2052,2048]{1,0:T(8,128)(2,1)} %convolution_convert_fusion.1) | data formatting | bytes 16809984
  276.8 69.0 %reduce-scatter.7.cloned.1.call-done = bf16[128,2052]{1,0:T(8,128)(2,1)} async-done(((bf16[2048,2052]{1,0:T(8,128)(2,1)}), bf16[128,2052]{1,0:T(8,128)(2,1)}) %reduce-scatter.7.cloned.1.call-update) | async-done | bytes 525328
  345.8 1.3 copy.59
  347.5 54.2 %psum.7 = f32[2052]{0:T(1024)S(1)} all-reduce(f32[2052]{0:T(1024)S(1)} %fusion.43), channel_id=1, replica_groups=mesh['req'=8,'mlp'=16] {'mlp'}, use_global_device_ids=true, to_apply=%region_6.7 | all-reduce | flops 2052 | bytes 16416 | tf_op jit(solution)/shard_map/psum | solution.py:129
  401.8 1.2 fusion.45
  404.0 11.7 %all-gather.12.cloned.1.call-done = bf16[2048,704]{0,1:T(8,128)(2,1)} async-done(((bf16[256,704]{0,1:T(8,128)(2,1)}), bf16[2048,704]{0,1:T(8,128)(2,1)}) %all-gather.12.cloned.1.call-update) | async-done | bytes 2883600 | tf_op jit(solution)/shard_map/all_gather | solution.py:135
  415.7 61.9 %all-gather.10.cloned.1.call-done = bf16[2052,2048]{1,0:T(8,128)(2,1)} async-done(((bf16[2052,128]{1,0:T(8,128)(2,1)}), bf16[2052,2048]{1,0:T(8,128)(2,1)}) %all-gather.10.cloned.1.call-update) | async-done | bytes 8405008 | tf_op jit(solution)/shard_map/all_gather | solution.py:133
  477.5 12.6 %fusion.60 = f32[2052,704]{0,1:T(8,128)} fusion(bf16[2052,2048]{1,0:T(8,128)(2,1)} %all-gather.10.cloned.1.call-done, bf16[2048,704]{0,1:T(8,128)(2,1)} %all-gather.12.cloned.1.call-done), kind=kOutput, calls=%fused_computation.85 | convolution fusion | flops 5917114368 | bytes 17067008 | tf_op jit(solution)/shard_map/dot_general | solution.py:13
  490.1 39.5 %all-gather.14.cloned.1.call-done = bf16[352,2048]{1,0:T(8,128)(2,1)} async-done(((bf16[352,256]{1,0:T(8,128)(2,1)}), bf16[352,2048]{1,0:T(8,128)(2,1)}) %all-gather.14.cloned.1.call-update) | async-done | bytes 1441808 | tf_op jit(solution)/shard_map/all_gather | solution.py:141
  529.7 11.1 %convolution_convert_fusion = bf16[2052,2048]{1,0:T(8,128)(2,1)} fusion(bf16[352,2048]{1,0:T(8,128)(2,1)} %all-gather.14.cloned.1.call-done, f32[2052,704]{0,1:T(8,128)} %fusion.60), kind=kOutput, calls=%fused_computation.48 | convolution fusion | flops 2967093504 | bytes 15625216 | tf_op jit(solution)/shard_map/dot_general | solution.py:139
  540.7 11.5 %copy.60 = bf16[2052,2048]{0,1:T(8,128)(2,1)} copy(bf16[2052,2048]{1,0:T(8,128)(2,1)} %convolution_convert_fusion) | data formatting | bytes 16809984
  552.3 71.9 %reduce-scatter.9.cloned.1.call-done = bf16[128,2052]{1,0:T(8,128)(2,1)} async-done(((bf16[2048,2052]{1,0:T(8,128)(2,1)}), bf16[128,2052]{1,0:T(8,128)(2,1)}) %reduce-scatter.9.cloned.1.call-update) | async-done | bytes 525328
  624.2 1.3 copy.61
  (223 shorter events, 60.6 us)
Async XLA Ops:
  7.2 1.9 copy-start
  7.2 3.5 copy-start.11
  7.2 58.1 %all-gather.8.cloned.1.call-start = ((), (), s32[]{:S(2)}) async-start(), calls=%async_computation.3 | async-start | bytes 1769472 | tf_op jit(solution)/shard_map/all_gather | solution.py:73
  9.0 119.5 %all-gather.6.cloned.1.call-start = ((), (), s32[]{:S(2)}) async-start(), calls=%async_computation.2 | async-start | bytes 8947712 | tf_op jit(solution)/shard_map/all_gather | solution.py:70
  10.6 335.2 %reduce-scatter.7.cloned.1.call-start = ((), (), s32[]{:S(2)}) async-start(), calls=%async_computation.7 | async-start | bytes 9469952
  136.0 1.7 copy-start.3
  137.7 0.7 copy-start.14
  138.3 2.3 copy-start.4
  138.4 3.4 copy-start.1
  144.5 1.3 slice-start
  144.5 1.3 copy-start.15
  145.8 108.8 %copy-start.10 = (f32[4,1,128,128]{3,2,1,0:T(8,128)S(1)}, f32[4,1,128,128]{3,2,1,0:T(8,128)}, u32[]{:S(2)}) copy-start(f32[4,1,128,128]{3,2,1,0:T(8,128)} %param.16) | copy-start | bytes 786436
  254.5 7.9 %copy-start.5 = (f32[2,1,128,128]{3,2,0,1:T(8,128)}, f32[2,1,128,128]{3,2,0,1:T(8,128)S(1)}, u32[]{:S(2)}) copy-start(f32[2,1,128,128]{3,2,0,1:T(8,128)S(1)} %get-tuple-element.114) | copy-start | bytes 393220
  254.6 2.3 copy-start.2
  254.6 2.3 copy-start.6
  254.6 2.3 copy-start.13
  254.8 7.7 %copy-start.7 = (f32[4,1,128,128]{3,2,1,0:T(8,128)}, f32[4,1,128,128]{3,2,1,0:T(8,128)S(1)}, u32[]{:S(2)}) copy-start(f32[4,1,128,128]{3,2,1,0:T(8,128)S(1)} %multiply_add_fusion) | copy-start | bytes 786436
  274.0 1.1 copy-start.8
  274.1 73.1 %copy-start.12 = (bf16[4,128]{1,0:T(4,128)(2,1)S(1)}, bf16[4,128]{1,0:T(4,128)(2,1)}, u32[]{:S(2)}) copy-start(bf16[4,128]{1,0:T(4,128)(2,1)} %param.14) | copy-start | bytes 3076
  274.1 141.6 %all-gather.12.cloned.1.call-start = ((), (), s32[]{:S(2)}) async-start(), calls=%async_computation.5 | async-start | bytes 3244032 | tf_op jit(solution)/shard_map/all_gather | solution.py:135
  275.9 201.6 %all-gather.10.cloned.1.call-start = ((), (), s32[]{:S(2)}) async-start(), calls=%async_computation.4 | async-start | bytes 8947712 | tf_op jit(solution)/shard_map/all_gather | solution.py:133
  347.5 55.5 %copy-start.9 = (f32[352,256]{1,0:T(8,128)S(1)}, f32[352,256]{1,0:T(8,128)}, u32[]{:S(2)}) copy-start(f32[352,256]{1,0:T(8,128)} %param.23) | copy-start | bytes 1081348
  403.0 126.7 %all-gather.14.cloned.1.call-start = ((), (), s32[]{:S(2)}) async-start(), calls=%async_computation.6 | async-start | bytes 1622016 | tf_op jit(solution)/shard_map/all_gather | solution.py:141
  403.7 220.5 %reduce-scatter.9.cloned.1.call-start = ((), (), s32[]{:S(2)}) async-start(), calls=%async_computation.8 | async-start | bytes 9469952
Sparse Core Ops, SparseCore 0:
  10.9 54.3 all-gather.7
  66.9 61.6 all-gather.5
  274.2 71.5 reduce-scatter.6
  348.4 67.2 all-gather.11
  417.1 60.3 all-gather.9
  479.6 50.0 all-gather.13
  552.4 71.7 reduce-scatter.8
where the time goes:
time: 641 us; the launch traced here: 634 us
  waiting for transfers between devices  339 us (53%)
  matrix products  121 us (19%)
  blocking collectives  87.3 us (14%)
  local copies, waits for them, and re-layouts  48.2 us (8%)
  other arithmetic  22.7 us (4%)
  between operations  14.4 us (2%)
    unnamed x9, waiting for transfers between devices  141 us
    all_gather x1, waiting for transfers between devices, on_device(): x_full = lax.all_gather(local_rows, 'mlp', axis=1, tiled=True)  63.3 us
    all_gather x1, waiting for transfers between devices, on_device(): normed = lax.all_gather(normed_part, 'mlp', axis=1, tiled=True)  61.9 us
    psum x1, blocking collectives, on_device(): square_sum = lax.psum(jnp.sum(residual_wide * residual_wide, axis=1), 'mlp')  54.2 us
    all_gather x1, waiting for transfers between devices, on_device(): lax.all_gather(w_down.astype(jnp.bfloat16), 'req', axis=1, tiled=True)  39.5 us
    all_gather x1, blocking collectives, project_output(): lax.all_gather(weights, 'req', axis=1, tiled=True)  33.1 us
    unnamed x37, local copies, waits for them, and re-layouts  31.3 us
    dot_general x16, matrix products, block_step(): jnp.einsum('pthc,phcv->pthv', query_tilde, carried, precision=lax.Precisi...  27.6 us
  transfers between devices with their start and end apart: 7, of which 7 were waited for; matrix products, arithmetic and copies ran while one was open for 3% of the time, Pallas kernels for 0%

commit v1 on v0

v1 whole, which is shorter than its diff:
```python
import functools

import jax
import jax.numpy as jnp
import numpy as np
from jax import lax
from jax.experimental import pallas as pl
from jax.experimental.pallas import tpu as pltpu
from jax.sharding import Mesh, PartitionSpec as P

EPS = 1e-5
HALF = 528
CH = 128
LEVELS = 7
BF = jnp.bfloat16
F32 = jnp.float32
SIZES = {"y": 4, "zh": 2, "zl": 2, "x": 4, "c": 2}
VMEM_LIMIT = 60 * 1024 * 1024


def shift(value, axis, step):
    n = SIZES[axis]
    return lax.ppermute(value, axis, [(i, (i + step) % n) for i in range(n)])


def ring_gather(own, axis):
    n = own.shape[0] // 2
    before = shift(own, axis, 1)
    ahead = shift(own, axis, -1)
    far0 = shift(before[:n], axis, 1)
    far1 = shift(ahead[n:], axis, -1)
    return [own, ahead, far0, far1, before]


def piece(refs, step, part, parts=2):
    if step == 2:
        n = parts // 2
        return refs[2 + part // n].at[part % n]
    return refs[{0: 0, 1: 1, 3: 4}[step]].at[part]


def weight_blocks(refs, idx):
    y, z = idx[0], idx[1] * 2 + idx[2]
    for k in range(4):
        for j in range(4):
            r = 2 * ((y + k) & 3) + (((z + j) & 3) >> 1)
            yield piece(refs, k, j, 4), j & 1, r


def level_matrix():
    t = np.arange(CH)[:, None]
    u = np.arange(CH)[None, :]
    rows = []
    for level in range(LEVELS):
        b = 1 << level
        ref = (t // (2 * b)) * 2 * b + b - 1
        late = (t % (2 * b)) >= b
        rows.append(np.where(late, (u > ref) & (u <= t), (u > t) & (u <= ref)))
    rows.append(u <= t)
    rows.append(u > t)
    return np.concatenate(rows, 0).astype(np.float32)


def dot_nt(a, b):
    return lax.dot_general(a, b, (((1,), (1,)), ((), ())), preferred_element_type=F32)


def dot_tn(a, b):
    return lax.dot_general(a, b, (((0,), (0,)), ((), ())), preferred_element_type=F32)


def dot_nn(a, b):
    return jnp.dot(a, b, preferred_element_type=F32)


def copy_all(copies, sems):
    started = []
    for i, (src, dst) in enumerate(copies):
        cp = pltpu.make_async_copy(src, dst, sems.at[i])
        cp.start()
        started.append(cp)
    return started


def col(r):
    return pl.ds(pl.multiple_of(r * 256, 256), 256)


def x_copies(refs, cat, x):
    out = []
    for k in range(4):
        for z in range(2):
            r = z * 4 + ((x + k) & 3)
            out.append((piece(refs, k, z), cat.at[:, col(r)]))
    return out


def head_out(o, gain):
    ms = jnp.mean(o * o, axis=-1, keepdims=True)
    return o * lax.rsqrt(ms + EPS) * gain


def mix_kernel(
    idx, xo0, xo1, xo2, xo3, xo4, xp0, xp1, xp2, xp3, xp4, w0, w1, w2, w3, w4,
    bias_ref, gain_ref, mat_ref, dst_ref,
    own_ref, other_ref, state_ref,
    xcat, wcat, mix, oscr, carry, sems,
):
    x, c, length = idx[3], idx[4], idx[5]
    copies = x_copies((xo0, xo1, xo2, xo3, xo4), xcat.at[0], x)
    copies += x_copies((xp0, xp1, xp2, xp3, xp4), xcat.at[1], x)
    for ref, j, r in weight_blocks((w0, w1, w2, w3, w4), idx):
        copies.append((ref, wcat.at[j * 384 : (j + 1) * 384, col(r)]))
    for cp in copy_all(copies, sems):
        cp.wait()
    for hr in range(2):
        ha = (c + hr) & 1

        def project(i, unused, hr=hr, ha=ha):
            rows = pl.ds(pl.multiple_of(i * 176, 16), 176)
            mix[ha, rows, :] = dot_nt(xcat[hr, rows, :], wcat[...])
            return unused

        lax.fori_loop(0, 3, project, 0)
    carry[...] = jnp.zeros_like(carry)
    t = lax.broadcasted_iota(jnp.int32, (CH, CH), 0)
    s = lax.broadcasted_iota(jnp.int32, (CH, CH), 1)
    pair = jnp.where(t > s, t ^ s, 0)
    diag = t == s
    row = lax.broadcasted_iota(jnp.int32, (CH, 128), 0)

    def chunk(n, unused):
        h = n // 4
        rows = pl.ds(pl.multiple_of((n % 4) * CH, CH), CH)
        alive = (row + n * CH) < length
        for j in range(2):
            z = mix[h, rows, j * 384 : j * 384 + 128] + bias_ref[j : j + 1, :]
            v = mix[h, rows, j * 384 + 128 : j * 384 + 256].astype(BF)
            q = mix[h, rows, j * 384 + 256 : j * 384 + 384]
            e = jnp.exp(-jnp.abs(z))
            logf = jnp.where(alive, jnp.minimum(z, 0.0) - jnp.log1p(e), 0.0)
            inv = 1.0 / (1.0 + e)
            k = jnp.where(alive, jnp.where(z >= 0, e * inv, inv), 0.0)
            hi = logf.astype(BF)
            lo = (logf - hi.astype(F32)).astype(BF)
            d = dot_nn(mat_ref[...], jnp.concatenate([hi, lo], axis=1))
            decay = jnp.exp(d[:, :128] + d[:, 128:])
            scores = jnp.where(diag, dot_nt(q.astype(BF), k.astype(BF)), 0.0)
            for level in range(LEVELS):
                el = decay[level * CH : (level + 1) * CH]
                part = dot_nt((q * el).astype(BF), (k * el).astype(BF))
                scores = jnp.where((pair >> level) == 1, part, scores)
            es = decay[LEVELS * CH : (LEVELS + 1) * CH]
            ee = decay[(LEVELS + 1) * CH :]
            held = carry[j]
            o = dot_nn(scores.astype(BF), v) + dot_nt((q * es).astype(BF), held.astype(BF))
            o = jnp.where(alive, o, 0.0)
            carry[j] = held * es[CH - 1 :, :] + dot_tn(v, (k * ee).astype(BF))
            oscr[h, rows, j * 128 : (j + 1) * 128] = head_out(o, gain_ref[j : j + 1, :]).astype(BF)
        return unused

    lax.fori_loop(0, 8, chunk, 0)
    first = lax.broadcasted_iota(jnp.int32, (16, 128), 0) == 0
    for h in range(2):
        for j in range(2):
            z = mix[h, 512:513, j * 384 : j * 384 + 128] + bias_ref[j : j + 1, :]
            v = mix[h, 512:513, j * 384 + 128 : j * 384 + 256]
            q = mix[h, 512:513, j * 384 + 256 : j * 384 + 384]
            e = jnp.exp(-jnp.abs(z))
            inv = 1.0 / (1.0 + e)
            f = jnp.where(z >= 0, inv, e * inv)
            k = jnp.where(z >= 0, e * inv, inv)
            ft = jnp.broadcast_to(f, (128, 128)).T
            kt = jnp.broadcast_to(k, (128, 128)).T
            qt = jnp.broadcast_to(q, (128, 128)).T
            nxt = ft * dst_ref[j, h] + kt * v
            state_ref[j, h] = nxt
            o = head_out(jnp.sum(nxt * qt, axis=0, keepdims=True), gain_ref[j : j + 1, :])
            wide = jnp.where(first, jnp.broadcast_to(o, (16, 128)), 0.0)
            oscr[h, 512:528, j * 128 : (j + 1) * 128] = wide.astype(BF)
    for j in range(2):
        state_ref[j, 2] = carry[j].T
    own_ref[...] = oscr[c]
    other_ref[...] = oscr[1 - c]


def anyspec():
    return pl.BlockSpec(memory_space=pl.ANY)


def vspec():
    return pl.BlockSpec(memory_space=pltpu.VMEM)


def sspec():
    return pl.BlockSpec(memory_space=pltpu.SMEM)


def mix_call(idx, xo, xp, w, bias, gain, dst):
    mat = jnp.asarray(level_matrix(), BF)
    return pl.pallas_call(
        mix_kernel,
        out_shape=(
            jax.ShapeDtypeStruct((HALF, 256), BF),
            jax.ShapeDtypeStruct((HALF, 256), BF),
            jax.ShapeDtypeStruct((2, 3, 128, 128), F32),
        ),
        in_specs=[sspec()] + [anyspec()] * 15 + [vspec()] * 4,
        out_specs=(vspec(),) * 3,
        scratch_shapes=[
            pltpu.VMEM((2, HALF, 2048), BF),
            pltpu.VMEM((768, 2048), BF),
            pltpu.VMEM((2, HALF, 768), F32),
            pltpu.VMEM((2, HALF, 256), BF),
            pltpu.VMEM((2, 128, 128), F32),
            pltpu.SemaphoreType.DMA((32,)),
        ],
        compiler_params=pltpu.CompilerParams(vmem_limit_bytes=VMEM_LIMIT),
        name="mix",
    )(idx, *xo, *xp, *w, bias, gain, mat, dst)


def spread(out_s, x, p0, p1, p2, p3):
    for z in range(2):
        p0[z] = out_s[z * 4 + x]
        for k, ref in ((1, p1), (2, p2), (3, p3)):
            ref[z] = out_s[z * 4 + ((x + k) & 3)].astype(BF)


PARTS = (
    jax.ShapeDtypeStruct((2, HALF, 256), F32),
    jax.ShapeDtypeStruct((2, HALF, 256), BF),
    jax.ShapeDtypeStruct((2, HALF, 256), BF),
    jax.ShapeDtypeStruct((2, HALF, 256), BF),
)


def out_kernel(
    idx, a_ref, b_ref, u0, u1, u2, u3, u4, v0, v1, v2, v3, v4,
    p0, p1, p2, p3, ocat, wcat, out_s, sems,
):
    copies = [(a_ref, ocat.at[:, 0:256]), (b_ref, ocat.at[:, 256:512])]
    for cc, refs in ((0, (u0, u1, u2, u3, u4)), (1, (v0, v1, v2, v3, v4))):
        for ref, j, r in weight_blocks(refs, idx):
            at = cc * 256 + j * 128
            copies.append((ref, wcat.at[r, at : at + 128, :]))
    for cp in copy_all(copies, sems):
        cp.wait()

    def block(r, unused):
        out_s[r] = dot_nn(ocat[...], wcat[r])
        return unused

    lax.fori_loop(0, 8, block, 0)
    spread(out_s, idx[3], p0, p1, p2, p3)


def out_call(idx, a, b, u, v):
    return pl.pallas_call(
        out_kernel,
        out_shape=PARTS,
        in_specs=[sspec()] + [anyspec()] * 12,
        out_specs=(vspec(),) * 4,
        scratch_shapes=[
            pltpu.VMEM((HALF, 512), BF),
            pltpu.VMEM((8, 512, 256), BF),
            pltpu.VMEM((8, HALF, 256), F32),
            pltpu.SemaphoreType.DMA((34,)),
        ],
        compiler_params=pltpu.CompilerParams(vmem_limit_bytes=VMEM_LIMIT),
        name="outp",
    )(idx, a, b, *u, *v)


def mlp_kernel(
    idx, x0, x1, x2, x3, x4, g0, g1, g2, g3, g4, h0, h1, h2, h3, h4,
    d0, d1, d2, d3, d4, e0, e1, e2, e3, e4, gain_ref,
    p0, p1, p2, p3, xcat, wg, wd, hid, out_s, sems,
):
    x = idx[3]
    first = copy_all(x_copies((x0, x1, x2, x3, x4), xcat, x), sems)
    copies = []
    for cc, refs in ((0, (g0, g1, g2, g3, g4)), (1, (h0, h1, h2, h3, h4))):
        for ref, j, r in weight_blocks(refs, idx):
            at = cc * 704 + j * 352
            copies.append((ref, wg.at[:, at : at + 352, col(r)]))
    second = copy_all(copies, sems.at[8:40])
    copies = []
    for cc, refs in ((0, (d0, d1, d2, d3, d4)), (1, (e0, e1, e2, e3, e4))):
        for ref, j, r in weight_blocks(refs, idx):
            at = cc * 704 + j * 352
            copies.append((ref, wd.at[at : at + 352, col(r)]))
    third = copy_all(copies, sems.at[40:72])
    for cp in first:
        cp.wait()

    def normalize(i, unused):
        rows = pl.ds(pl.multiple_of(i * 48, 16), 48)
        r = xcat[rows, :].astype(F32)
        ms = jnp.mean(r * r, axis=-1, keepdims=True)
        xcat[rows, :] = (r * lax.rsqrt(ms + EPS) * gain_ref[...]).astype(BF)
        return unused

    lax.fori_loop(0, 11, normalize, 0)
    for cp in second:
        cp.wait()

    def expand(i, unused):
        rows = pl.ds(pl.multiple_of(i * 176, 16), 176)
        xv = xcat[rows, :]
        gate = dot_nt(xv, wg[0])
        up = dot_nt(xv, wg[1])
        hid[rows, :] = (gate / (1.0 + jnp.exp(-gate)) * up).astype(BF)
        return unused

    lax.fori_loop(0, 3, expand, 0)
    for cp in third:
        cp.wait()

    def block(r, unused):
        out_s[r] = dot_nn(hid[...], wd[:, col(r)])
        return unused

    lax.fori_loop(0, 8, block, 0)
    spread(out_s, x, p0, p1, p2, p3)


def mlp_call(idx, xs, g, h, d, e, gain):
    return pl.pallas_call(
        mlp_kernel,
        out_shape=PARTS,
        in_specs=[sspec()] + [anyspec()] * 25 + [vspec()],
        out_specs=(vspec(),) * 4,
        scratch_shapes=[
            pltpu.VMEM((HALF, 2048), BF),
            pltpu.VMEM((2, 1408, 2048), BF),
            pltpu.VMEM((1408, 2048), BF),
            pltpu.VMEM((HALF, 1408), BF),
            pltpu.VMEM((8, HALF, 256), F32),
            pltpu.SemaphoreType.DMA((72,)),
        ],
        compiler_params=pltpu.CompilerParams(vmem_limit_bytes=VMEM_LIMIT),
        name="mlp",
    )(idx, *xs, *g, *h, *d, *e, gain)


def swap(value, axis):
    return shift(value, axis, 1)


def z_gather(local):
    perm = lambda step: [(i, (i + step) % 4) for i in range(4)]
    return jnp.stack([local] + [lax.ppermute(local, ("zh", "zl"), perm(-k)) for k in (1, 2, 3)])


def after(value, *others):
    return lax.optimization_barrier((value,) + others)[0]


def reduce_parts(parts):
    p0, p1, p2, p3 = parts
    r2 = shift(p2, "x", 2)
    r1 = shift(p1, "x", 1)
    r3 = shift(p3, "x", -1)
    return p0 + r1.astype(F32) + r2.astype(F32) + r3.astype(F32)


def on_device(
    prompt_tokens, decode_tokens, prompt_lengths, decode_states, w_fio, forget_bias,
    head_gain, w_out, mlp_gain, w_gu, w_down,
):
    ax = {name: lax.axis_index(name) for name in SIZES}
    zl = ax["zl"]
    length = jnp.where(zl == 0, prompt_lengths[0], prompt_lengths[1])
    idx = jnp.stack([ax["y"], ax["zh"], zl, ax["x"], ax["c"], length]).astype(jnp.int32)

    rows = jnp.concatenate(
        [
            prompt_tokens.reshape(2, 2, 512, 128),
            decode_tokens.reshape(2, 2, 1, 128),
            jnp.zeros((2, 2, HALF - 513, 128), BF),
        ],
        axis=2,
    ).reshape(4, HALF, 128)
    got = lax.all_to_all(rows, ("zl", "c"), 0, 0, tiled=True)
    x_own = got.reshape(2, 2, HALF, 128).transpose(0, 2, 1, 3).reshape(2, HALF, 256)

    fio = z_gather(w_fio.astype(BF).T)
    fio = ring_gather(fio, "y")
    xs = ring_gather(x_own, "x")
    xp = [swap(v, "c") for v in xs]

    wo = z_gather(after(w_out, x_own, fio[0]).astype(BF))
    wo = ring_gather(after(wo, fio[1], fio[4]), "y")
    wo2 = [swap(v, "c") for v in wo]
    gu = z_gather(after(w_gu, wo[0]).astype(BF).T.reshape(2, 352, 256))
    gu = ring_gather(after(gu, fio[2], fio[3], wo[1], wo[4]), "y")
    gu2 = [swap(v, "c") for v in gu]
    wd = z_gather(after(w_down, gu[0]).astype(BF))
    wd = ring_gather(after(wd, gu[2], gu[3]), "y")
    wd2 = [swap(v, "c") for v in wd]

    small = jnp.stack([forget_bias, head_gain])
    small2 = swap(small, "zl")
    bias = jnp.stack([small[0], small2[0]])
    gain = jnp.stack([small[1], small2[1]])
    ds = decode_states.reshape(2, 2, 128, 128)
    ds_keep = jnp.where(zl == 0, ds[0], ds[1])
    ds_send = jnp.where(zl == 0, ds[1], ds[0])
    dst = jnp.stack([ds_keep, swap(ds_send, "zl")])

    ho, hs, states = mix_call(idx, xs, xp, fio, bias, gain, dst)
    hr = swap(hs, "c")
    mine, other = states[0], swap(states[1], "zl")
    decode_next = jnp.where(
        zl == 0,
        jnp.concatenate([mine[:2], other[:2]]),
        jnp.concatenate([other[:2], mine[:2]]),
    ).reshape(4, 1, 128, 128)
    prompt_states = jnp.where(
        zl == 0, jnp.stack([mine[2], other[2]]), jnp.stack([other[2], mine[2]])
    ).reshape(2, 1, 128, 128)

    attention = reduce_parts(out_call(idx, ho, hr, wo, wo2))
    attention = after(attention, decode_next, prompt_states)
    residual = (x_own.astype(F32) + attention).astype(BF)
    rs = ring_gather(residual, "x")
    down = reduce_parts(mlp_call(idx, rs, gu, gu2, wd, wd2, mlp_gain.reshape(1, 2048)))
    layer = (residual.astype(F32) + down).astype(BF)
    layer = layer.reshape(2, HALF, 2, 128).transpose(0, 2, 1, 3).reshape(4, HALF, 128)
    back = lax.all_to_all(layer, ("zl", "c"), 0, 0, tiled=True)
    prompt_out = back[:, :512].reshape(2, 1024, 128)
    decode_out = back[:, 512]
    return (prompt_out, decode_out, prompt_states, decode_next)


def solution(mesh):
    wide = Mesh(mesh.devices.reshape(tuple(SIZES.values())), tuple(SIZES))
    req = ("y", "zh")
    mlp = ("zl", "x", "c")
    return jax.shard_map(
        on_device,
        mesh=wide,
        in_specs=(
            P(req, None, mlp),
            P(req, mlp),
            P(req),
            P(req, mlp, None, None),
            P(req, mlp),
            P(mlp),
            P(mlp),
            P(mlp, req),
            P(),
            P(req, mlp),
            P(mlp, req),
        ),
        out_specs=(
            P(req, None, mlp),
            P(req, mlp),
            P(req, mlp, None, None),
            P(req, mlp, None, None),
        ),
        check_vma=False,
    )
```

time: 641 us -> 292 us (0.46)
  waiting for transfers between devices: 339 us -> 103 us
  matrix products: 121 us -> 0 us
  starting transfers between devices: 0.47 us -> 95.7 us
  blocking collectives: 87.3 us -> 0 us
  Pallas kernels: 0 us -> 54.2 us
  local copies, waits for them, and re-layouts: 48.2 us -> 20.5 us
  between operations: 14.4 us -> 2.55 us
  other arithmetic: 22.7 us -> 15.9 us
    all_gather x5 -> x0, waiting for transfers between devices: 198 us -> none  [the longest x1 63.3 us: on_device(): x_full = lax.all_gather(local_rows, 'mlp', axis=1, tiled=True)]
    unnamed x9 -> x0, waiting for transfers between devices: 141 us -> none
    dot_general x69 -> x0, matrix products: 121 us -> none  [the longest x16 27.6 us: block_step(): jnp.einsum('pthc,phcv->pthv', query_tilde, carried, precision=lax.Precisi...]
    ppermute x0 -> x66, waiting for transfers between devices: none -> 90.1 us  [the longest x54 76.4 us: shift(): return lax.ppermute(value, axis, [(i, (i + step) % n) for i in range(n)])]
    ppermute x0 -> x66, starting transfers between devices: none -> 85.8 us  [the longest x54 68.4 us: shift(): return lax.ppermute(value, axis, [(i, (i + step) % n) for i in range(n)])]
    psum x1 -> x0, blocking collectives: 54.2 us -> none  [on_device(): square_sum = lax.psum(jnp.sum(residual_wide * residual_wide, axis=1), 'mlp')]
    pallas_call x0 -> x3, Pallas kernels: none -> 54.2 us  [the longest x1 23.9 us: mlp_call(): pl.pallas_call(mlp_kernel, out_shape=PARTS, in_specs=[sspec()] + [anyspec...]
    all_gather x1 -> x0, blocking collectives: 33.1 us -> none  [project_output(): lax.all_gather(weights, 'req', axis=1, tiled=True)]
  transfers between devices with their start and end apart: 7 -> 68, of which waited for: 7 -> 23; matrix products, arithmetic and copies ran while one was open for 3% -> 10% of each run, Pallas kernels for 0% -> 10%
where the time goes in v1:
time: 292 us; the launch traced here: 291 us
  waiting for transfers between devices  103 us (35%)
  starting transfers between devices  95.7 us (33%)
  Pallas kernels  54.2 us (19%)
  local copies, waits for them, and re-layouts  20.5 us (7%)
  other arithmetic  15.9 us (5%)
    ppermute x54, waiting for transfers between devices, shift(): return lax.ppermute(value, axis, [(i, (i + step) % n) for i in range(n)])  76.4 us
    ppermute x54, starting transfers between devices, shift(): return lax.ppermute(value, axis, [(i, (i + step) % n) for i in range(n)])  68.4 us
    pallas_call x1, Pallas kernels, mlp_call(): pl.pallas_call(mlp_kernel, out_shape=PARTS, in_specs=[sspec()] + [anyspec...  23.9 us
    pallas_call x1, Pallas kernels, mix_call(): pl.pallas_call(mix_kernel, out_shape=(jax.ShapeDtypeStruct((HALF, 256), B...  23.5 us
    ppermute x12, starting transfers between devices, z_gather(): lax.ppermute(local, ('zh', 'zl'), perm(-k))  17.4 us
    ppermute x12, waiting for transfers between devices, z_gather(): lax.ppermute(local, ('zh', 'zl'), perm(-k))  13.8 us
    all_to_all x1, waiting for transfers between devices, on_device(): back = lax.all_to_all(layer, ('zl', 'c'), 0, 0, tiled=True)  7.48 us
    pallas_call x1, Pallas kernels, out_call(): pl.pallas_call(out_kernel, out_shape=PARTS, in_specs=[sspec()] + [anyspec...  6.74 us
  transfers between devices with their start and end apart: 68, of which 23 were waited for; matrix products, arithmetic and copies ran while one was open for 10% of the time, Pallas kernels for 10%

profile of v1, /device:TPU:1, one launch (start us, length us, event | category | flops | bytes accessed | tf_op | source)
XLA Modules:
  0.0 291.4 jit_solution(4115477758782925235)
XLA Ops:
  1.8 4.5 %collective-permute-start.10 = (bf16[384,256]{1,0:T(8,128)(2,1)S(1)}, bf16[384,256]{1,0:T(8,128)(2,1)S(1)}, u32[]{:S(2)}, u32[]{:S(2)}) collective-permute-start(bf16[384,256]{1,0:T(8,128)(2,1)S(1)} %bitcast.82), channel_id=1, source_target_pairs={{0,16},{8,24},{16,0},{24,8},{1,17},{9,25},{17,1},{25,9},{2,18},{10... | collective-permute-start | bytes 589832 | tf_op jit(solution)/shard_map/ppermute | solution.py:353
  8.5 2.0 maximum_maximum_fusion
  10.5 5.0 %all-to-all-start = ((bf16[4,528,128]{2,1,0:T(8,128)(2,1)}), bf16[4,528,128]{2,1,0:T(8,128)(2,1)S(1)}, u32[]{:S(2)}, u32[]{:S(2)}) async-start(bf16[4,528,128]{2,1,0:T(8,128)(2,1)} %maximum_maximum_fusion), calls=%async_computation | async-start | bytes 1081344 | tf_op jit(solution)/shard_map/all_to_all | solution.py:385
  15.7 1.4 collective-permute-start.13
  17.1 1.5 collective-permute-start.12
  18.6 5.0 %all-to-all-done = bf16[4,528,128]{2,1,0:T(8,128)(2,1)S(1)} async-done(((bf16[4,528,128]{2,1,0:T(8,128)(2,1)}), bf16[4,528,128]{2,1,0:T(8,128)(2,1)S(1)}, u32[]{:S(2)}, u32[]{:S(2)}) %all-to-all-start) | async-done | bytes 540704 | tf_op jit(solution)/shard_map/all_to_all | solution.py:385
  25.6 1.2 collective-permute-start.1
  26.8 1.5 collective-permute-start
  28.3 1.2 collective-permute-done.20
  30.9 2.7 collective-permute-done.19
  34.3 4.1 %collective-permute-done.21 = bf16[128,256]{1,0:T(8,128)(2,1)S(1)} collective-permute-done((bf16[128,256]{1,0:T(8,128)(2,1)S(1)}, bf16[128,256]{1,0:T(8,128)(2,1)S(1)}, u32[]{:S(2)}, u32[]{:S(2)}) %collective-permute-start.21) | collective-permute-done | bytes 65568 | tf_op jit(solution)/shard_map/ppermute | solution.py:353
  38.4 3.6 %collective-permute-start.4 = (bf16[2,528,256]{2,1,0:T(8,128)(2,1)S(1)}, bf16[2,528,256]{2,1,0:T(8,128)(2,1)S(1)}, u32[]{:S(2)}, u32[]{:S(2)}) collective-permute-start(bf16[2,528,256]{2,1,0:T(8,128)(2,1)S(1)} %bitcast.76), channel_id=1, source_target_pairs={{0,1},{1,0},{2,3},{3,2},{4,5},{5,4},{6,7},{7,6},{8,9},{9,8},{10,11... | collective-permute-start | bytes 1622024 | tf_op jit(solution)/shard_map/ppermute | solution.py:23
  45.0 1.3 collective-permute-start.2
  47.3 1.5 collective-permute-start.3
  48.8 1.3 collective-permute-start.23
  50.8 1.5 collective-permute-start.17
  52.3 2.7 collective-permute-done.17
  55.0 1.4 collective-permute-start.41
  56.4 2.5 collective-permute-start.39
  59.6 1.4 collective-permute-start.14
  61.0 1.4 collective-permute-start.22
  63.1 3.6 %collective-permute-done.22.u1 = bf16[4,128,256]{2,1,0:T(8,128)(2,1)} collective-permute-done((bf16[4,128,256]{2,1,0:T(8,128)(2,1)S(1)}, bf16[4,128,256]{2,1,0:T(8,128)(2,1)}, u32[]{:S(2)}, u32[]{:S(2)}) %collective-permute-start.22) | collective-permute-done | bytes 262176 | tf_op jit(solution)/shard_map/ppermute | solution.py:23
  68.5 6.3 %collective-permute-start.8 = (bf16[2,528,256]{2,1,0:T(8,128)(2,1)}, bf16[2,528,256]{2,1,0:T(8,128)(2,1)S(1)}, u32[]{:S(2)}, u32[]{:S(2)}) collective-permute-start(bf16[2,528,256]{2,1,0:T(8,128)(2,1)} %collective-permute-done.1.xo4), channel_id=1, source_target_pairs={{0,1},{1,0},{2,3},{3,2},{4,5},{5,4},{6,7},{7,6},{8,9},{9,8},{10,11... | collective-permute-start | bytes 1622024 | tf_op jit(solution)/shard_map/ppermute | solution.py:23
  74.9 1.7 collective-permute-start.15
  80.8 1.3 collective-permute-start.25
  82.0 6.4 %collective-permute-done.25.u3 = bf16[2,128,256]{2,1,0:T(8,128)(2,1)} collective-permute-done((bf16[2,128,256]{2,1,0:T(8,128)(2,1)S(1)}, bf16[2,128,256]{2,1,0:T(8,128)(2,1)}, u32[]{:S(2)}, u32[]{:S(2)}) %collective-permute-start.25) | collective-permute-done | bytes 131104 | tf_op jit(solution)/shard_map/ppermute | solution.py:23
  88.4 1.3 collective-permute-start.7
  90.4 1.7 pad_maximum_fusion.4.dst_ref
  93.5 1.4 pad_maximum_fusion.g0
  96.0 23.5 %mix.1 = (bf16[528,256]{1,0:T(8,128)(2,1)}, bf16[528,256]{1,0:T(8,128)(2,1)}, f32[2,3,128,128]{3,2,1,0:T(8,128)}) custom-call(s32[6]{0:T(128)} %stack.114.idx, bf16[2,528,256]{2,1,0:T(8,128)(2,1)} %bitcast.77, bf16[2,528,256]{2,1,0:T(8,128)(2,1)} %collective-permute-done.xo1, bf16[1,528,256]{2,1,0:T(8,128)(2,1)} %copy-done.40, ...), custom_call_target="tpu_custom_call" | custom-call | tf_op jit(solution)/shard_map/mix/pallas_call | solution.py:201
  119.5 1.4 collective-permute-start.43
  120.9 1.7 collective-permute-start.42
  123.1 1.6 slice_bitcast_fusion
  128.3 6.7 %outp.1 = (f32[2,528,256]{2,1,0:T(8,128)}, bf16[2,528,256]{2,1,0:T(8,128)(2,1)}, bf16[2,528,256]{2,1,0:T(8,128)(2,1)}, bf16[2,528,256]{2,1,0:T(8,128)(2,1)}) custom-call(s32[6]{0:T(128)} %stack.114.idx, bf16[528,256]{1,0:T(8,128)(2,1)} %get-tuple-element.22.a_ref, bf16[528,256]{1,0:T(8,128)(2,1)} %collective-permute-done.18.b_ref, ...), custom_call_target="tpu_custom_call" | custom-call | tf_op jit(solution)/shard_map/outp/pallas_call | solution.py:259
  135.2 2.4 collective-permute-start.32
  138.8 1.5 slice_bitcast_fusion.3
  141.9 8.5 %collective-permute-done.31 = bf16[2,528,256]{2,1,0:T(8,128)(2,1)S(1)} collective-permute-done((bf16[2,528,256]{2,1,0:T(8,128)(2,1)}, bf16[2,528,256]{2,1,0:T(8,128)(2,1)S(1)}, u32[]{:S(2)}, u32[]{:S(2)}) %collective-permute-start.31) | collective-permute-done | bytes 540704 | tf_op jit(solution)/shard_map/ppermute | solution.py:23
  150.4 2.5 collective-permute-start.52
  152.9 8.7 %collective-permute-done.32 = bf16[2,528,256]{2,1,0:T(8,128)(2,1)S(1)} collective-permute-done((bf16[2,528,256]{2,1,0:T(8,128)(2,1)}, bf16[2,528,256]{2,1,0:T(8,128)(2,1)S(1)}, u32[]{:S(2)}, u32[]{:S(2)}) %collective-permute-start.32) | collective-permute-done | bytes 540704 | tf_op jit(solution)/shard_map/ppermute | solution.py:23
  161.6 1.6 collective-permute-start.51
  163.2 3.1 %collective-permute-start.46 = (bf16[4,2,352,256]{3,2,1,0:T(8,128)(2,1)S(1)}, bf16[4,2,352,256]{3,2,1,0:T(8,128)(2,1)S(1)}, u32[]{:S(2)}, u32[]{:S(2)}) collective-permute-start(bf16[4,2,352,256]{3,2,1,0:T(8,128)(2,1)S(1)} %pad_maximum_fusion.g0), channel_id=1, source_target_pairs={{0,1},{1,0},{2,3},{3,2},{4,5},{5,4},{6,7},{7,6},{8,9},{9,8},{10,11... | collective-permute-start | bytes 4325384 | tf_op jit(solution)/shard_map/ppermute | solution.py:23
  166.3 1.5 convert_add_fusion
  168.0 1.5 slice.135
  169.5 2.4 collective-permute-start.45
  173.3 5.6 %collective-permute-done.53 = bf16[352,256]{1,0:T(8,128)(2,1)S(1)} collective-permute-done((bf16[352,256]{1,0:T(8,128)(2,1)S(1)}, bf16[352,256]{1,0:T(8,128)(2,1)S(1)}, u32[]{:S(2)}, u32[]{:S(2)}) %collective-permute-start.53) | collective-permute-done | bytes 180256 | tf_op jit(solution)/shard_map/ppermute | solution.py:353
  178.9 2.3 collective-permute-start.35
  181.3 5.6 %collective-permute-done.44.g2 = bf16[2,2,352,256]{3,2,1,0:T(8,128)(2,1)S(1)} collective-permute-done((bf16[2,2,352,256]{3,2,1,0:T(8,128)(2,1)S(1)}, bf16[2,2,352,256]{3,2,1,0:T(8,128)(2,1)S(1)}, u32[]{:S(2)}, u32[]{:S(2)}) %collective-permute-start.44) | collective-permute-done | bytes 720928 | tf_op jit(solution)/shard_map/ppermute | solution.py:23
  187.7 2.9 collective-permute-start.54
  191.3 3.4 %collective-permute-start.38 = (bf16[1,528,256]{2,1,0:T(8,128)(2,1)S(1)}, bf16[1,528,256]{2,1,0:T(8,128)(2,1)S(1)}, u32[]{:S(2)}, u32[]{:S(2)}) collective-permute-start(bf16[1,528,256]{2,1,0:T(8,128)(2,1)S(1)} %slice.133), channel_id=1, source_target_pairs={{0,6},{2,0},{4,2},{6,4},{1,7},{3,1},{5,3},{7,5},{8,14},{10,8},{12,... | collective-permute-start | bytes 811016 | tf_op jit(solution)/shard_map/ppermute | solution.py:23
  194.8 3.8 %collective-permute-done.37.x2 = bf16[1,528,256]{2,1,0:T(8,128)(2,1)S(1)} collective-permute-done((bf16[1,528,256]{2,1,0:T(8,128)(2,1)S(1)}, bf16[1,528,256]{2,1,0:T(8,128)(2,1)S(1)}, u32[]{:S(2)}, u32[]{:S(2)}) %collective-permute-start.37) | collective-permute-done | bytes 270368 | tf_op jit(solution)/shard_map/ppermute | solution.py:23
  198.6 3.3 %collective-permute-start.48 = (bf16[2,2,352,256]{3,2,1,0:T(8,128)(2,1)S(1)}, bf16[2,2,352,256]{3,2,1,0:T(8,128)(2,1)S(1)}, u32[]{:S(2)}, u32[]{:S(2)}) collective-permute-start(bf16[2,2,352,256]{3,2,1,0:T(8,128)(2,1)S(1)} %collective-permute-done.44.g2), channel_id=1, source_target_pairs={{0,1},{1,0},{2,3},{3,2},{4,5},{5,4},{6,7},{7,6},{8,9},{9,8},{10,11... | collective-permute-start | bytes 2162696 | tf_op jit(solution)/shard_map/ppermute | solution.py:23
  202.6 3.3 %collective-permute-done.55.d4 = bf16[4,352,256]{2,1,0:T(8,128)(2,1)S(1)} collective-permute-done((bf16[4,352,256]{2,1,0:T(8,128)(2,1)S(1)}, bf16[4,352,256]{2,1,0:T(8,128)(2,1)S(1)}, u32[]{:S(2)}, u32[]{:S(2)}) %collective-permute-start.55) | collective-permute-done | bytes 720928 | tf_op jit(solution)/shard_map/ppermute | solution.py:23
  205.9 1.7 collective-permute-start.58
  210.5 1.7 collective-permute-start.57
  212.2 6.5 %collective-permute-done.56.d2 = bf16[2,352,256]{2,1,0:T(8,128)(2,1)S(1)} collective-permute-done((bf16[2,352,256]{2,1,0:T(8,128)(2,1)S(1)}, bf16[2,352,256]{2,1,0:T(8,128)(2,1)S(1)}, u32[]{:S(2)}, u32[]{:S(2)}) %collective-permute-start.56) | collective-permute-done | bytes 360480 | tf_op jit(solution)/shard_map/ppermute | solution.py:23
  218.7 1.3 collective-permute-start.60
  220.1 1.2 collective-permute-start.61
  221.4 1.2 collective-permute-done.61.e3
  223.5 23.9 %mlp.1 = (f32[2,528,256]{2,1,0:T(8,128)}, bf16[2,528,256]{2,1,0:T(8,128)(2,1)}, bf16[2,528,256]{2,1,0:T(8,128)(2,1)}, bf16[2,528,256]{2,1,0:T(8,128)(2,1)}) custom-call(s32[6]{0:T(128)} %stack.114.idx, bf16[2,528,256]{2,1,0:T(8,128)(2,1)} %copy-done.1, bf16[2,528,256]{2,1,0:T(8,128)(2,1)} %copy-done.17, bf16[1,528,256]{2,1,0:T(8,128)(2,1)} %copy-done.43, ...), custom_call_target="tpu_custom_call" | custom-call | tf_op jit(solution)/shard_map/mlp/pallas_call | solution.py:329
  248.2 1.9 collective-permute-start.65
  250.1 23.8 %collective-permute-done.63 = bf16[2,528,256]{2,1,0:T(8,128)(2,1)S(1)} collective-permute-done((bf16[2,528,256]{2,1,0:T(8,128)(2,1)}, bf16[2,528,256]{2,1,0:T(8,128)(2,1)S(1)}, u32[]{:S(2)}, u32[]{:S(2)}) %collective-permute-start.63) | collective-permute-done | bytes 540704 | tf_op jit(solution)/shard_map/ppermute | solution.py:23
  274.3 1.6 add_convert_fusion
  276.9 4.9 %all-to-all-start.1 = ((bf16[4,528,128]{2,1,0:T(8,128)(2,1)}), bf16[4,528,128]{2,1,0:T(8,128)(2,1)S(1)}, u32[]{:S(2)}, u32[]{:S(2)}) async-start(bf16[4,528,128]{2,1,0:T(8,128)(2,1)} %bitcast.43), calls=%async_computation.1 | async-start | bytes 1081344 | tf_op jit(solution)/shard_map/all_to_all | solution.py:431
  282.5 7.5 %all-to-all-done.1 = bf16[4,528,128]{2,1,0:T(8,128)(2,1)S(1)} async-done(((bf16[4,528,128]{2,1,0:T(8,128)(2,1)}), bf16[4,528,128]{2,1,0:T(8,128)(2,1)S(1)}, u32[]{:S(2)}, u32[]{:S(2)}) %all-to-all-start.1) | async-done | bytes 540704 | tf_op jit(solution)/shard_map/all_to_all | solution.py:431
  (233 shorter events, 40.6 us)
Async XLA Ops:
  1.8 13.7 %collective-permute-start.10 = (bf16[384,256]{1,0:T(8,128)(2,1)S(1)}, bf16[384,256]{1,0:T(8,128)(2,1)S(1)}, u32[]{:S(2)}, u32[]{:S(2)}) collective-permute-start(bf16[384,256]{1,0:T(8,128)(2,1)S(1)} %bitcast.82), channel_id=1, source_target_pairs={{0,16},{8,24},{16,0},{24,8},{1,17},{9,25},{17,1},{25,9},{2,18},{10... | collective-permute-start | bytes 589832 | tf_op jit(solution)/shard_map/ppermute | solution.py:353
  6.3 9.3 %collective-permute-start.9 = (bf16[384,256]{1,0:T(8,128)(2,1)S(1)}, bf16[384,256]{1,0:T(8,128)(2,1)S(1)}, u32[]{:S(2)}, u32[]{:S(2)}) collective-permute-start(bf16[384,256]{1,0:T(8,128)(2,1)S(1)} %bitcast.83), channel_id=1, source_target_pairs={{0,24},{8,0},{16,8},{24,16},{1,25},{9,1},{17,9},{25,17},{2,26},{10... | collective-permute-start | bytes 589832 | tf_op jit(solution)/shard_map/ppermute | solution.py:353
  6.7 8.9 %collective-permute-start.11 = (bf16[384,256]{1,0:T(8,128)(2,1)S(1)}, bf16[384,256]{1,0:T(8,128)(2,1)S(1)}, u32[]{:S(2)}, u32[]{:S(2)}) collective-permute-start(bf16[384,256]{1,0:T(8,128)(2,1)S(1)} %bitcast.84), channel_id=1, source_target_pairs={{0,8},{8,16},{16,24},{24,0},{1,9},{9,17},{17,25},{25,1},{2,10},{10... | collective-permute-start | bytes 589832 | tf_op jit(solution)/shard_map/ppermute | solution.py:353
  10.5 13.1 %all-to-all-start = ((bf16[4,528,128]{2,1,0:T(8,128)(2,1)}), bf16[4,528,128]{2,1,0:T(8,128)(2,1)S(1)}, u32[]{:S(2)}, u32[]{:S(2)}) async-start(bf16[4,528,128]{2,1,0:T(8,128)(2,1)} %maximum_maximum_fusion), calls=%async_computation | async-start | bytes 1081344 | tf_op jit(solution)/shard_map/all_to_all | solution.py:385
  15.7 31.5 %collective-permute-start.13 = (bf16[4,384,256]{2,1,0:T(8,128)(2,1)S(1)}, bf16[4,384,256]{2,1,0:T(8,128)(2,1)S(1)}, u32[]{:S(2)}, u32[]{:S(2)}) collective-permute-start(bf16[4,384,256]{2,1,0:T(8,128)(2,1)S(1)} %pad_maximum_fusion.1.w0), channel_id=1, source_target_pairs={{0,32},{32,64},{64,96},{96,0},{1,33},{33,65},{65,97},{97,1},{2,34}... | collective-permute-start | bytes 2359304 | tf_op jit(solution)/shard_map/ppermute | solution.py:23
  17.1 31.7 %collective-permute-start.12 = (bf16[4,384,256]{2,1,0:T(8,128)(2,1)S(1)}, bf16[4,384,256]{2,1,0:T(8,128)(2,1)S(1)}, u32[]{:S(2)}, u32[]{:S(2)}) collective-permute-start(bf16[4,384,256]{2,1,0:T(8,128)(2,1)S(1)} %pad_maximum_fusion.1.w0), channel_id=1, source_target_pairs={{0,96},{32,0},{64,32},{96,64},{1,97},{33,1},{65,33},{97,65},{2,98}... | collective-permute-start | bytes 2359304 | tf_op jit(solution)/shard_map/ppermute | solution.py:23
  24.8 4.7 %collective-permute-start.20 = (bf16[128,256]{1,0:T(8,128)(2,1)S(1)}, bf16[128,256]{1,0:T(8,128)(2,1)S(1)}, u32[]{:S(2)}, u32[]{:S(2)}) collective-permute-start(bf16[128,256]{1,0:T(8,128)(2,1)S(1)} %convert_element_type.44), channel_id=1, source_target_pairs={{0,16},{8,24},{16,0},{24,8},{1,17},{9,25},{17,1},{25,9},{2,18},{10... | collective-permute-start | bytes 196616 | tf_op jit(solution)/shard_map/ppermute | solution.py:353
  25.6 18.3 %collective-permute-start.1 = (bf16[2,528,256]{2,1,0:T(8,128)(2,1)S(1)}, bf16[2,528,256]{2,1,0:T(8,128)(2,1)}, u32[]{:S(2)}, u32[]{:S(2)}) collective-permute-start(bf16[2,528,256]{2,1,0:T(8,128)(2,1)S(1)} %bitcast.74), channel_id=1, source_target_pairs={{0,2},{2,4},{4,6},{6,0},{1,3},{3,5},{5,7},{7,1},{8,10},{10,12},{12... | collective-permute-start | bytes 1622024 | tf_op jit(solution)/shard_map/ppermute | solution.py:23
  26.8 18.2 %collective-permute-start = (bf16[2,528,256]{2,1,0:T(8,128)(2,1)S(1)}, bf16[2,528,256]{2,1,0:T(8,128)(2,1)}, u32[]{:S(2)}, u32[]{:S(2)}) collective-permute-start(bf16[2,528,256]{2,1,0:T(8,128)(2,1)S(1)} %bitcast.75), channel_id=1, source_target_pairs={{0,6},{2,0},{4,2},{6,4},{1,7},{3,1},{5,3},{7,5},{8,14},{10,8},{12,... | collective-permute-start | bytes 1622024 | tf_op jit(solution)/shard_map/ppermute | solution.py:23
  33.6 4.7 %collective-permute-start.21 = (bf16[128,256]{1,0:T(8,128)(2,1)S(1)}, bf16[128,256]{1,0:T(8,128)(2,1)S(1)}, u32[]{:S(2)}, u32[]{:S(2)}) collective-permute-start(bf16[128,256]{1,0:T(8,128)(2,1)S(1)} %convert_element_type.44), channel_id=1, source_target_pairs={{0,8},{8,16},{16,24},{24,0},{1,9},{9,17},{17,25},{25,1},{2,10},{10... | collective-permute-start | bytes 196616 | tf_op jit(solution)/shard_map/ppermute | solution.py:353
  38.4 18.0 %collective-permute-start.4 = (bf16[2,528,256]{2,1,0:T(8,128)(2,1)S(1)}, bf16[2,528,256]{2,1,0:T(8,128)(2,1)S(1)}, u32[]{:S(2)}, u32[]{:S(2)}) collective-permute-start(bf16[2,528,256]{2,1,0:T(8,128)(2,1)S(1)} %bitcast.76), channel_id=1, source_target_pairs={{0,1},{1,0},{2,3},{3,2},{4,5},{5,4},{6,7},{7,6},{8,9},{9,8},{10,11... | collective-permute-start | bytes 1622024 | tf_op jit(solution)/shard_map/ppermute | solution.py:23
  43.9 6.9 %collective-permute-start.16 = (f32[2,128]{1,0:T(2,128)S(1)}, f32[2,128]{1,0:T(2,128)S(1)}, u32[]{:S(2)}, u32[]{:S(2)}) collective-permute-start(f32[2,128]{1,0:T(2,128)S(1)} %pad_maximum_fusion.6), channel_id=1, source_target_pairs={{0,8},{8,0},{1,9},{9,1},{2,10},{10,2},{3,11},{11,3},{4,12},{12,4},... | collective-permute-start | bytes 3080 | tf_op jit(solution)/shard_map/ppermute | solution.py:23
  45.0 11.4 %collective-permute-start.2 = (bf16[1,528,256]{2,1,0:T(8,128)(2,1)S(1)}, bf16[1,528,256]{2,1,0:T(8,128)(2,1)S(1)}, u32[]{:S(2)}, u32[]{:S(2)}) collective-permute-start(bf16[1,528,256]{2,1,0:T(8,128)(2,1)S(1)} %slice.121), channel_id=1, source_target_pairs={{0,2},{2,4},{4,6},{6,0},{1,3},{3,5},{5,7},{7,1},{8,10},{10,12},{12... | collective-permute-start | bytes 811016 | tf_op jit(solution)/shard_map/ppermute | solution.py:23
  47.3 12.4 %collective-permute-start.3 = (bf16[1,528,256]{2,1,0:T(8,128)(2,1)S(1)}, bf16[1,528,256]{2,1,0:T(8,128)(2,1)S(1)}, u32[]{:S(2)}, u32[]{:S(2)}) collective-permute-start(bf16[1,528,256]{2,1,0:T(8,128)(2,1)S(1)} %slice.122), channel_id=1, source_target_pairs={{0,6},{2,0},{4,2},{6,4},{1,7},{3,1},{5,3},{7,5},{8,14},{10,8},{12,... | collective-permute-start | bytes 811016 | tf_op jit(solution)/shard_map/ppermute | solution.py:23
  48.8 12.2 %collective-permute-start.23 = (bf16[4,128,256]{2,1,0:T(8,128)(2,1)S(1)}, bf16[4,128,256]{2,1,0:T(8,128)(2,1)S(1)}, u32[]{:S(2)}, u32[]{:S(2)}) collective-permute-start(bf16[4,128,256]{2,1,0:T(8,128)(2,1)S(1)} %pad_maximum_fusion.5.u0), channel_id=1, source_target_pairs={{0,32},{32,64},{64,96},{96,0},{1,33},{33,65},{65,97},{97,1},{2,34}... | collective-permute-start | bytes 786440 | tf_op jit(solution)/shard_map/ppermute | solution.py:23
  50.8 4.2 %collective-permute-start.17 = (f32[2,128,128]{2,1,0:T(8,128)S(1)}, f32[2,128,128]{2,1,0:T(8,128)S(1)}, u32[]{:S(2)}, u32[]{:S(2)}) collective-permute-start(f32[2,128,128]{2,1,0:T(8,128)S(1)} %get-tuple-element.55), channel_id=1, source_target_pairs={{0,8},{8,0},{1,9},{9,1},{2,10},{10,2},{3,11},{11,3},{4,12},{12,4},... | collective-permute-start | bytes 393224 | tf_op jit(solution)/shard_map/ppermute | solution.py:23
  55.0 13.5 %collective-permute-start.41 = (bf16[2,352,256]{2,1,0:T(8,128)(2,1)S(1)}, bf16[2,352,256]{2,1,0:T(8,128)(2,1)}, u32[]{:S(2)}, u32[]{:S(2)}) collective-permute-start(bf16[2,352,256]{2,1,0:T(8,128)(2,1)S(1)} %bitcast.78), channel_id=1, source_target_pairs={{0,8},{8,16},{16,24},{24,0},{1,9},{9,17},{17,25},{25,1},{2,10},{10... | collective-permute-start | bytes 1081352 | tf_op jit(solution)/shard_map/ppermute | solution.py:353
  56.4 18.5 %collective-permute-start.40 = (bf16[2,352,256]{2,1,0:T(8,128)(2,1)S(1)}, bf16[2,352,256]{2,1,0:T(8,128)(2,1)S(1)}, u32[]{:S(2)}, u32[]{:S(2)}) collective-permute-start(bf16[2,352,256]{2,1,0:T(8,128)(2,1)S(1)} %bitcast.79), channel_id=1, source_target_pairs={{0,16},{8,24},{16,0},{24,8},{1,17},{9,25},{17,1},{25,9},{2,18},{10... | collective-permute-start | bytes 1081352 | tf_op jit(solution)/shard_map/ppermute | solution.py:353
  56.4 18.5 %collective-permute-start.39 = (bf16[2,352,256]{2,1,0:T(8,128)(2,1)S(1)}, bf16[2,352,256]{2,1,0:T(8,128)(2,1)S(1)}, u32[]{:S(2)}, u32[]{:S(2)}) collective-permute-start(bf16[2,352,256]{2,1,0:T(8,128)(2,1)S(1)} %bitcast.80), channel_id=1, source_target_pairs={{0,24},{8,0},{16,8},{24,16},{1,25},{9,1},{17,9},{25,17},{2,26},{10... | collective-permute-start | bytes 1081352 | tf_op jit(solution)/shard_map/ppermute | solution.py:353
  59.6 20.3 %collective-permute-start.14 = (bf16[2,384,256]{2,1,0:T(8,128)(2,1)}, bf16[2,384,256]{2,1,0:T(8,128)(2,1)S(1)}, u32[]{:S(2)}, u32[]{:S(2)}) collective-permute-start(bf16[2,384,256]{2,1,0:T(8,128)(2,1)} %slice.123), channel_id=1, source_target_pairs={{0,32},{32,64},{64,96},{96,0},{1,33},{33,65},{65,97},{97,1},{2,34}... | collective-permute-start | bytes 1179656 | tf_op jit(solution)/shard_map/ppermute | solution.py:23
  61.0 5.7 %collective-permute-start.22 = (bf16[4,128,256]{2,1,0:T(8,128)(2,1)S(1)}, bf16[4,128,256]{2,1,0:T(8,128)(2,1)}, u32[]{:S(2)}, u32[]{:S(2)}) collective-permute-start(bf16[4,128,256]{2,1,0:T(8,128)(2,1)S(1)} %pad_maximum_fusion.5.u0), channel_id=1, source_target_pairs={{0,96},{32,0},{64,32},{96,64},{1,97},{33,1},{65,33},{97,65},{2,98}... | collective-permute-start | bytes 786440 | tf_op jit(solution)/shard_map/ppermute | solution.py:23
  66.7 14.0 %collective-permute-start.24 = (bf16[2,128,256]{2,1,0:T(8,128)(2,1)}, bf16[2,128,256]{2,1,0:T(8,128)(2,1)}, u32[]{:S(2)}, u32[]{:S(2)}) collective-permute-start(bf16[2,128,256]{2,1,0:T(8,128)(2,1)} %slice.127), channel_id=1, source_target_pairs={{0,32},{32,64},{64,96},{96,0},{1,33},{33,65},{65,97},{97,1},{2,34}... | collective-permute-start | bytes 393224 | tf_op jit(solution)/shard_map/ppermute | solution.py:23
  68.5 23.6 %collective-permute-start.8 = (bf16[2,528,256]{2,1,0:T(8,128)(2,1)}, bf16[2,528,256]{2,1,0:T(8,128)(2,1)S(1)}, u32[]{:S(2)}, u32[]{:S(2)}) collective-permute-start(bf16[2,528,256]{2,1,0:T(8,128)(2,1)} %collective-permute-done.1.xo4), channel_id=1, source_target_pairs={{0,1},{1,0},{2,3},{3,2},{4,5},{5,4},{6,7},{7,6},{8,9},{9,8},{10,11... | collective-permute-start | bytes 1622024 | tf_op jit(solution)/shard_map/ppermute | solution.py:23
  74.8 17.7 %collective-permute-start.5 = (bf16[2,528,256]{2,1,0:T(8,128)(2,1)}, bf16[2,528,256]{2,1,0:T(8,128)(2,1)S(1)}, u32[]{:S(2)}, u32[]{:S(2)}) collective-permute-start(bf16[2,528,256]{2,1,0:T(8,128)(2,1)} %collective-permute-done.xo1), channel_id=1, source_target_pairs={{0,1},{1,0},{2,3},{3,2},{4,5},{5,4},{6,7},{7,6},{8,9},{9,8},{10,11... | collective-permute-start | bytes 1622024 | tf_op jit(solution)/shard_map/ppermute | solution.py:23
  74.9 15.3 %collective-permute-start.15 = (bf16[2,384,256]{2,1,0:T(8,128)(2,1)}, bf16[2,384,256]{2,1,0:T(8,128)(2,1)S(1)}, u32[]{:S(2)}, u32[]{:S(2)}) collective-permute-start(bf16[2,384,256]{2,1,0:T(8,128)(2,1)} %slice.124), channel_id=1, source_target_pairs={{0,96},{32,0},{64,32},{96,64},{1,97},{33,1},{65,33},{97,65},{2,98}... | collective-permute-start | bytes 1179656 | tf_op jit(solution)/shard_map/ppermute | solution.py:23
  80.0 12.7 %collective-permute-start.6 = (bf16[1,528,256]{2,1,0:T(8,128)(2,1)}, bf16[1,528,256]{2,1,0:T(8,128)(2,1)S(1)}, u32[]{:S(2)}, u32[]{:S(2)}) collective-permute-start(bf16[1,528,256]{2,1,0:T(8,128)(2,1)} %copy-done.40), channel_id=1, source_target_pairs={{0,1},{1,0},{2,3},{3,2},{4,5},{5,4},{6,7},{7,6},{8,9},{9,8},{10,11... | collective-permute-start | bytes 811016 | tf_op jit(solution)/shard_map/ppermute | solution.py:23
  80.8 7.6 %collective-permute-start.25 = (bf16[2,128,256]{2,1,0:T(8,128)(2,1)S(1)}, bf16[2,128,256]{2,1,0:T(8,128)(2,1)}, u32[]{:S(2)}, u32[]{:S(2)}) collective-permute-start(bf16[2,128,256]{2,1,0:T(8,128)(2,1)S(1)} %slice.128), channel_id=1, source_target_pairs={{0,96},{32,0},{64,32},{96,64},{1,97},{33,1},{65,33},{97,65},{2,98}... | collective-permute-start | bytes 393224 | tf_op jit(solution)/shard_map/ppermute | solution.py:23
  88.4 7.4 %collective-permute-start.7 = (bf16[1,528,256]{2,1,0:T(8,128)(2,1)}, bf16[1,528,256]{2,1,0:T(8,128)(2,1)}, u32[]{:S(2)}, u32[]{:S(2)}) collective-permute-start(bf16[1,528,256]{2,1,0:T(8,128)(2,1)} %copy-done.41), channel_id=1, source_target_pairs={{0,1},{1,0},{2,3},{3,2},{4,5},{5,4},{6,7},{7,6},{8,9},{9,8},{10,11... | collective-permute-start | bytes 811016 | tf_op jit(solution)/shard_map/ppermute | solution.py:23
  90.3 29.3 %collective-permute-start.26 = (bf16[4,128,256]{2,1,0:T(8,128)(2,1)S(1)}, bf16[4,128,256]{2,1,0:T(8,128)(2,1)}, u32[]{:S(2)}, u32[]{:S(2)}) collective-permute-start(bf16[4,128,256]{2,1,0:T(8,128)(2,1)S(1)} %copy-done.19), channel_id=1, source_target_pairs={{0,1},{1,0},{2,3},{3,2},{4,5},{5,4},{6,7},{7,6},{8,9},{9,8},{10,11... | collective-permute-start | bytes 786440 | tf_op jit(solution)/shard_map/ppermute | solution.py:23
  92.1 34.3 %collective-permute-start.30 = (bf16[4,128,256]{2,1,0:T(8,128)(2,1)}, bf16[4,128,256]{2,1,0:T(8,128)(2,1)}, u32[]{:S(2)}, u32[]{:S(2)}) collective-permute-start(bf16[4,128,256]{2,1,0:T(8,128)(2,1)} %copy-done.28), channel_id=1, source_target_pairs={{0,1},{1,0},{2,3},{3,2},{4,5},{5,4},{6,7},{7,6},{8,9},{9,8},{10,11... | collective-permute-start | bytes 786440 | tf_op jit(solution)/shard_map/ppermute | solution.py:23
  92.6 28.3 %collective-permute-start.28 = (bf16[2,128,256]{2,1,0:T(8,128)(2,1)}, bf16[2,128,256]{2,1,0:T(8,128)(2,1)}, u32[]{:S(2)}, u32[]{:S(2)}) collective-permute-start(bf16[2,128,256]{2,1,0:T(8,128)(2,1)} %collective-permute-done.24.u2), channel_id=1, source_target_pairs={{0,1},{1,0},{2,3},{3,2},{4,5},{5,4},{6,7},{7,6},{8,9},{9,8},{10,11... | collective-permute-start | bytes 393224 | tf_op jit(solution)/shard_map/ppermute | solution.py:23
  92.7 29.9 %collective-permute-start.29 = (bf16[2,128,256]{2,1,0:T(8,128)(2,1)}, bf16[2,128,256]{2,1,0:T(8,128)(2,1)}, u32[]{:S(2)}, u32[]{:S(2)}) collective-permute-start(bf16[2,128,256]{2,1,0:T(8,128)(2,1)} %collective-permute-done.25.u3), channel_id=1, source_target_pairs={{0,1},{1,0},{2,3},{3,2},{4,5},{5,4},{6,7},{7,6},{8,9},{9,8},{10,11... | collective-permute-start | bytes 393224 | tf_op jit(solution)/shard_map/ppermute | solution.py:23
  95.8 32.6 %collective-permute-start.27 = (bf16[4,128,256]{2,1,0:T(8,128)(2,1)}, bf16[4,128,256]{2,1,0:T(8,128)(2,1)}, u32[]{:S(2)}, u32[]{:S(2)}) collective-permute-start(bf16[4,128,256]{2,1,0:T(8,128)(2,1)} %collective-permute-done.22.u1), channel_id=1, source_target_pairs={{0,1},{1,0},{2,3},{3,2},{4,5},{5,4},{6,7},{7,6},{8,9},{9,8},{10,11... | collective-permute-start | bytes 786440 | tf_op jit(solution)/shard_map/ppermute | solution.py:23
  119.5 48.3 %collective-permute-start.43 = (bf16[4,2,352,256]{3,2,1,0:T(8,128)(2,1)S(1)}, bf16[4,2,352,256]{3,2,1,0:T(8,128)(2,1)S(1)}, u32[]{:S(2)}, u32[]{:S(2)}) collective-permute-start(bf16[4,2,352,256]{3,2,1,0:T(8,128)(2,1)S(1)} %pad_maximum_fusion.g0), channel_id=1, source_target_pairs={{0,32},{32,64},{64,96},{96,0},{1,33},{33,65},{65,97},{97,1},{2,34}... | collective-permute-start | bytes 4325384 | tf_op jit(solution)/shard_map/ppermute | solution.py:23
  120.9 47.1 %collective-permute-start.42 = (bf16[4,2,352,256]{3,2,1,0:T(8,128)(2,1)S(1)}, bf16[4,2,352,256]{3,2,1,0:T(8,128)(2,1)}, u32[]{:S(2)}, u32[]{:S(2)}) collective-permute-start(bf16[4,2,352,256]{3,2,1,0:T(8,128)(2,1)S(1)} %pad_maximum_fusion.g0), channel_id=1, source_target_pairs={{0,96},{32,0},{64,32},{96,64},{1,97},{33,1},{65,33},{97,65},{2,98}... | collective-permute-start | bytes 4325384 | tf_op jit(solution)/shard_map/ppermute | solution.py:23
  122.6 5.8 %collective-permute-start.18 = (bf16[528,256]{1,0:T(8,128)(2,1)}, bf16[528,256]{1,0:T(8,128)(2,1)}, u32[]{:S(2)}, u32[]{:S(2)}) collective-permute-start(bf16[528,256]{1,0:T(8,128)(2,1)} %get-tuple-element.23), channel_id=1, source_target_pairs={{0,1},{1,0},{2,3},{3,2},{4,5},{5,4},{6,7},{7,6},{8,9},{9,8},{10,11... | collective-permute-start | bytes 811016 | tf_op jit(solution)/shard_map/ppermute | solution.py:23
  126.4 11.2 %collective-permute-start.34 = (f32[3,128,128]{2,1,0:T(8,128)}, f32[3,128,128]{2,1,0:T(8,128)}, u32[]{:S(2)}, u32[]{:S(2)}) collective-permute-start(f32[3,128,128]{2,1,0:T(8,128)} %slice_bitcast_fusion), channel_id=1, source_target_pairs={{0,8},{8,0},{1,9},{9,1},{2,10},{10,2},{3,11},{11,3},{4,12},{12,4},... | collective-permute-start | bytes 589832 | tf_op jit(solution)/shard_map/ppermute | solution.py:23
  135.1 15.3 %collective-permute-start.31 = (bf16[2,528,256]{2,1,0:T(8,128)(2,1)}, bf16[2,528,256]{2,1,0:T(8,128)(2,1)S(1)}, u32[]{:S(2)}, u32[]{:S(2)}) collective-permute-start(bf16[2,528,256]{2,1,0:T(8,128)(2,1)} %get-tuple-element.27), channel_id=1, source_target_pairs={{0,2},{2,4},{4,6},{6,0},{1,3},{3,5},{5,7},{7,1},{8,10},{10,12},{12... | collective-permute-start | bytes 1622024 | tf_op jit(solution)/shard_map/ppermute | solution.py:23
  135.2 26.4 %collective-permute-start.32 = (bf16[2,528,256]{2,1,0:T(8,128)(2,1)}, bf16[2,528,256]{2,1,0:T(8,128)(2,1)S(1)}, u32[]{:S(2)}, u32[]{:S(2)}) collective-permute-start(bf16[2,528,256]{2,1,0:T(8,128)(2,1)} %get-tuple-element.28), channel_id=1, source_target_pairs={{0,4},{2,6},{4,0},{6,2},{1,5},{3,7},{5,1},{7,3},{8,12},{10,14},{12... | collective-permute-start | bytes 1622024 | tf_op jit(solution)/shard_map/ppermute | solution.py:23
  137.6 25.6 %collective-permute-start.33 = (bf16[2,528,256]{2,1,0:T(8,128)(2,1)}, bf16[2,528,256]{2,1,0:T(8,128)(2,1)S(1)}, u32[]{:S(2)}, u32[]{:S(2)}) collective-permute-start(bf16[2,528,256]{2,1,0:T(8,128)(2,1)} %get-tuple-element.29), channel_id=1, source_target_pairs={{0,6},{2,0},{4,2},{6,4},{1,7},{3,1},{5,3},{7,5},{8,14},{10,8},{12,... | collective-permute-start | bytes 1622024 | tf_op jit(solution)/shard_map/ppermute | solution.py:23
  150.4 21.6 %collective-permute-start.52 = (bf16[352,256]{1,0:T(8,128)(2,1)}, bf16[352,256]{1,0:T(8,128)(2,1)S(1)}, u32[]{:S(2)}, u32[]{:S(2)}) collective-permute-start(bf16[352,256]{1,0:T(8,128)(2,1)} %convert_element_type.51), channel_id=1, source_target_pairs={{0,16},{8,24},{16,0},{24,8},{1,17},{9,25},{17,1},{25,9},{2,18},{10... | collective-permute-start | bytes 540680 | tf_op jit(solution)/shard_map/ppermute | solution.py:353
  161.6 10.5 %collective-permute-start.51 = (bf16[352,256]{1,0:T(8,128)(2,1)}, bf16[352,256]{1,0:T(8,128)(2,1)S(1)}, u32[]{:S(2)}, u32[]{:S(2)}) collective-permute-start(bf16[352,256]{1,0:T(8,128)(2,1)} %convert_element_type.51), channel_id=1, source_target_pairs={{0,24},{8,0},{16,8},{24,16},{1,25},{9,1},{17,9},{25,17},{2,26},{10... | collective-permute-start | bytes 540680 | tf_op jit(solution)/shard_map/ppermute | solution.py:353
  163.2 28.1 %collective-permute-start.46 = (bf16[4,2,352,256]{3,2,1,0:T(8,128)(2,1)S(1)}, bf16[4,2,352,256]{3,2,1,0:T(8,128)(2,1)S(1)}, u32[]{:S(2)}, u32[]{:S(2)}) collective-permute-start(bf16[4,2,352,256]{3,2,1,0:T(8,128)(2,1)S(1)} %pad_maximum_fusion.g0), channel_id=1, source_target_pairs={{0,1},{1,0},{2,3},{3,2},{4,5},{5,4},{6,7},{7,6},{8,9},{9,8},{10,11... | collective-permute-start | bytes 4325384 | tf_op jit(solution)/shard_map/ppermute | solution.py:23
  167.9 19.0 %collective-permute-start.44 = (bf16[2,2,352,256]{3,2,1,0:T(8,128)(2,1)S(1)}, bf16[2,2,352,256]{3,2,1,0:T(8,128)(2,1)S(1)}, u32[]{:S(2)}, u32[]{:S(2)}) collective-permute-start(bf16[2,2,352,256]{3,2,1,0:T(8,128)(2,1)S(1)} %slice.134), channel_id=1, source_target_pairs={{0,32},{32,64},{64,96},{96,0},{1,33},{33,65},{65,97},{97,1},{2,34}... | collective-permute-start | bytes 2162696 | tf_op jit(solution)/shard_map/ppermute | solution.py:23
  169.5 18.2 %collective-permute-start.45 = (bf16[2,2,352,256]{3,2,1,0:T(8,128)(2,1)S(1)}, bf16[2,2,352,256]{3,2,1,0:T(8,128)(2,1)S(1)}, u32[]{:S(2)}, u32[]{:S(2)}) collective-permute-start(bf16[2,2,352,256]{3,2,1,0:T(8,128)(2,1)S(1)} %slice.135), channel_id=1, source_target_pairs={{0,96},{32,0},{64,32},{96,64},{1,97},{33,1},{65,33},{97,65},{2,98}... | collective-permute-start | bytes 2162696 | tf_op jit(solution)/shard_map/ppermute | solution.py:23
  172.0 15.7 %collective-permute-start.36 = (bf16[2,528,256]{2,1,0:T(8,128)(2,1)S(1)}, bf16[2,528,256]{2,1,0:T(8,128)(2,1)S(1)}, u32[]{:S(2)}, u32[]{:S(2)}) collective-permute-start(bf16[2,528,256]{2,1,0:T(8,128)(2,1)S(1)} %add_convert_fusion.1.x0), channel_id=1, source_target_pairs={{0,2},{2,4},{4,6},{6,0},{1,3},{3,5},{5,7},{7,1},{8,10},{10,12},{12... | collective-permute-start | bytes 1622024 | tf_op jit(solution)/shard_map/ppermute | solution.py:23
  172.1 6.8 %collective-permute-start.53 = (bf16[352,256]{1,0:T(8,128)(2,1)S(1)}, bf16[352,256]{1,0:T(8,128)(2,1)S(1)}, u32[]{:S(2)}, u32[]{:S(2)}) collective-permute-start(bf16[352,256]{1,0:T(8,128)(2,1)S(1)} %copy-done.48), channel_id=1, source_target_pairs={{0,8},{8,16},{16,24},{24,0},{1,9},{9,17},{17,25},{25,1},{2,10},{10... | collective-permute-start | bytes 540680 | tf_op jit(solution)/shard_map/ppermute | solution.py:353
  178.9 12.3 %collective-permute-start.35 = (bf16[2,528,256]{2,1,0:T(8,128)(2,1)S(1)}, bf16[2,528,256]{2,1,0:T(8,128)(2,1)S(1)}, u32[]{:S(2)}, u32[]{:S(2)}) collective-permute-start(bf16[2,528,256]{2,1,0:T(8,128)(2,1)S(1)} %add_convert_fusion.1.x0), channel_id=1, source_target_pairs={{0,6},{2,0},{4,2},{6,4},{1,7},{3,1},{5,3},{7,5},{8,14},{10,8},{12,... | collective-permute-start | bytes 1622024 | tf_op jit(solution)/shard_map/ppermute | solution.py:23
  186.9 21.7 %collective-permute-start.50 = (bf16[4,2,352,256]{3,2,1,0:T(8,128)(2,1)S(1)}, bf16[4,2,352,256]{3,2,1,0:T(8,128)(2,1)S(1)}, u32[]{:S(2)}, u32[]{:S(2)}) collective-permute-start(bf16[4,2,352,256]{3,2,1,0:T(8,128)(2,1)S(1)} %collective-permute-done.43.g4), channel_id=1, source_target_pairs={{0,1},{1,0},{2,3},{3,2},{4,5},{5,4},{6,7},{7,6},{8,9},{9,8},{10,11... | collective-permute-start | bytes 4325384 | tf_op jit(solution)/shard_map/ppermute | solution.py:23
  187.7 18.2 %collective-permute-start.55 = (bf16[4,352,256]{2,1,0:T(8,128)(2,1)S(1)}, bf16[4,352,256]{2,1,0:T(8,128)(2,1)S(1)}, u32[]{:S(2)}, u32[]{:S(2)}) collective-permute-start(bf16[4,352,256]{2,1,0:T(8,128)(2,1)S(1)} %pad_maximum_fusion.2.d0), channel_id=1, source_target_pairs={{0,32},{32,64},{64,96},{96,0},{1,33},{33,65},{65,97},{97,1},{2,34}... | collective-permute-start | bytes 2162696 | tf_op jit(solution)/shard_map/ppermute | solution.py:23
  187.7 19.9 %collective-permute-start.54 = (bf16[4,352,256]{2,1,0:T(8,128)(2,1)S(1)}, bf16[4,352,256]{2,1,0:T(8,128)(2,1)S(1)}, u32[]{:S(2)}, u32[]{:S(2)}) collective-permute-start(bf16[4,352,256]{2,1,0:T(8,128)(2,1)S(1)} %pad_maximum_fusion.2.d0), channel_id=1, source_target_pairs={{0,96},{32,0},{64,32},{96,64},{1,97},{33,1},{65,33},{97,65},{2,98}... | collective-permute-start | bytes 2162696 | tf_op jit(solution)/shard_map/ppermute | solution.py:23
  191.3 7.3 %collective-permute-start.37 = (bf16[1,528,256]{2,1,0:T(8,128)(2,1)S(1)}, bf16[1,528,256]{2,1,0:T(8,128)(2,1)S(1)}, u32[]{:S(2)}, u32[]{:S(2)}) collective-permute-start(bf16[1,528,256]{2,1,0:T(8,128)(2,1)S(1)} %slice.132), channel_id=1, source_target_pairs={{0,2},{2,4},{4,6},{6,0},{1,3},{3,5},{5,7},{7,1},{8,10},{10,12},{12... | collective-permute-start | bytes 811016 | tf_op jit(solution)/shard_map/ppermute | solution.py:23
  191.3 10.6 %collective-permute-start.38 = (bf16[1,528,256]{2,1,0:T(8,128)(2,1)S(1)}, bf16[1,528,256]{2,1,0:T(8,128)(2,1)S(1)}, u32[]{:S(2)}, u32[]{:S(2)}) collective-permute-start(bf16[1,528,256]{2,1,0:T(8,128)(2,1)S(1)} %slice.133), channel_id=1, source_target_pairs={{0,6},{2,0},{4,2},{6,4},{1,7},{3,1},{5,3},{7,5},{8,14},{10,8},{12,... | collective-permute-start | bytes 811016 | tf_op jit(solution)/shard_map/ppermute | solution.py:23
  198.6 9.2 %collective-permute-start.48 = (bf16[2,2,352,256]{3,2,1,0:T(8,128)(2,1)S(1)}, bf16[2,2,352,256]{3,2,1,0:T(8,128)(2,1)S(1)}, u32[]{:S(2)}, u32[]{:S(2)}) collective-permute-start(bf16[2,2,352,256]{3,2,1,0:T(8,128)(2,1)S(1)} %collective-permute-done.44.g2), channel_id=1, source_target_pairs={{0,1},{1,0},{2,3},{3,2},{4,5},{5,4},{6,7},{7,6},{8,9},{9,8},{10,11... | collective-permute-start | bytes 2162696 | tf_op jit(solution)/shard_map/ppermute | solution.py:23
  201.9 19.4 %collective-permute-start.47 = (bf16[4,2,352,256]{3,2,1,0:T(8,128)(2,1)}, bf16[4,2,352,256]{3,2,1,0:T(8,128)(2,1)S(1)}, u32[]{:S(2)}, u32[]{:S(2)}) collective-permute-start(bf16[4,2,352,256]{3,2,1,0:T(8,128)(2,1)} %collective-permute-done.42.g1), channel_id=1, source_target_pairs={{0,1},{1,0},{2,3},{3,2},{4,5},{5,4},{6,7},{7,6},{8,9},{9,8},{10,11... | collective-permute-start | bytes 4325384 | tf_op jit(solution)/shard_map/ppermute | solution.py:23
  205.9 3.5 %collective-permute-start.58 = (bf16[4,352,256]{2,1,0:T(8,128)(2,1)S(1)}, bf16[4,352,256]{2,1,0:T(8,128)(2,1)S(1)}, u32[]{:S(2)}, u32[]{:S(2)}) collective-permute-start(bf16[4,352,256]{2,1,0:T(8,128)(2,1)S(1)} %pad_maximum_fusion.2.d0), channel_id=1, source_target_pairs={{0,1},{1,0},{2,3},{3,2},{4,5},{5,4},{6,7},{7,6},{8,9},{9,8},{10,11... | collective-permute-start | bytes 2162696 | tf_op jit(solution)/shard_map/ppermute | solution.py:23
  207.8 10.9 %collective-permute-start.56 = (bf16[2,352,256]{2,1,0:T(8,128)(2,1)S(1)}, bf16[2,352,256]{2,1,0:T(8,128)(2,1)S(1)}, u32[]{:S(2)}, u32[]{:S(2)}) collective-permute-start(bf16[2,352,256]{2,1,0:T(8,128)(2,1)S(1)} %slice.136), channel_id=1, source_target_pairs={{0,32},{32,64},{64,96},{96,0},{1,33},{33,65},{65,97},{97,1},{2,34}... | collective-permute-start | bytes 1081352 | tf_op jit(solution)/shard_map/ppermute | solution.py:23
  208.7 12.7 %collective-permute-start.62 = (bf16[4,352,256]{2,1,0:T(8,128)(2,1)S(1)}, bf16[4,352,256]{2,1,0:T(8,128)(2,1)S(1)}, u32[]{:S(2)}, u32[]{:S(2)}) collective-permute-start(bf16[4,352,256]{2,1,0:T(8,128)(2,1)S(1)} %collective-permute-done.55.d4), channel_id=1, source_target_pairs={{0,1},{1,0},{2,3},{3,2},{4,5},{5,4},{6,7},{7,6},{8,9},{9,8},{10,11... | collective-permute-start | bytes 2162696 | tf_op jit(solution)/shard_map/ppermute | solution.py:23
  209.4 11.9 %collective-permute-start.59 = (bf16[4,352,256]{2,1,0:T(8,128)(2,1)S(1)}, bf16[4,352,256]{2,1,0:T(8,128)(2,1)S(1)}, u32[]{:S(2)}, u32[]{:S(2)}) collective-permute-start(bf16[4,352,256]{2,1,0:T(8,128)(2,1)S(1)} %collective-permute-done.54.d1), channel_id=1, source_target_pairs={{0,1},{1,0},{2,3},{3,2},{4,5},{5,4},{6,7},{7,6},{8,9},{9,8},{10,11... | collective-permute-start | bytes 2162696 | tf_op jit(solution)/shard_map/ppermute | solution.py:23
  210.5 9.6 %collective-permute-start.57 = (bf16[2,352,256]{2,1,0:T(8,128)(2,1)S(1)}, bf16[2,352,256]{2,1,0:T(8,128)(2,1)S(1)}, u32[]{:S(2)}, u32[]{:S(2)}) collective-permute-start(bf16[2,352,256]{2,1,0:T(8,128)(2,1)S(1)} %slice.137), channel_id=1, source_target_pairs={{0,96},{32,0},{64,32},{96,64},{1,97},{33,1},{65,33},{97,65},{2,98}... | collective-permute-start | bytes 1081352 | tf_op jit(solution)/shard_map/ppermute | solution.py:23
  247.4 26.6 %collective-permute-start.63 = (bf16[2,528,256]{2,1,0:T(8,128)(2,1)}, bf16[2,528,256]{2,1,0:T(8,128)(2,1)S(1)}, u32[]{:S(2)}, u32[]{:S(2)}) collective-permute-start(bf16[2,528,256]{2,1,0:T(8,128)(2,1)} %get-tuple-element.37), channel_id=1, source_target_pairs={{0,2},{2,4},{4,6},{6,0},{1,3},{3,5},{5,7},{7,1},{8,10},{10,12},{12... | collective-permute-start | bytes 1622024 | tf_op jit(solution)/shard_map/ppermute | solution.py:23
  247.5 26.5 %collective-permute-start.64 = (bf16[2,528,256]{2,1,0:T(8,128)(2,1)}, bf16[2,528,256]{2,1,0:T(8,128)(2,1)S(1)}, u32[]{:S(2)}, u32[]{:S(2)}) collective-permute-start(bf16[2,528,256]{2,1,0:T(8,128)(2,1)} %get-tuple-element.38), channel_id=1, source_target_pairs={{0,4},{2,6},{4,0},{6,2},{1,5},{3,7},{5,1},{7,3},{8,12},{10,14},{12... | collective-permute-start | bytes 1622024 | tf_op jit(solution)/shard_map/ppermute | solution.py:23
  248.2 26.1 %collective-permute-start.65 = (bf16[2,528,256]{2,1,0:T(8,128)(2,1)}, bf16[2,528,256]{2,1,0:T(8,128)(2,1)S(1)}, u32[]{:S(2)}, u32[]{:S(2)}) collective-permute-start(bf16[2,528,256]{2,1,0:T(8,128)(2,1)} %get-tuple-element.39), channel_id=1, source_target_pairs={{0,6},{2,0},{4,2},{6,4},{1,7},{3,1},{5,3},{7,5},{8,14},{10,8},{12,... | collective-permute-start | bytes 1622024 | tf_op jit(solution)/shard_map/ppermute | solution.py:23
  276.9 13.1 %all-to-all-start.1 = ((bf16[4,528,128]{2,1,0:T(8,128)(2,1)}), bf16[4,528,128]{2,1,0:T(8,128)(2,1)S(1)}, u32[]{:S(2)}, u32[]{:S(2)}) async-start(bf16[4,528,128]{2,1,0:T(8,128)(2,1)} %bitcast.43), calls=%async_computation.1 | async-start | bytes 1081344 | tf_op jit(solution)/shard_map/all_to_all | solution.py:431
  (58 other events, 802.7 us)

commit v2 on v1

--- a/solution.py
+++ b/solution.py
@@ -5,6 +5,7 @@
 import numpy as np
 from jax import lax
 from jax.experimental import pallas as pl
+from jax.experimental.layout import Layout, with_layout_constraint
 from jax.experimental.pallas import tpu as pltpu
 from jax.sharding import Mesh, PartitionSpec as P
 
@@ -32,19 +33,10 @@
     return [own, ahead, far0, far1, before]
 
 
-def piece(refs, step, part, parts=2):
+def piece(refs, step, part):
     if step == 2:
-        n = parts // 2
-        return refs[2 + part // n].at[part % n]
+        return refs[2 + part].at[0]
     return refs[{0: 0, 1: 1, 3: 4}[step]].at[part]
-
-
-def weight_blocks(refs, idx):
-    y, z = idx[0], idx[1] * 2 + idx[2]
-    for k in range(4):
-        for j in range(4):
-            r = 2 * ((y + k) & 3) + (((z + j) & 3) >> 1)
-            yield piece(refs, k, j, 4), j & 1, r
 
 
 def level_matrix():
@@ -101,27 +93,28 @@
 
 
 def mix_kernel(
-    idx, xo0, xo1, xo2, xo3, xo4, xp0, xp1, xp2, xp3, xp4, w0, w1, w2, w3, w4,
+    idx, xo0, xo1, xo2, xo3, xo4, xpm, xp2, xp3, w_ref,
     bias_ref, gain_ref, mat_ref, dst_ref,
-    own_ref, other_ref, state_ref,
+    own_ref, other_ref, keep_ref, send_ref,
     xcat, wcat, mix, oscr, carry, sems,
 ):
     x, c, length = idx[3], idx[4], idx[5]
-    copies = x_copies((xo0, xo1, xo2, xo3, xo4), xcat.at[0], x)
-    copies += x_copies((xp0, xp1, xp2, xp3, xp4), xcat.at[1], x)
-    for ref, j, r in weight_blocks((w0, w1, w2, w3, w4), idx):
-        copies.append((ref, wcat.at[j * 384 : (j + 1) * 384, col(r)]))
+    copies = x_copies((xo0, xo1, xo2, xo3, xo4), xcat.at[0:HALF], x)
+    copies += x_copies((xpm.at[0], xpm.at[1], xp2, xp3, xpm.at[2]), xcat.at[HALF : 2 * HALF], x)
+    for i in range(16):
+        at = pl.multiple_of(((i & 1) ^ idx[2]) * 384, 128)
+        r = i // 2
+        copies.append((w_ref.at[i, 0:384], wcat.at[pl.ds(at, 384), r * 256 : (r + 1) * 256]))
     for cp in copy_all(copies, sems):
         cp.wait()
-    for hr in range(2):
-        ha = (c + hr) & 1
-
-        def project(i, unused, hr=hr, ha=ha):
-            rows = pl.ds(pl.multiple_of(i * 176, 16), 176)
-            mix[ha, rows, :] = dot_nt(xcat[hr, rows, :], wcat[...])
-            return unused
-
-        lax.fori_loop(0, 3, project, 0)
+
+    def project(i, unused):
+        part = dot_nt(xcat[...], wcat[pl.ds(pl.multiple_of(i * 256, 256), 256), :])
+        mix[c, :, col(i)] = part[:HALF]
+        mix[1 - c, :, col(i)] = part[HALF:]
+        return unused
+
+    lax.fori_loop(0, 3, project, 0)
     carry[...] = jnp.zeros_like(carry)
     t = lax.broadcasted_iota(jnp.int32, (CH, CH), 0)
     s = lax.broadcasted_iota(jnp.int32, (CH, CH), 1)
@@ -174,12 +167,12 @@
             kt = jnp.broadcast_to(k, (128, 128)).T
             qt = jnp.broadcast_to(q, (128, 128)).T
             nxt = ft * dst_ref[j, h] + kt * v
-            state_ref[j, h] = nxt
+            (keep_ref, send_ref)[j][h] = nxt
             o = head_out(jnp.sum(nxt * qt, axis=0, keepdims=True), gain_ref[j : j + 1, :])
             wide = jnp.where(first, jnp.broadcast_to(o, (16, 128)), 0.0)
             oscr[h, 512:528, j * 128 : (j + 1) * 128] = wide.astype(BF)
     for j in range(2):
-        state_ref[j, 2] = carry[j].T
+        (keep_ref, send_ref)[j][2] = carry[j].T
     own_ref[...] = oscr[c]
     other_ref[...] = oscr[1 - c]
 
@@ -194,6 +187,10 @@
 
 def sspec():
     return pl.BlockSpec(memory_space=pltpu.SMEM)
+
+
+def cost(us):
+    return pl.CostEstimate(flops=us, transcendentals=0, bytes_accessed=us)
 
 
 def mix_call(idx, xo, xp, w, bias, gain, dst):
@@ -203,12 +200,13 @@
         out_shape=(
             jax.ShapeDtypeStruct((HALF, 256), BF),
             jax.ShapeDtypeStruct((HALF, 256), BF),
-            jax.ShapeDtypeStruct((2, 3, 128, 128), F32),
+            jax.ShapeDtypeStruct((3, 128, 128), F32),
+            jax.ShapeDtypeStruct((3, 128, 128), F32),
         ),
-        in_specs=[sspec()] + [anyspec()] * 15 + [vspec()] * 4,
-        out_specs=(vspec(),) * 3,
+        in_specs=[sspec()] + [anyspec()] * 9 + [vspec()] * 4,
+        out_specs=(vspec(),) * 4,
         scratch_shapes=[
-            pltpu.VMEM((2, HALF, 2048), BF),
+            pltpu.VMEM((2 * HALF, 2048), BF),
             pltpu.VMEM((768, 2048), BF),
             pltpu.VMEM((2, HALF, 768), F32),
             pltpu.VMEM((2, HALF, 256), BF),
@@ -216,8 +214,9 @@
             pltpu.SemaphoreType.DMA((32,)),
         ],
         compiler_params=pltpu.CompilerParams(vmem_limit_bytes=VMEM_LIMIT),
+        cost_estimate=cost(24),
         name="mix",
-    )(idx, *xo, *xp, *w, bias, gain, mat, dst)
+    )(idx, *xo, *xp, w, bias, gain, mat, dst)
 
 
 def spread(out_s, x, p0, p1, p2, p3):
@@ -236,14 +235,15 @@
 
 
 def out_kernel(
-    idx, a_ref, b_ref, u0, u1, u2, u3, u4, v0, v1, v2, v3, v4,
+    idx, a_ref, b_ref, u_ref, v_ref,
     p0, p1, p2, p3, ocat, wcat, out_s, sems,
 ):
     copies = [(a_ref, ocat.at[:, 0:256]), (b_ref, ocat.at[:, 256:512])]
-    for cc, refs in ((0, (u0, u1, u2, u3, u4)), (1, (v0, v1, v2, v3, v4))):
-        for ref, j, r in weight_blocks(refs, idx):
-            at = cc * 256 + j * 128
-            copies.append((ref, wcat.at[r, at : at + 128, :]))
+    for i in range(16):
+        for cc in range(2):
+            src = v_ref.at[i] if cc else u_ref.at[i, 384:512]
+            at = pl.multiple_of(cc * 256 + ((i & 1) ^ idx[2]) * 128, 128)
+            copies.append((src, wcat.at[i // 2, pl.ds(at, 128), :]))
     for cp in copy_all(copies, sems):
         cp.wait()
 
@@ -259,7 +259,7 @@
     return pl.pallas_call(
         out_kernel,
         out_shape=PARTS,
-        in_specs=[sspec()] + [anyspec()] * 12,
+        in_specs=[sspec()] + [anyspec()] * 4,
         out_specs=(vspec(),) * 4,
         scratch_shapes=[
             pltpu.VMEM((HALF, 512), BF),
@@ -268,29 +268,32 @@
             pltpu.SemaphoreType.DMA((34,)),
         ],
         compiler_params=pltpu.CompilerParams(vmem_limit_bytes=VMEM_LIMIT),
+        cost_estimate=cost(7),
         name="outp",
-    )(idx, a, b, *u, *v)
+    )(idx, a, b, u, v)
 
 
 def mlp_kernel(
-    idx, x0, x1, x2, x3, x4, g0, g1, g2, g3, g4, h0, h1, h2, h3, h4,
-    d0, d1, d2, d3, d4, e0, e1, e2, e3, e4, gain_ref,
+    idx, x0, x1, x2, x3, x4, g_ref, h_ref, gain_ref,
     p0, p1, p2, p3, xcat, wg, wd, hid, out_s, sems,
 ):
     x = idx[3]
     first = copy_all(x_copies((x0, x1, x2, x3, x4), xcat, x), sems)
     copies = []
-    for cc, refs in ((0, (g0, g1, g2, g3, g4)), (1, (h0, h1, h2, h3, h4))):
-        for ref, j, r in weight_blocks(refs, idx):
-            at = cc * 704 + j * 352
-            copies.append((ref, wg.at[:, at : at + 352, col(r)]))
-    second = copy_all(copies, sems.at[8:40])
+    for cc, ref in ((0, g_ref), (1, h_ref)):
+        for i in range(16):
+            at, r = cc * 704 + (i & 1) * 352, i // 2
+            for g in range(2):
+                dst = wg.at[g, at : at + 352, r * 256 : (r + 1) * 256]
+                copies.append((ref.at[i, g * 352 : (g + 1) * 352], dst))
+    second = copy_all(copies, sems.at[8:72])
     copies = []
-    for cc, refs in ((0, (d0, d1, d2, d3, d4)), (1, (e0, e1, e2, e3, e4))):
-        for ref, j, r in weight_blocks(refs, idx):
-            at = cc * 704 + j * 352
-            copies.append((ref, wd.at[at : at + 352, col(r)]))
-    third = copy_all(copies, sems.at[40:72])
+    for cc, ref in ((0, g_ref), (1, h_ref)):
+        for i in range(16):
+            at, r = cc * 704 + (i & 1) * 352, i // 2
+            dst = wd.at[at : at + 352, r * 256 : (r + 1) * 256]
+            copies.append((ref.at[i, 704:1056], dst))
+    third = copy_all(copies, sems.at[72:104])
     for cp in first:
         cp.wait()
 
@@ -305,15 +308,10 @@
     for cp in second:
         cp.wait()
 
-    def expand(i, unused):
-        rows = pl.ds(pl.multiple_of(i * 176, 16), 176)
-        xv = xcat[rows, :]
-        gate = dot_nt(xv, wg[0])
-        up = dot_nt(xv, wg[1])
-        hid[rows, :] = (gate / (1.0 + jnp.exp(-gate)) * up).astype(BF)
-        return unused
-
-    lax.fori_loop(0, 3, expand, 0)
+    for lo, hi in ((0, 768), (768, 1408)):
+        gate = dot_nt(xcat[...], wg[0, lo:hi, :])
+        up = dot_nt(xcat[...], wg[1, lo:hi, :])
+        hid[:, lo:hi] = (gate / (1.0 + jnp.exp(-gate)) * up).astype(BF)
     for cp in third:
         cp.wait()
 
@@ -325,11 +323,11 @@
     spread(out_s, x, p0, p1, p2, p3)
 
 
-def mlp_call(idx, xs, g, h, d, e, gain):
+def mlp_call(idx, xs, g, h, gain):
     return pl.pallas_call(
         mlp_kernel,
         out_shape=PARTS,
-        in_specs=[sspec()] + [anyspec()] * 25 + [vspec()],
+        in_specs=[sspec()] + [anyspec()] * 7 + [vspec()],
         out_specs=(vspec(),) * 4,
         scratch_shapes=[
             pltpu.VMEM((HALF, 2048), BF),
@@ -337,31 +335,28 @@
             pltpu.VMEM((1408, 2048), BF),
             pltpu.VMEM((HALF, 1408), BF),
             pltpu.VMEM((8, HALF, 256), F32),
-            pltpu.SemaphoreType.DMA((72,)),
+            pltpu.SemaphoreType.DMA((104,)),
         ],
         compiler_params=pltpu.CompilerParams(vmem_limit_bytes=VMEM_LIMIT),
+        cost_estimate=cost(20),
         name="mlp",
-    )(idx, *xs, *g, *h, *d, *e, gain)
+    )(idx, *xs, g, h, gain)
 
 
 def swap(value, axis):
     return shift(value, axis, 1)
 
 
-def z_gather(local):
-    perm = lambda step: [(i, (i + step) % 4) for i in range(4)]
-    return jnp.stack([local] + [lax.ppermute(local, ("zh", "zl"), perm(-k)) for k in (1, 2, 3)])
-
-
 def after(value, *others):
     return lax.optimization_barrier((value,) + others)[0]
 
 
-def reduce_parts(parts):
+def reduce_parts(parts, *others):
     p0, p1, p2, p3 = parts
     r2 = shift(p2, "x", 2)
     r1 = shift(p1, "x", 1)
     r3 = shift(p3, "x", -1)
+    r1 = after(r1, r2, r3, *others)
     return p0 + r1.astype(F32) + r2.astype(F32) + r3.astype(F32)
 
 
@@ -385,33 +380,31 @@
     got = lax.all_to_all(rows, ("zl", "c"), 0, 0, tiled=True)
     x_own = got.reshape(2, 2, HALF, 128).transpose(0, 2, 1, 3).reshape(2, HALF, 256)
 
-    fio = z_gather(w_fio.astype(BF).T)
-    fio = ring_gather(fio, "y")
-    xs = ring_gather(x_own, "x")
-    xp = [swap(v, "c") for v in xs]
-
-    wo = z_gather(after(w_out, x_own, fio[0]).astype(BF))
-    wo = ring_gather(after(wo, fio[1], fio[4]), "y")
-    wo2 = [swap(v, "c") for v in wo]
-    gu = z_gather(after(w_gu, wo[0]).astype(BF).T.reshape(2, 352, 256))
-    gu = ring_gather(after(gu, fio[2], fio[3], wo[1], wo[4]), "y")
-    gu2 = [swap(v, "c") for v in gu]
-    wd = z_gather(after(w_down, gu[0]).astype(BF))
-    wd = ring_gather(after(wd, gu[2], gu[3]), "y")
-    wd2 = [swap(v, "c") for v in wd]
-
     small = jnp.stack([forget_bias, head_gain])
-    small2 = swap(small, "zl")
-    bias = jnp.stack([small[0], small2[0]])
-    gain = jnp.stack([small[1], small2[1]])
-    ds = decode_states.reshape(2, 2, 128, 128)
+    ds = decode_states.reshape(2, 256, 128)
     ds_keep = jnp.where(zl == 0, ds[0], ds[1])
     ds_send = jnp.where(zl == 0, ds[1], ds[0])
-    dst = jnp.stack([ds_keep, swap(ds_send, "zl")])
-
-    ho, hs, states = mix_call(idx, xs, xp, fio, bias, gain, dst)
+    other = swap(jnp.concatenate([ds_send, small]), "zl")
+    early = jnp.concatenate([w_fio.astype(BF).T, w_out.astype(BF)])
+    early = with_layout_constraint(early, Layout((0, 1)))
+    early = lax.all_gather(early, ("y", "zh", "zl")).reshape(16, 512, 256)
+    x_own, other = lax.optimization_barrier((x_own, other))
+    bias = jnp.stack([small[0], other[256]])
+    gain = jnp.stack([small[1], other[257]])
+    dst = jnp.stack([ds_keep, other[:256]]).reshape(2, 2, 128, 128)
+
+    x_before, x_ahead = shift(x_own, "x", 1), shift(x_own, "x", -1)
+    x_mid = swap(jnp.stack([x_own, x_ahead, x_before]), "c")
+    xs = [x_own, x_ahead, shift(x_before[:1], "x", 1), shift(x_ahead[1:], "x", -1), x_before]
+    xp = [x_mid, swap(xs[2], "c"), swap(xs[3], "c")]
+    wo2 = swap(early[:, 384:], "c")
+    late = jnp.concatenate([w_gu.astype(BF).T, w_down.astype(BF)])
+    late = after(late, early, *xp)
+    late = lax.all_gather(late, ("y", "zh", "zl")).reshape(16, 1056, 256)
+
+    ho, hs, mine, sent = mix_call(idx, xs, xp, early, bias, gain, dst)
     hr = swap(hs, "c")
-    mine, other = states[0], swap(states[1], "zl")
+    other = swap(sent, "zl")
     decode_next = jnp.where(
         zl == 0,
         jnp.concatenate([mine[:2], other[:2]]),
@@ -421,11 +414,11 @@
         zl == 0, jnp.stack([mine[2], other[2]]), jnp.stack([other[2], mine[2]])
     ).reshape(2, 1, 128, 128)
 
-    attention = reduce_parts(out_call(idx, ho, hr, wo, wo2))
-    attention = after(attention, decode_next, prompt_states)
+    attention = reduce_parts(out_call(idx, ho, hr, early, wo2), other)
     residual = (x_own.astype(F32) + attention).astype(BF)
     rs = ring_gather(residual, "x")
-    down = reduce_parts(mlp_call(idx, rs, gu, gu2, wd, wd2, mlp_gain.reshape(1, 2048)))
+    late2 = swap(after(late, rs[1], rs[4]), "c")
+    down = reduce_parts(mlp_call(idx, rs, late, late2, mlp_gain.reshape(1, 2048)))
     layer = (residual.astype(F32) + down).astype(BF)
     layer = layer.reshape(2, HALF, 2, 128).transpose(0, 2, 1, 3).reshape(4, HALF, 128)
     back = lax.all_to_all(layer, ("zl", "c"), 0, 0, tiled=True)

time: 292 us -> 233 us (0.80)
  starting transfers between devices: 95.7 us -> 38.9 us
  local copies, waits for them, and re-layouts: 20.5 us -> 6.23 us
  between operations: 2.55 us -> 15.5 us
  waiting for transfers between devices: 103 us -> 113 us
  Pallas kernels: 54.2 us -> 47.5 us
  other arithmetic: 15.9 us -> 12.1 us
    ppermute x54 -> x22, starting transfers between devices: 68.4 us -> 29.4 us  [shift(): return lax.ppermute(value, axis, [(i, (i + step) % n) for i in range(n)])]
    ppermute x12 -> x0, starting transfers between devices: 17.4 us -> none  [z_gather(): lax.ppermute(local, ('zh', 'zl'), perm(-k))]
    ppermute x12 -> x0, waiting for transfers between devices: 13.8 us -> none  [z_gather(): lax.ppermute(local, ('zh', 'zl'), perm(-k))]
    ppermute x54 -> x22, waiting for transfers between devices: 76.4 us -> 89 us  [shift(): return lax.ppermute(value, axis, [(i, (i + step) % n) for i in range(n)])]
    all_gather x0 -> x2, waiting for transfers between devices: none -> 10.1 us  [the longest x1 10.1 us: on_device(): early = lax.all_gather(early, ('y', 'zh', 'zl')).reshape(16, 512, 256)]
    slice x6 -> x1, local copies, waits for them, and re-layouts: 4.15 us -> 0.02 us  [ring_gather(): far1 = shift(ahead[n:], axis, -1)]
    pallas_call x1, Pallas kernels: 23.9 us -> 20.2 us  [mlp_call(): pl.pallas_call(mlp_kernel, out_shape=PARTS, in_specs=[sspec()] + [anyspec...]
    pallas_call x1, Pallas kernels: 23.5 us -> 20.4 us  [mix_call(): pl.pallas_call(mix_kernel, out_shape=(jax.ShapeDtypeStruct((HALF, 256), B...]
  transfers between devices with their start and end apart: 68 -> 26, of which waited for: 23 -> 16; matrix products, arithmetic and copies ran while one was open for 10% -> 5% of each run, Pallas kernels for 10% -> 12%
where the time goes in v2:
time: 233 us
  waiting for transfers between devices  113 us (48%)
  Pallas kernels  47.5 us (20%)
  starting transfers between devices  38.9 us (17%)
  between operations  15.5 us (7%)
  other arithmetic  12.1 us (5%)
  local copies, waits for them, and re-layouts  6.23 us (3%)
    ppermute x22, waiting for transfers between devices, shift(): return lax.ppermute(value, axis, [(i, (i + step) % n) for i in range(n)])  89 us
    ppermute x22, starting transfers between devices, shift(): return lax.ppermute(value, axis, [(i, (i + step) % n) for i in range(n)])  29.4 us
    pallas_call x1, Pallas kernels, mix_call(): pl.pallas_call(mix_kernel, out_shape=(jax.ShapeDtypeStruct((HALF, 256), B...  20.4 us
    pallas_call x1, Pallas kernels, mlp_call(): pl.pallas_call(mlp_kernel, out_shape=PARTS, in_specs=[sspec()] + [anyspec...  20.2 us
    all_gather x1, waiting for transfers between devices, on_device(): early = lax.all_gather(early, ('y', 'zh', 'zl')).reshape(16, 512, 256)  10.1 us
    pallas_call x1, Pallas kernels, out_call(): pl.pallas_call(out_kernel, out_shape=PARTS, in_specs=[sspec()] + [anyspec...  6.91 us
    all_to_all x1, waiting for transfers between devices, on_device(): back = lax.all_to_all(layer, ('zl', 'c'), 0, 0, tiled=True)  6.74 us
    all_to_all x1, waiting for transfers between devices, on_device(): got = lax.all_to_all(rows, ('zl', 'c'), 0, 0, tiled=True)  6.62 us
  transfers between devices with their start and end apart: 26, of which 16 were waited for; matrix products, arithmetic and copies ran while one was open for 5% of the time, Pallas kernels for 12%

profile of v2, /device:TPU:1, one launch (start us, length us, event | category | flops | bytes accessed | tf_op | source)
XLA Modules:
  0.0 232.8 jit_solution(18435510396522276066)
XLA Ops:
  7.2 1.0 convert_element_type.44
  8.2 1.1 copy.33
  9.3 0.7 pad_maximum_fusion.3
  10.2 1.0 maximum_maximum_fusion
  11.2 4.9 %all-to-all-start = ((bf16[4,528,128]{2,1,0:T(8,128)(2,1)}), bf16[4,528,128]{2,1,0:T(8,128)(2,1)S(1)}, u32[]{:S(2)}, u32[]{:S(2)}) async-start(bf16[4,528,128]{2,1,0:T(8,128)(2,1)} %maximum_maximum_fusion), calls=%async_computation | async-start | bytes 1081344 | tf_op jit(solution)/shard_map/all_to_all | solution.py:380
  16.1 1.5 collective-permute-start
  17.6 6.6 %all-to-all-done = bf16[4,528,128]{2,1,0:T(8,128)(2,1)S(1)} async-done(((bf16[4,528,128]{2,1,0:T(8,128)(2,1)}), bf16[4,528,128]{2,1,0:T(8,128)(2,1)S(1)}, u32[]{:S(2)}, u32[]{:S(2)}) %all-to-all-start) | async-done | bytes 540704 | tf_op jit(solution)/shard_map/all_to_all | solution.py:380
  24.2 0.1 copy.40
  24.3 2.8 %collective-permute-done = f32[258,128]{1,0:T(8,128)S(1)} collective-permute-done((f32[258,128]{1,0:T(8,128)S(1)}, f32[258,128]{1,0:T(8,128)S(1)}, u32[]{:S(2)}, u32[]{:S(2)}) %collective-permute-start) | collective-permute-done | bytes 132128 | tf_op jit(solution)/shard_map/ppermute | solution.py:24
  27.1 1.3 collective-permute-start.2
  28.4 1.4 collective-permute-start.1
  29.8 10.7 %collective-permute-done.2.xo4 = bf16[2,528,256]{2,1,0:T(8,128)(2,1)S(1)} collective-permute-done((bf16[2,528,256]{2,1,0:T(8,128)(2,1)S(1)}, bf16[2,528,256]{2,1,0:T(8,128)(2,1)S(1)}, u32[]{:S(2)}, u32[]{:S(2)}) %collective-permute-start.2) | collective-permute-done | bytes 540704 | tf_op jit(solution)/shard_map/ppermute | solution.py:24
  40.5 1.5 pad_maximum_fusion
  42.0 2.6 %collective-permute-start.5 = (bf16[3,2,528,256]{3,2,1,0:T(8,128)(2,1)}, bf16[3,2,528,256]{3,2,1,0:T(8,128)(2,1)S(1)}, u32[]{:S(2)}, u32[]{:S(2)}) collective-permute-start(bf16[3,2,528,256]{3,2,1,0:T(8,128)(2,1)} %pad_maximum_fusion), channel_id=1, source_target_pairs={{0,1},{1,0},{2,3},{3,2},{4,5},{5,4},{6,7},{7,6},{8,9},{9,8},{10,11... | collective-permute-start | bytes 4866056 | tf_op jit(solution)/shard_map/ppermute | solution.py:24
  44.6 1.2 collective-permute-start.3
  45.8 1.6 collective-permute-start.4
  47.5 6.6 %collective-permute-done.3.xo2 = bf16[1,528,256]{2,1,0:T(8,128)(2,1)S(1)} collective-permute-done((bf16[1,528,256]{2,1,0:T(8,128)(2,1)S(1)}, bf16[1,528,256]{2,1,0:T(8,128)(2,1)S(1)}, u32[]{:S(2)}, u32[]{:S(2)}) %collective-permute-start.3) | collective-permute-done | bytes 270368 | tf_op jit(solution)/shard_map/ppermute | solution.py:24
  54.1 0.7 collective-permute-start.6
  54.8 0.1 collective-permute-start.7
  55.0 0.9 pad_maximum_fusion.1
  55.8 0.1 collective-permute-done.6.xp2
  56.0 0.4 collective-permute-done.7.xp3
  56.4 10.1 %all-gather.5.cloned.1.call-done = bf16[8192,256]{1,0:T(8,128)(2,1)} async-done(((bf16[512,256]{1,0:T(8,128)(2,1)}), bf16[8192,256]{1,0:T(8,128)(2,1)}) %all-gather.5.cloned.1.call-update) | async-done | bytes 4194320 | tf_op jit(solution)/shard_map/all_gather | solution.py:390
  66.5 1.3 slice.92
  67.8 0.8 collective-permute-start.9
  68.6 0.6 fusion.4
  70.4 0.6 stack.70.idx
  71.0 0.6 pad_maximum_fusion.6
  71.6 0.7 pad_maximum_fusion.4.dst_ref
  72.3 20.4 %mix.1 = (bf16[528,256]{1,0:T(8,128)(2,1)}, bf16[528,256]{1,0:T(8,128)(2,1)}, f32[3,128,128]{2,1,0:T(8,128)}, f32[3,128,128]{2,1,0:T(8,128)}) custom-call(s32[6]{0:T(128)} %stack.70.idx, bf16[2,528,256]{2,1,0:T(8,128)(2,1)} %bitcast.58, bf16[2,528,256]{2,1,0:T(8,128)(2,1)} %copy-done.4, bf16[1,528,256]{2,1,0:T(8,128)(2,1)} %copy-done.11, ...), custom_call_target="tpu_custom_call" | custom-call | flops 24 | bytes 24 | tf_op jit(solution)/shard_map/mix/pallas_call | solution.py:198
  92.7 0.1 collective-permute-start.8
  92.8 1.7 collective-permute-done.8.b_ref
  94.5 0.7 copy-done.15
  95.2 6.9 %outp.1 = (f32[2,528,256]{2,1,0:T(8,128)}, bf16[2,528,256]{2,1,0:T(8,128)(2,1)}, bf16[2,528,256]{2,1,0:T(8,128)(2,1)}, bf16[2,528,256]{2,1,0:T(8,128)(2,1)}) custom-call(s32[6]{0:T(128)} %stack.70.idx, bf16[528,256]{1,0:T(8,128)(2,1)} %get-tuple-element.24.a_ref, bf16[528,256]{1,0:T(8,128)(2,1)} %copy-done.15, bf16[16,512,256]{2,1,0:T(8,128)(2,1)} %bitcast.54, ...), custom_call_target="tpu_custom_call" | custom-call | flops 7 | bytes 7 | tf_op jit(solution)/shard_map/outp/pallas_call | solution.py:259
  102.1 1.3 collective-permute-start.10
  103.4 2.4 %collective-permute-start.11 = (bf16[2,528,256]{2,1,0:T(8,128)(2,1)}, bf16[2,528,256]{2,1,0:T(8,128)(2,1)S(1)}, u32[]{:S(2)}, u32[]{:S(2)}) collective-permute-start(bf16[2,528,256]{2,1,0:T(8,128)(2,1)} %get-tuple-element.28), channel_id=1, source_target_pairs={{0,4},{2,6},{4,0},{6,2},{1,5},{3,7},{5,1},{7,3},{8,12},{10,14},{12... | collective-permute-start | bytes 1622024 | tf_op jit(solution)/shard_map/ppermute | solution.py:24
  105.8 1.2 collective-permute-start.12
  107.0 1.1 collective-permute-start.13
  108.0 9.7 %collective-permute-done.13 = f32[3,128,128]{2,1,0:T(8,128)S(1)} collective-permute-done((f32[3,128,128]{2,1,0:T(8,128)S(1)}, f32[3,128,128]{2,1,0:T(8,128)S(1)}, u32[]{:S(2)}, u32[]{:S(2)}) %collective-permute-start.13) | collective-permute-done | bytes 196640 | tf_op jit(solution)/shard_map/ppermute | solution.py:24
  117.7 12.2 %collective-permute-done.11 = bf16[2,528,256]{2,1,0:T(8,128)(2,1)S(1)} collective-permute-done((bf16[2,528,256]{2,1,0:T(8,128)(2,1)}, bf16[2,528,256]{2,1,0:T(8,128)(2,1)S(1)}, u32[]{:S(2)}, u32[]{:S(2)}) %collective-permute-start.11) | collective-permute-done | bytes 540704 | tf_op jit(solution)/shard_map/ppermute | solution.py:24
  129.9 1.7 add_convert_fusion.1.x0
  131.6 1.1 collective-permute-start.15
  132.7 1.6 collective-permute-start.14
  134.3 11.4 %collective-permute-done.15.x4 = bf16[2,528,256]{2,1,0:T(8,128)(2,1)S(1)} collective-permute-done((bf16[2,528,256]{2,1,0:T(8,128)(2,1)S(1)}, bf16[2,528,256]{2,1,0:T(8,128)(2,1)S(1)}, u32[]{:S(2)}, u32[]{:S(2)}) %collective-permute-start.15) | collective-permute-done | bytes 540704 | tf_op jit(solution)/shard_map/ppermute | solution.py:24
  145.7 1.9 collective-permute-start.18
  147.7 0.7 collective-permute-start.16
  148.4 2.3 collective-permute-start.17
  150.7 6.4 %collective-permute-done.16.x2 = bf16[1,528,256]{2,1,0:T(8,128)(2,1)S(1)} collective-permute-done((bf16[1,528,256]{2,1,0:T(8,128)(2,1)S(1)}, bf16[1,528,256]{2,1,0:T(8,128)(2,1)S(1)}, u32[]{:S(2)}, u32[]{:S(2)}) %collective-permute-start.16) | collective-permute-done | bytes 270368 | tf_op jit(solution)/shard_map/ppermute | solution.py:24
  157.0 4.1 %collective-permute-done.18.h_ref = bf16[16,1056,256]{2,1,0:T(8,128)(2,1)} collective-permute-done((bf16[16,1056,256]{2,1,0:T(8,128)(2,1)}, bf16[16,1056,256]{2,1,0:T(8,128)(2,1)}, u32[]{:S(2)}, u32[]{:S(2)}) %collective-permute-start.18) | collective-permute-done | bytes 8650784 | tf_op jit(solution)/shard_map/ppermute | solution.py:24
  161.2 20.2 %mlp.1 = (f32[2,528,256]{2,1,0:T(8,128)}, bf16[2,528,256]{2,1,0:T(8,128)(2,1)}, bf16[2,528,256]{2,1,0:T(8,128)(2,1)}, bf16[2,528,256]{2,1,0:T(8,128)(2,1)}) custom-call(s32[6]{0:T(128)} %stack.70.idx, bf16[2,528,256]{2,1,0:T(8,128)(2,1)} %copy-done.2, bf16[2,528,256]{2,1,0:T(8,128)(2,1)} %copy-done.7, bf16[1,528,256]{2,1,0:T(8,128)(2,1)} %copy-done.16, ...), custom_call_target="tpu_custom_call" | custom-call | flops 20 | bytes 20 | tf_op jit(solution)/shard_map/mlp/pallas_call | solution.py:327
  181.4 0.7 collective-permute-start.19
  182.1 3.1 %collective-permute-start.20 = (bf16[2,528,256]{2,1,0:T(8,128)(2,1)}, bf16[2,528,256]{2,1,0:T(8,128)(2,1)S(1)}, u32[]{:S(2)}, u32[]{:S(2)}) collective-permute-start(bf16[2,528,256]{2,1,0:T(8,128)(2,1)} %get-tuple-element.36), channel_id=1, source_target_pairs={{0,4},{2,6},{4,0},{6,2},{1,5},{3,7},{5,1},{7,3},{8,12},{10,14},{12... | collective-permute-start | bytes 1622024 | tf_op jit(solution)/shard_map/ppermute | solution.py:24
  185.2 0.8 collective-permute-start.21
  186.0 10.3 %collective-permute-done.19 = bf16[2,528,256]{2,1,0:T(8,128)(2,1)S(1)} collective-permute-done((bf16[2,528,256]{2,1,0:T(8,128)(2,1)}, bf16[2,528,256]{2,1,0:T(8,128)(2,1)S(1)}, u32[]{:S(2)}, u32[]{:S(2)}) %collective-permute-start.19) | collective-permute-done | bytes 540704 | tf_op jit(solution)/shard_map/ppermute | solution.py:24
  196.4 12.7 %collective-permute-done.20 = bf16[2,528,256]{2,1,0:T(8,128)(2,1)S(1)} collective-permute-done((bf16[2,528,256]{2,1,0:T(8,128)(2,1)}, bf16[2,528,256]{2,1,0:T(8,128)(2,1)S(1)}, u32[]{:S(2)}, u32[]{:S(2)}) %collective-permute-start.20) | collective-permute-done | bytes 540704 | tf_op jit(solution)/shard_map/ppermute | solution.py:24
  209.0 1.8 add_convert_fusion
  210.8 0.1 fusion.2
  210.9 0.9 pad_maximum_fusion.2
  211.8 4.6 %all-to-all-start.1 = ((bf16[4,528,128]{2,1,0:T(8,128)(2,1)}), bf16[4,528,128]{2,1,0:T(8,128)(2,1)S(1)}, u32[]{:S(2)}, u32[]{:S(2)}) async-start(bf16[4,528,128]{2,1,0:T(8,128)(2,1)} %bitcast.26), calls=%async_computation.1 | async-start | bytes 1081344 | tf_op jit(solution)/shard_map/all_to_all | solution.py:424
  216.4 0.7 fusion.1
  217.1 0.7 fusion
  217.8 6.7 %all-to-all-done.1 = bf16[4,528,128]{2,1,0:T(8,128)(2,1)S(1)} async-done(((bf16[4,528,128]{2,1,0:T(8,128)(2,1)}), bf16[4,528,128]{2,1,0:T(8,128)(2,1)S(1)}, u32[]{:S(2)}, u32[]{:S(2)}) %all-to-all-start.1) | async-done | bytes 540704 | tf_op jit(solution)/shard_map/all_to_all | solution.py:424
  224.6 0.6 copy.41
  225.1 0.8 slice.97
  (81 shorter events, 0.5 us)
Async XLA Ops:
  7.2 2.9 %copy-start.23 = (bf16[4,128]{1,0:T(4,128)(2,1)S(1)}, bf16[4,128]{1,0:T(4,128)(2,1)}, u32[]{:S(2)}) copy-start(bf16[4,128]{1,0:T(4,128)(2,1)} %param.13) | copy-start | bytes 3076
  7.2 3.0 %copy-start.9 = (bf16[2,1024,128]{2,1,0:T(8,128)(2,1)S(1)}, bf16[2,1024,128]{2,1,0:T(8,128)(2,1)}, u32[]{:S(2)}) copy-start(bf16[2,1024,128]{2,1,0:T(8,128)(2,1)} %param.12) | copy-start | bytes 1572868
  7.2 59.3 %all-gather.5.cloned.1.call-start = ((), (), s32[]{:S(2)}) async-start(), calls=%async_computation.2 | async-start | bytes 4456448 | tf_op jit(solution)/shard_map/all_gather | solution.py:390
  10.2 5.9 %copy-start.18 = (f32[4,1,128,128]{3,2,1,0:T(8,128)S(1)}, f32[4,1,128,128]{3,2,1,0:T(8,128)}, u32[]{:S(2)}) copy-start(f32[4,1,128,128]{3,2,1,0:T(8,128)} %param.15) | copy-start | bytes 786436
  10.2 5.9 %copy-start.20 = (f32[128]{0:T(128)S(1)}, f32[128]{0:T(128)}, u32[]{:S(2)}) copy-start(f32[128]{0:T(128)} %param.18) | copy-start | bytes 1540
  10.2 5.9 %copy-start.21 = (f32[128]{0:T(128)S(1)}, f32[128]{0:T(128)}, u32[]{:S(2)}) copy-start(f32[128]{0:T(128)} %param.17) | copy-start | bytes 1540
  11.2 13.0 %all-to-all-start = ((bf16[4,528,128]{2,1,0:T(8,128)(2,1)}), bf16[4,528,128]{2,1,0:T(8,128)(2,1)S(1)}, u32[]{:S(2)}, u32[]{:S(2)}) async-start(bf16[4,528,128]{2,1,0:T(8,128)(2,1)} %maximum_maximum_fusion), calls=%async_computation | async-start | bytes 1081344 | tf_op jit(solution)/shard_map/all_to_all | solution.py:380
  16.0 129.6 %all-gather.7.cloned.1.call-start = ((), (), s32[]{:S(2)}) async-start(), calls=%async_computation.3 | async-start | bytes 9191424 | tf_op jit(solution)/shard_map/all_gather | solution.py:403
  16.1 11.0 %collective-permute-start = (f32[258,128]{1,0:T(8,128)S(1)}, f32[258,128]{1,0:T(8,128)S(1)}, u32[]{:S(2)}, u32[]{:S(2)}) collective-permute-start(f32[258,128]{1,0:T(8,128)S(1)} %pad_maximum_fusion.5), channel_id=1, source_target_pairs={{0,8},{8,0},{1,9},{9,1},{2,10},{10,2},{3,11},{11,3},{4,12},{12,4},... | collective-permute-start | bytes 396296 | tf_op jit(solution)/shard_map/ppermute | solution.py:24
  24.3 17.7 %copy-start = (bf16[2,2,66,8,128]{4,3,1,2,0:T(8,128)(2,1)}, bf16[2,2,66,8,128]{4,3,1,2,0:T(8,128)(2,1)S(1)}, u32[]{:S(2)}) copy-start(bf16[2,2,66,8,128]{4,3,1,2,0:T(8,128)(2,1)S(1)} %copy.40) | copy-start | bytes 1622020
  27.1 13.4 %collective-permute-start.2 = (bf16[2,528,256]{2,1,0:T(8,128)(2,1)S(1)}, bf16[2,528,256]{2,1,0:T(8,128)(2,1)S(1)}, u32[]{:S(2)}, u32[]{:S(2)}) collective-permute-start(bf16[2,528,256]{2,1,0:T(8,128)(2,1)S(1)} %bitcast.55), channel_id=1, source_target_pairs={{0,2},{2,4},{4,6},{6,0},{1,3},{3,5},{5,7},{7,1},{8,10},{10,12},{12... | collective-permute-start | bytes 1622024 | tf_op jit(solution)/shard_map/ppermute | solution.py:24
  28.4 12.1 %collective-permute-start.1 = (bf16[2,528,256]{2,1,0:T(8,128)(2,1)S(1)}, bf16[2,528,256]{2,1,0:T(8,128)(2,1)S(1)}, u32[]{:S(2)}, u32[]{:S(2)}) collective-permute-start(bf16[2,528,256]{2,1,0:T(8,128)(2,1)S(1)} %bitcast.56), channel_id=1, source_target_pairs={{0,6},{2,0},{4,2},{6,4},{1,7},{3,1},{5,3},{7,5},{8,14},{10,8},{12,... | collective-permute-start | bytes 1622024 | tf_op jit(solution)/shard_map/ppermute | solution.py:24
  40.5 4.1 %copy-start.3 = (bf16[2,528,256]{2,1,0:T(8,128)(2,1)}, bf16[2,528,256]{2,1,0:T(8,128)(2,1)S(1)}, u32[]{:S(2)}) copy-start(bf16[2,528,256]{2,1,0:T(8,128)(2,1)S(1)} %collective-permute-done.2.xo4) | copy-start | bytes 1622020
  40.5 5.3 %copy-start.4 = (bf16[2,528,256]{2,1,0:T(8,128)(2,1)}, bf16[2,528,256]{2,1,0:T(8,128)(2,1)S(1)}, u32[]{:S(2)}) copy-start(bf16[2,528,256]{2,1,0:T(8,128)(2,1)S(1)} %collective-permute-done.1.xo1) | copy-start | bytes 1622020
  42.0 12.9 %copy-start.8 = (f32[256,704]{0,1:T(8,128)S(1)}, f32[256,704]{0,1:T(8,128)}, u32[]{:S(2)}) copy-start(f32[256,704]{0,1:T(8,128)} %param.21) | copy-start | bytes 2162692
  42.0 12.9 %copy-start.10 = (f32[352,256]{1,0:T(8,128)S(1)}, f32[352,256]{1,0:T(8,128)}, u32[]{:S(2)}) copy-start(f32[352,256]{1,0:T(8,128)} %param.22) | copy-start | bytes 1081348
  42.0 14.4 %collective-permute-start.5 = (bf16[3,2,528,256]{3,2,1,0:T(8,128)(2,1)}, bf16[3,2,528,256]{3,2,1,0:T(8,128)(2,1)S(1)}, u32[]{:S(2)}, u32[]{:S(2)}) collective-permute-start(bf16[3,2,528,256]{3,2,1,0:T(8,128)(2,1)} %pad_maximum_fusion), channel_id=1, source_target_pairs={{0,1},{1,0},{2,3},{3,2},{4,5},{5,4},{6,7},{7,6},{8,9},{9,8},{10,11... | collective-permute-start | bytes 4866056 | tf_op jit(solution)/shard_map/ppermute | solution.py:24
  44.6 9.5 %collective-permute-start.3 = (bf16[1,528,256]{2,1,0:T(8,128)(2,1)S(1)}, bf16[1,528,256]{2,1,0:T(8,128)(2,1)S(1)}, u32[]{:S(2)}, u32[]{:S(2)}) collective-permute-start(bf16[1,528,256]{2,1,0:T(8,128)(2,1)S(1)} %slice.90), channel_id=1, source_target_pairs={{0,2},{2,4},{4,6},{6,0},{1,3},{3,5},{5,7},{7,1},{8,10},{10,12},{12... | collective-permute-start | bytes 811016 | tf_op jit(solution)/shard_map/ppermute | solution.py:24
  45.8 9.0 %collective-permute-start.4 = (bf16[1,528,256]{2,1,0:T(8,128)(2,1)S(1)}, bf16[1,528,256]{2,1,0:T(8,128)(2,1)S(1)}, u32[]{:S(2)}, u32[]{:S(2)}) collective-permute-start(bf16[1,528,256]{2,1,0:T(8,128)(2,1)S(1)} %slice.91), channel_id=1, source_target_pairs={{0,6},{2,0},{4,2},{6,4},{1,7},{3,1},{5,3},{7,5},{8,14},{10,8},{12,... | collective-permute-start | bytes 811016 | tf_op jit(solution)/shard_map/ppermute | solution.py:24
  54.1 1.7 copy-start.11
  54.1 1.9 collective-permute-start.6
  54.8 1.0 copy-start.12
  54.8 1.6 collective-permute-start.7
  56.0 10.5 %copy-start.13 = (bf16[1,528,256]{2,1,0:T(8,128)(2,1)}, bf16[1,528,256]{2,1,0:T(8,128)(2,1)S(1)}, u32[]{:S(2)}) copy-start(bf16[1,528,256]{2,1,0:T(8,128)(2,1)S(1)} %collective-permute-done.6.xp2) | copy-start | bytes 811012
  56.4 10.1 %copy-start.14 = (bf16[1,528,256]{2,1,0:T(8,128)(2,1)}, bf16[1,528,256]{2,1,0:T(8,128)(2,1)S(1)}, u32[]{:S(2)}) copy-start(bf16[1,528,256]{2,1,0:T(8,128)(2,1)S(1)} %collective-permute-done.7.xp3) | copy-start | bytes 811012
  56.4 11.5 %copy-start.5 = (bf16[3,2,528,256]{3,2,1,0:T(8,128)(2,1)}, bf16[3,2,528,256]{3,2,1,0:T(8,128)(2,1)S(1)}, u32[]{:S(2)}) copy-start(bf16[3,2,528,256]{3,2,1,0:T(8,128)(2,1)S(1)} %collective-permute-done.5.xpm) | copy-start | bytes 4866052
  66.5 2.1 copy-start.22
  67.8 26.7 %collective-permute-start.9 = (bf16[16,128,256]{2,1,0:T(8,128)(2,1)S(1)}, bf16[16,128,256]{2,1,0:T(8,128)(2,1)}, u32[]{:S(2)}, u32[]{:S(2)}) collective-permute-start(bf16[16,128,256]{2,1,0:T(8,128)(2,1)S(1)} %slice.92), channel_id=1, source_target_pairs={{0,1},{1,0},{2,3},{3,2},{4,5},{5,4},{6,7},{7,6},{8,9},{9,8},{10,11... | collective-permute-start | bytes 3145736 | tf_op jit(solution)/shard_map/ppermute | solution.py:24
  92.7 1.8 collective-permute-start.8
  94.5 0.7 copy-start.15
  95.2 11.8 %copy-start.24 = (f32[3,128,128]{2,1,0:T(8,128)S(1)}, f32[3,128,128]{2,1,0:T(8,128)}, u32[]{:S(2)}) copy-start(f32[3,128,128]{2,1,0:T(8,128)} %get-tuple-element.30) | copy-start | bytes 589828
  95.2 34.7 %copy-start.1 = (bf16[2,2,66,8,128]{4,3,1,2,0:T(8,128)(2,1)S(1)}, bf16[2,2,66,8,128]{4,3,1,2,0:T(8,128)(2,1)}, u32[]{:S(2)}) copy-start(bf16[2,2,66,8,128]{4,3,1,2,0:T(8,128)(2,1)} %copy-done) | copy-start | bytes 1622020
  102.1 15.6 %collective-permute-start.10 = (bf16[2,528,256]{2,1,0:T(8,128)(2,1)}, bf16[2,528,256]{2,1,0:T(8,128)(2,1)S(1)}, u32[]{:S(2)}, u32[]{:S(2)}) collective-permute-start(bf16[2,528,256]{2,1,0:T(8,128)(2,1)} %get-tuple-element.27), channel_id=1, source_target_pairs={{0,2},{2,4},{4,6},{6,0},{1,3},{3,5},{5,7},{7,1},{8,10},{10,12},{12... | collective-permute-start | bytes 1622024 | tf_op jit(solution)/shard_map/ppermute | solution.py:24
  103.4 26.5 %collective-permute-start.11 = (bf16[2,528,256]{2,1,0:T(8,128)(2,1)}, bf16[2,528,256]{2,1,0:T(8,128)(2,1)S(1)}, u32[]{:S(2)}, u32[]{:S(2)}) collective-permute-start(bf16[2,528,256]{2,1,0:T(8,128)(2,1)} %get-tuple-element.28), channel_id=1, source_target_pairs={{0,4},{2,6},{4,0},{6,2},{1,5},{3,7},{5,1},{7,3},{8,12},{10,14},{12... | collective-permute-start | bytes 1622024 | tf_op jit(solution)/shard_map/ppermute | solution.py:24
  105.8 24.1 %collective-permute-start.12 = (bf16[2,528,256]{2,1,0:T(8,128)(2,1)}, bf16[2,528,256]{2,1,0:T(8,128)(2,1)S(1)}, u32[]{:S(2)}, u32[]{:S(2)}) collective-permute-start(bf16[2,528,256]{2,1,0:T(8,128)(2,1)} %get-tuple-element.29), channel_id=1, source_target_pairs={{0,6},{2,0},{4,2},{6,4},{1,7},{3,1},{5,3},{7,5},{8,14},{10,8},{12,... | collective-permute-start | bytes 1622024 | tf_op jit(solution)/shard_map/ppermute | solution.py:24
  107.0 10.7 %collective-permute-start.13 = (f32[3,128,128]{2,1,0:T(8,128)S(1)}, f32[3,128,128]{2,1,0:T(8,128)S(1)}, u32[]{:S(2)}, u32[]{:S(2)}) collective-permute-start(f32[3,128,128]{2,1,0:T(8,128)S(1)} %copy-done.24), channel_id=1, source_target_pairs={{0,8},{8,0},{1,9},{9,1},{2,10},{10,2},{3,11},{11,3},{4,12},{12,4},... | collective-permute-start | bytes 589832 | tf_op jit(solution)/shard_map/ppermute | solution.py:24
  131.5 29.6 %copy-start.2 = (bf16[2,528,256]{2,1,0:T(8,128)(2,1)}, bf16[2,528,256]{2,1,0:T(8,128)(2,1)S(1)}, u32[]{:S(2)}) copy-start(bf16[2,528,256]{2,1,0:T(8,128)(2,1)S(1)} %add_convert_fusion.1.x0) | copy-start | bytes 1622020
  131.6 14.1 %collective-permute-start.15 = (bf16[2,528,256]{2,1,0:T(8,128)(2,1)S(1)}, bf16[2,528,256]{2,1,0:T(8,128)(2,1)S(1)}, u32[]{:S(2)}, u32[]{:S(2)}) collective-permute-start(bf16[2,528,256]{2,1,0:T(8,128)(2,1)S(1)} %add_convert_fusion.1.x0), channel_id=1, source_target_pairs={{0,2},{2,4},{4,6},{6,0},{1,3},{3,5},{5,7},{7,1},{8,10},{10,12},{12... | collective-permute-start | bytes 1622024 | tf_op jit(solution)/shard_map/ppermute | solution.py:24
  132.7 13.0 %collective-permute-start.14 = (bf16[2,528,256]{2,1,0:T(8,128)(2,1)S(1)}, bf16[2,528,256]{2,1,0:T(8,128)(2,1)S(1)}, u32[]{:S(2)}, u32[]{:S(2)}) collective-permute-start(bf16[2,528,256]{2,1,0:T(8,128)(2,1)S(1)} %add_convert_fusion.1.x0), channel_id=1, source_target_pairs={{0,6},{2,0},{4,2},{6,4},{1,7},{3,1},{5,3},{7,5},{8,14},{10,8},{12,... | collective-permute-start | bytes 1622024 | tf_op jit(solution)/shard_map/ppermute | solution.py:24
  145.7 15.5 %copy-start.6 = (bf16[2,528,256]{2,1,0:T(8,128)(2,1)}, bf16[2,528,256]{2,1,0:T(8,128)(2,1)S(1)}, u32[]{:S(2)}) copy-start(bf16[2,528,256]{2,1,0:T(8,128)(2,1)S(1)} %collective-permute-done.15.x4) | copy-start | bytes 1622020
  145.7 15.5 %copy-start.7 = (bf16[2,528,256]{2,1,0:T(8,128)(2,1)}, bf16[2,528,256]{2,1,0:T(8,128)(2,1)S(1)}, u32[]{:S(2)}) copy-start(bf16[2,528,256]{2,1,0:T(8,128)(2,1)S(1)} %collective-permute-done.14.x1) | copy-start | bytes 1622020
  145.7 15.4 %collective-permute-start.18 = (bf16[16,1056,256]{2,1,0:T(8,128)(2,1)}, bf16[16,1056,256]{2,1,0:T(8,128)(2,1)}, u32[]{:S(2)}, u32[]{:S(2)}) collective-permute-start(bf16[16,1056,256]{2,1,0:T(8,128)(2,1)} %bitcast.60), channel_id=1, source_target_pairs={{0,1},{1,0},{2,3},{3,2},{4,5},{5,4},{6,7},{7,6},{8,9},{9,8},{10,11... | collective-permute-start | bytes 25952264 | tf_op jit(solution)/shard_map/ppermute | solution.py:24
  147.7 9.4 %collective-permute-start.16 = (bf16[1,528,256]{2,1,0:T(8,128)(2,1)S(1)}, bf16[1,528,256]{2,1,0:T(8,128)(2,1)S(1)}, u32[]{:S(2)}, u32[]{:S(2)}) collective-permute-start(bf16[1,528,256]{2,1,0:T(8,128)(2,1)S(1)} %slice.93), channel_id=1, source_target_pairs={{0,2},{2,4},{4,6},{6,0},{1,3},{3,5},{5,7},{7,1},{8,10},{10,12},{12... | collective-permute-start | bytes 811016 | tf_op jit(solution)/shard_map/ppermute | solution.py:24
  148.4 8.6 %collective-permute-start.17 = (bf16[1,528,256]{2,1,0:T(8,128)(2,1)S(1)}, bf16[1,528,256]{2,1,0:T(8,128)(2,1)S(1)}, u32[]{:S(2)}, u32[]{:S(2)}) collective-permute-start(bf16[1,528,256]{2,1,0:T(8,128)(2,1)S(1)} %slice.94), channel_id=1, source_target_pairs={{0,6},{2,0},{4,2},{6,4},{1,7},{3,1},{5,3},{7,5},{8,14},{10,8},{12,... | collective-permute-start | bytes 811016 | tf_op jit(solution)/shard_map/ppermute | solution.py:24
  157.0 4.1 %copy-start.16 = (bf16[1,528,256]{2,1,0:T(8,128)(2,1)}, bf16[1,528,256]{2,1,0:T(8,128)(2,1)S(1)}, u32[]{:S(2)}) copy-start(bf16[1,528,256]{2,1,0:T(8,128)(2,1)S(1)} %collective-permute-done.16.x2) | copy-start | bytes 811012
  157.0 4.1 %copy-start.17 = (bf16[1,528,256]{2,1,0:T(8,128)(2,1)}, bf16[1,528,256]{2,1,0:T(8,128)(2,1)S(1)}, u32[]{:S(2)}) copy-start(bf16[1,528,256]{2,1,0:T(8,128)(2,1)S(1)} %collective-permute-done.17.x3) | copy-start | bytes 811012
  161.2 24.8 %copy-start.19 = (f32[3,128,128]{2,1,0:T(8,128)S(1)}, f32[3,128,128]{2,1,0:T(8,128)}, u32[]{:S(2)}) copy-start(f32[3,128,128]{2,1,0:T(8,128)} %get-tuple-element.39) | copy-start | bytes 589828
  181.4 15.0 %collective-permute-start.19 = (bf16[2,528,256]{2,1,0:T(8,128)(2,1)}, bf16[2,528,256]{2,1,0:T(8,128)(2,1)S(1)}, u32[]{:S(2)}, u32[]{:S(2)}) collective-permute-start(bf16[2,528,256]{2,1,0:T(8,128)(2,1)} %get-tuple-element.35), channel_id=1, source_target_pairs={{0,2},{2,4},{4,6},{6,0},{1,3},{3,5},{5,7},{7,1},{8,10},{10,12},{12... | collective-permute-start | bytes 1622024 | tf_op jit(solution)/shard_map/ppermute | solution.py:24
  182.1 26.9 %collective-permute-start.20 = (bf16[2,528,256]{2,1,0:T(8,128)(2,1)}, bf16[2,528,256]{2,1,0:T(8,128)(2,1)S(1)}, u32[]{:S(2)}, u32[]{:S(2)}) collective-permute-start(bf16[2,528,256]{2,1,0:T(8,128)(2,1)} %get-tuple-element.36), channel_id=1, source_target_pairs={{0,4},{2,6},{4,0},{6,2},{1,5},{3,7},{5,1},{7,3},{8,12},{10,14},{12... | collective-permute-start | bytes 1622024 | tf_op jit(solution)/shard_map/ppermute | solution.py:24
  185.2 23.8 %collective-permute-start.21 = (bf16[2,528,256]{2,1,0:T(8,128)(2,1)}, bf16[2,528,256]{2,1,0:T(8,128)(2,1)S(1)}, u32[]{:S(2)}, u32[]{:S(2)}) collective-permute-start(bf16[2,528,256]{2,1,0:T(8,128)(2,1)} %get-tuple-element.37), channel_id=1, source_target_pairs={{0,6},{2,0},{4,2},{6,4},{1,7},{3,1},{5,3},{7,5},{8,14},{10,8},{12,... | collective-permute-start | bytes 1622024 | tf_op jit(solution)/shard_map/ppermute | solution.py:24
  211.8 12.8 %all-to-all-start.1 = ((bf16[4,528,128]{2,1,0:T(8,128)(2,1)}), bf16[4,528,128]{2,1,0:T(8,128)(2,1)S(1)}, u32[]{:S(2)}, u32[]{:S(2)}) async-start(bf16[4,528,128]{2,1,0:T(8,128)(2,1)} %bitcast.26), calls=%async_computation.1 | async-start | bytes 1081344 | tf_op jit(solution)/shard_map/all_to_all | solution.py:424
Sparse Core Ops, SparseCore 0:
  10.7 55.6 all-gather.4
  68.7 74.4 all-gather.6

commit v3 on v2

--- a/solution.py
+++ b/solution.py
@@ -152,7 +152,7 @@
             oscr[h, rows, j * 128 : (j + 1) * 128] = head_out(o, gain_ref[j : j + 1, :]).astype(BF)
         return unused
 
-    lax.fori_loop(0, 8, chunk, 0)
+    lax.fori_loop(0, 8, chunk, 0, unroll=2)
     first = lax.broadcasted_iota(jnp.int32, (16, 128), 0) == 0
     for h in range(2):
         for j in range(2):
@@ -219,82 +219,89 @@
     )(idx, *xo, *xp, w, bias, gain, mat, dst)
 
 
-def spread(out_s, x, p0, p1, p2, p3):
-    for z in range(2):
-        p0[z] = out_s[z * 4 + x]
-        for k, ref in ((1, p1), (2, p2), (3, p3)):
-            ref[z] = out_s[z * 4 + ((x + k) & 3)].astype(BF)
-
-
-PARTS = (
-    jax.ShapeDtypeStruct((2, HALF, 256), F32),
-    jax.ShapeDtypeStruct((2, HALF, 256), BF),
-    jax.ShapeDtypeStruct((2, HALF, 256), BF),
-    jax.ShapeDtypeStruct((2, HALF, 256), BF),
-)
-
-
-def out_kernel(
-    idx, a_ref, b_ref, u_ref, v_ref,
-    p0, p1, p2, p3, ocat, wcat, out_s, sems,
-):
+PART = jax.ShapeDtypeStruct((2, HALF, 256), F32)
+FAR = jax.ShapeDtypeStruct((1, HALF, 256), BF)
+
+
+def shapes_of(steps):
+    return (FAR, FAR) if steps == (2,) else (PART,) * len(steps)
+
+
+def put(steps, outs, s, z, value):
+    if steps == (2,):
+        outs[z][0] = value.astype(BF)
+    else:
+        outs[s][z] = value
+
+
+def blocks_of(steps, x):
+    for s, k in enumerate(steps):
+        for z in range(2):
+            yield s * 2 + z, s, z, z * 4 + ((x + k) & 3)
+
+
+def out_kernel(steps, idx, a_ref, b_ref, u_ref, v_ref, *rest):
+    outs, (ocat, wcat, sems) = rest[:-3], rest[-3:]
     copies = [(a_ref, ocat.at[:, 0:256]), (b_ref, ocat.at[:, 256:512])]
-    for i in range(16):
-        for cc in range(2):
-            src = v_ref.at[i] if cc else u_ref.at[i, 384:512]
-            at = pl.multiple_of(cc * 256 + ((i & 1) ^ idx[2]) * 128, 128)
-            copies.append((src, wcat.at[i // 2, pl.ds(at, 128), :]))
+    for slot, s, z, r in blocks_of(steps, idx[3]):
+        for j in range(2):
+            for cc in range(2):
+                src = v_ref.at[2 * r + j] if cc else u_ref.at[2 * r + j, 384:512]
+                at = pl.multiple_of(cc * 256 + (j ^ idx[2]) * 128, 128)
+                copies.append((src, wcat.at[slot, pl.ds(at, 128), :]))
     for cp in copy_all(copies, sems):
         cp.wait()
-
-    def block(r, unused):
-        out_s[r] = dot_nn(ocat[...], wcat[r])
-        return unused
-
-    lax.fori_loop(0, 8, block, 0)
-    spread(out_s, idx[3], p0, p1, p2, p3)
-
-
-def out_call(idx, a, b, u, v):
+    for slot, s, z, r in blocks_of(steps, idx[3]):
+        put(steps, outs, s, z, dot_nn(ocat[...], wcat[slot]))
+
+
+def out_call(steps, idx, a, b, u, v):
+    n = len(steps)
     return pl.pallas_call(
-        out_kernel,
-        out_shape=PARTS,
+        functools.partial(out_kernel, steps),
+        out_shape=shapes_of(steps),
         in_specs=[sspec()] + [anyspec()] * 4,
-        out_specs=(vspec(),) * 4,
+        out_specs=(vspec(),) * len(shapes_of(steps)),
         scratch_shapes=[
             pltpu.VMEM((HALF, 512), BF),
-            pltpu.VMEM((8, 512, 256), BF),
-            pltpu.VMEM((8, HALF, 256), F32),
-            pltpu.SemaphoreType.DMA((34,)),
+            pltpu.VMEM((2 * n, 512, 256), BF),
+            pltpu.SemaphoreType.DMA((2 + 8 * n,)),
         ],
         compiler_params=pltpu.CompilerParams(vmem_limit_bytes=VMEM_LIMIT),
-        cost_estimate=cost(7),
+        cost_estimate=cost(2 * n),
         name="outp",
     )(idx, a, b, u, v)
 
 
-def mlp_kernel(
-    idx, x0, x1, x2, x3, x4, g_ref, h_ref, gain_ref,
-    p0, p1, p2, p3, xcat, wg, wd, hid, out_s, sems,
-):
+def down_copies(steps, x, refs, wd):
+    out = []
+    for slot, s, z, r in blocks_of(steps, x):
+        for j in range(2):
+            for cc, ref in enumerate(refs):
+                at = cc * 704 + j * 352
+                out.append((ref.at[2 * r + j, 704:1056], wd.at[slot, at : at + 352, :]))
+    return out
+
+
+def down_dots(steps, x, hid, wd, outs):
+    for slot, s, z, r in blocks_of(steps, x):
+        total = dot_nn(hid[0], wd[slot, 0:704, :]) + dot_nn(hid[1], wd[slot, 704:1408, :])
+        put(steps, outs, s, z, total)
+
+
+def mlp_kernel(idx, x0, x1, x2, x3, x4, g_ref, h_ref, gain_ref, hid, q0, q1, xcat, wg, wd, sems):
     x = idx[3]
-    first = copy_all(x_copies((x0, x1, x2, x3, x4), xcat, x), sems)
-    copies = []
+    started = [copy_all(x_copies((x0, x1, x2, x3, x4), xcat, x), sems)]
     for cc, ref in ((0, g_ref), (1, h_ref)):
+        copies = []
         for i in range(16):
-            at, r = cc * 704 + (i & 1) * 352, i // 2
             for g in range(2):
-                dst = wg.at[g, at : at + 352, r * 256 : (r + 1) * 256]
+                at, r = (i & 1) * 352, i // 2
+                dst = wg.at[cc, g, at : at + 352, r * 256 : (r + 1) * 256]
                 copies.append((ref.at[i, g * 352 : (g + 1) * 352], dst))
-    second = copy_all(copies, sems.at[8:72])
-    copies = []
-    for cc, ref in ((0, g_ref), (1, h_ref)):
-        for i in range(16):
-            at, r = cc * 704 + (i & 1) * 352, i // 2
-            dst = wd.at[at : at + 352, r * 256 : (r + 1) * 256]
-            copies.append((ref.at[i, 704:1056], dst))
-    third = copy_all(copies, sems.at[72:104])
-    for cp in first:
+        started.append(copy_all(copies, sems.at[8 + cc * 32 : 40 + cc * 32]))
+    last = copy_all(down_copies((2,), x, (g_ref, h_ref), wd), sems.at[72:80])
+    for cp in started[0]:
         cp.wait()
 
     def normalize(i, unused):
@@ -305,44 +312,58 @@
         return unused
 
     lax.fori_loop(0, 11, normalize, 0)
-    for cp in second:
+    for cc in range(2):
+        for cp in started[1 + cc]:
+            cp.wait()
+        gate = dot_nt(xcat[...], wg[cc, 0])
+        up = dot_nt(xcat[...], wg[cc, 1])
+        hid[cc] = (gate / (1.0 + jnp.exp(-gate)) * up).astype(BF)
+    for cp in last:
         cp.wait()
-
-    for lo, hi in ((0, 768), (768, 1408)):
-        gate = dot_nt(xcat[...], wg[0, lo:hi, :])
-        up = dot_nt(xcat[...], wg[1, lo:hi, :])
-        hid[:, lo:hi] = (gate / (1.0 + jnp.exp(-gate)) * up).astype(BF)
-    for cp in third:
-        cp.wait()
-
-    def block(r, unused):
-        out_s[r] = dot_nn(hid[...], wd[:, col(r)])
-        return unused
-
-    lax.fori_loop(0, 8, block, 0)
-    spread(out_s, x, p0, p1, p2, p3)
+    down_dots((2,), x, hid, wd, (q0, q1))
 
 
 def mlp_call(idx, xs, g, h, gain):
     return pl.pallas_call(
         mlp_kernel,
-        out_shape=PARTS,
+        out_shape=(jax.ShapeDtypeStruct((2, HALF, 704), BF), FAR, FAR),
         in_specs=[sspec()] + [anyspec()] * 7 + [vspec()],
-        out_specs=(vspec(),) * 4,
+        out_specs=(vspec(),) * 3,
         scratch_shapes=[
             pltpu.VMEM((HALF, 2048), BF),
-            pltpu.VMEM((2, 1408, 2048), BF),
-            pltpu.VMEM((1408, 2048), BF),
-            pltpu.VMEM((HALF, 1408), BF),
-            pltpu.VMEM((8, HALF, 256), F32),
-            pltpu.SemaphoreType.DMA((104,)),
+            pltpu.VMEM((2, 2, 704, 2048), BF),
+            pltpu.VMEM((2, 1408, 256), BF),
+            pltpu.SemaphoreType.DMA((80,)),
         ],
         compiler_params=pltpu.CompilerParams(vmem_limit_bytes=VMEM_LIMIT),
-        cost_estimate=cost(20),
+        cost_estimate=cost(16),
         name="mlp",
     )(idx, *xs, g, h, gain)
 
 
+def down_kernel(steps, idx, hid, g_ref, h_ref, p0, p1, p2, wd, sems):
+    for cp in copy_all(down_copies(steps, idx[3], (g_ref, h_ref), wd), sems):
+        cp.wait()
+    down_dots(steps, idx[3], hid, wd, (p0, p1, p2))
+
+
+def down_call(steps, idx, hid, g, h):
+    n = len(steps)
+    return pl.pallas_call(
+        functools.partial(down_kernel, steps),
+        out_shape=shapes_of(steps),
+        in_specs=[sspec(), vspec()] + [anyspec()] * 2,
+        out_specs=(vspec(),) * n,
+        scratch_shapes=[
+            pltpu.VMEM((2 * n, 1408, 256), BF),
+            pltpu.SemaphoreType.DMA((8 * n,)),
+        ],
+        compiler_params=pltpu.CompilerParams(vmem_limit_bytes=VMEM_LIMIT),
+        cost_estimate=cost(5),
+        name="down",
+    )(idx, hid, g, h)
+
+
 def swap(value, axis):
     return shift(value, axis, 1)
 
@@ -351,13 +372,17 @@
     return lax.optimization_barrier((value,) + others)[0]
 
 
-def reduce_parts(parts, *others):
-    p0, p1, p2, p3 = parts
-    r2 = shift(p2, "x", 2)
+def reduce_parts(far, rest, *others):
+    p1, p3, p0 = rest
+    a, b = shift(far[0], "x", 1), shift(far[1], "x", -1)
+    a, b = lax.optimization_barrier((a, b))
+    keep = (0, 0, 0)
+    p1 = (p1 + lax.pad(a.astype(F32), F32(0), ((0, 1, 0), keep, keep))).astype(BF)
+    p3 = (p3 + lax.pad(b.astype(F32), F32(0), ((1, 0, 0), keep, keep))).astype(BF)
     r1 = shift(p1, "x", 1)
     r3 = shift(p3, "x", -1)
-    r1 = after(r1, r2, r3, *others)
-    return p0 + r1.astype(F32) + r2.astype(F32) + r3.astype(F32)
+    r1 = after(r1, r3, *others)
+    return p0 + r1.astype(F32) + r3.astype(F32)
 
 
 def on_device(
@@ -388,12 +413,13 @@
     early = jnp.concatenate([w_fio.astype(BF).T, w_out.astype(BF)])
     early = with_layout_constraint(early, Layout((0, 1)))
     early = lax.all_gather(early, ("y", "zh", "zl")).reshape(16, 512, 256)
-    x_own, other = lax.optimization_barrier((x_own, other))
+    x_own, other, idx = lax.optimization_barrier((x_own, other, idx))
     bias = jnp.stack([small[0], other[256]])
     gain = jnp.stack([small[1], other[257]])
     dst = jnp.stack([ds_keep, other[:256]]).reshape(2, 2, 128, 128)
 
     x_before, x_ahead = shift(x_own, "x", 1), shift(x_own, "x", -1)
+    x_ahead, bias, gain, dst = lax.optimization_barrier((x_ahead, bias, gain, dst))
     x_mid = swap(jnp.stack([x_own, x_ahead, x_before]), "c")
     xs = [x_own, x_ahead, shift(x_before[:1], "x", 1), shift(x_ahead[1:], "x", -1), x_before]
     xp = [x_mid, swap(xs[2], "c"), swap(xs[3], "c")]
@@ -414,11 +440,14 @@
         zl == 0, jnp.stack([mine[2], other[2]]), jnp.stack([other[2], mine[2]])
     ).reshape(2, 1, 128, 128)
 
-    attention = reduce_parts(out_call(idx, ho, hr, early, wo2), other)
+    far = out_call((2,), idx, ho, hr, early, wo2)
+    rest = out_call((1, 3, 0), idx, after(ho, *far), hr, early, wo2)
+    attention = reduce_parts(far, rest, other)
     residual = (x_own.astype(F32) + attention).astype(BF)
     rs = ring_gather(residual, "x")
     late2 = swap(after(late, rs[1], rs[4]), "c")
-    down = reduce_parts(mlp_call(idx, rs, late, late2, mlp_gain.reshape(1, 2048)))
+    hid, *far = mlp_call(idx, rs, late, late2, mlp_gain.reshape(1, 2048))
+    down = reduce_parts(far, down_call((1, 3, 0), idx, hid, late, late2))
     layer = (residual.astype(F32) + down).astype(BF)
     layer = layer.reshape(2, HALF, 2, 128).transpose(0, 2, 1, 3).reshape(4, HALF, 128)
     back = lax.all_to_all(layer, ("zl", "c"), 0, 0, tiled=True)

time: 233 us -> 220 us (0.944)
  waiting for transfers between devices: 113 us -> 96.2 us
    ppermute x22 -> x24, waiting for transfers between devices: 89 us -> 68.2 us  [shift(): return lax.ppermute(value, axis, [(i, (i + step) % n) for i in range(n)])]
    all_gather x1, waiting for transfers between devices: 0.02 us -> 9.55 us  [on_device(): late = lax.all_gather(late, ('y', 'zh', 'zl')).reshape(16, 1056, 256)]
    convert_element_type x0 -> x4, other arithmetic: none -> 2.93 us  [the longest x2 2.77 us: reduce_parts(): (p1 + lax.pad(a.astype(F32), F32(0), ((0, 1, 0), keep, keep))).astype(BF)]
    all_gather x1, waiting for transfers between devices: 10.1 us -> 7.43 us  [on_device(): early = lax.all_gather(early, ('y', 'zh', 'zl')).reshape(16, 512, 256)]
    pallas_call x2 -> x4, Pallas kernels: 27.1 us -> 28.9 us  [the longest x1 13.6 us: mlp_call(): pl.pallas_call(mlp_kernel, out_shape=(jax.ShapeDtypeStruct((2, HALF, 704)...]
    ppermute x22 -> x24, starting transfers between devices: 29.4 us -> 30.2 us  [shift(): return lax.ppermute(value, axis, [(i, (i + step) % n) for i in range(n)])]
  transfers between devices with their start and end apart: 26 -> 28, of which waited for: 16 -> 18; matrix products, arithmetic and copies ran while one was open for 5% -> 5% of each run, Pallas kernels for 12% -> 16%
where the time goes in v3:
time: 220 us
  waiting for transfers between devices  96.2 us (44%)
  Pallas kernels  48 us (22%)
  starting transfers between devices  40.5 us (18%)
  between operations  15.6 us (7%)
  other arithmetic  12 us (5%)
  local copies, waits for them, and re-layouts  7.59 us (3%)
    ppermute x24, waiting for transfers between devices, shift(): return lax.ppermute(value, axis, [(i, (i + step) % n) for i in range(n)])  68.2 us
    ppermute x24, starting transfers between devices, shift(): return lax.ppermute(value, axis, [(i, (i + step) % n) for i in range(n)])  30.2 us
    pallas_call x1, Pallas kernels, mix_call(): pl.pallas_call(mix_kernel, out_shape=(jax.ShapeDtypeStruct((HALF, 256), B...  19.1 us
    pallas_call x1, Pallas kernels, mlp_call(): pl.pallas_call(mlp_kernel, out_shape=(jax.ShapeDtypeStruct((2, HALF, 704)...  13.6 us
    all_gather x1, waiting for transfers between devices, on_device(): late = lax.all_gather(late, ('y', 'zh', 'zl')).reshape(16, 1056, 256)  9.55 us
    pallas_call x2, Pallas kernels, out_call(): pl.pallas_call(functools.partial(out_kernel, steps), out_shape=shapes_of(...  7.64 us
    pallas_call x1, Pallas kernels, down_call(): pl.pallas_call(functools.partial(down_kernel, steps), out_shape=shapes_of...  7.61 us
    all_gather x1, waiting for transfers between devices, on_device(): early = lax.all_gather(early, ('y', 'zh', 'zl')).reshape(16, 512, 256)  7.43 us
  transfers between devices with their start and end apart: 28, of which 18 were waited for; matrix products, arithmetic and copies ran while one was open for 5% of the time, Pallas kernels for 16%

profile of v3, /device:TPU:1, one launch (start us, length us, event | category | flops | bytes accessed | tf_op | source)
XLA Modules:
  0.0 219.9 jit_solution(10350100628213483389)
XLA Ops:
  7.2 1.0 convert_element_type.54
  8.2 1.1 copy.33
  9.3 0.7 pad_maximum_fusion.4
  10.2 1.0 maximum_maximum_fusion
  11.2 5.0 %all-to-all-start = ((bf16[4,528,128]{2,1,0:T(8,128)(2,1)}), bf16[4,528,128]{2,1,0:T(8,128)(2,1)S(1)}, u32[]{:S(2)}, u32[]{:S(2)}) async-start(bf16[4,528,128]{2,1,0:T(8,128)(2,1)} %maximum_maximum_fusion), calls=%async_computation | async-start | bytes 1081344 | tf_op jit(solution)/shard_map/all_to_all | solution.py:405
  16.3 1.5 collective-permute-start
  17.7 0.6 fusion.4
  19.5 0.6 stack.70.idx
  20.1 4.3 %all-to-all-done = bf16[4,528,128]{2,1,0:T(8,128)(2,1)S(1)} async-done(((bf16[4,528,128]{2,1,0:T(8,128)(2,1)}), bf16[4,528,128]{2,1,0:T(8,128)(2,1)S(1)}, u32[]{:S(2)}, u32[]{:S(2)}) %all-to-all-start) | async-done | bytes 540704 | tf_op jit(solution)/shard_map/all_to_all | solution.py:405
  24.5 2.8 %collective-permute-done = f32[258,128]{1,0:T(8,128)S(1)} collective-permute-done((f32[258,128]{1,0:T(8,128)S(1)}, f32[258,128]{1,0:T(8,128)S(1)}, u32[]{:S(2)}, u32[]{:S(2)}) %collective-permute-start) | collective-permute-done | bytes 132128 | tf_op jit(solution)/shard_map/ppermute | solution.py:24
  27.3 2.7 %collective-permute-start.1 = (bf16[2,528,256]{2,1,0:T(8,128)(2,1)S(1)}, bf16[2,528,256]{2,1,0:T(8,128)(2,1)S(1)}, u32[]{:S(2)}, u32[]{:S(2)}) collective-permute-start(bf16[2,528,256]{2,1,0:T(8,128)(2,1)S(1)} %bitcast.59), channel_id=1, source_target_pairs={{0,6},{2,0},{4,2},{6,4},{1,7},{3,1},{5,3},{7,5},{8,14},{10,8},{12,... | collective-permute-start | bytes 1622024 | tf_op jit(solution)/shard_map/ppermute | solution.py:24
  30.0 0.6 pad_maximum_fusion.6
  30.6 0.8 pad_maximum_fusion.3.dst_ref
  31.4 8.4 %collective-permute-done.1.xo1 = bf16[2,528,256]{2,1,0:T(8,128)(2,1)S(1)} collective-permute-done((bf16[2,528,256]{2,1,0:T(8,128)(2,1)S(1)}, bf16[2,528,256]{2,1,0:T(8,128)(2,1)S(1)}, u32[]{:S(2)}, u32[]{:S(2)}) %collective-permute-start.1) | collective-permute-done | bytes 540704 | tf_op jit(solution)/shard_map/ppermute | solution.py:24
  39.8 3.1 %collective-permute-done.2.xo4 = bf16[2,528,256]{2,1,0:T(8,128)(2,1)S(1)} collective-permute-done((bf16[2,528,256]{2,1,0:T(8,128)(2,1)S(1)}, bf16[2,528,256]{2,1,0:T(8,128)(2,1)S(1)}, u32[]{:S(2)}, u32[]{:S(2)}) %collective-permute-start.2) | collective-permute-done | bytes 540704 | tf_op jit(solution)/shard_map/ppermute | solution.py:24
  42.9 1.4 pad_maximum_fusion
  44.3 3.0 %collective-permute-start.5 = (bf16[3,2,528,256]{3,2,1,0:T(8,128)(2,1)}, bf16[3,2,528,256]{3,2,1,0:T(8,128)(2,1)S(1)}, u32[]{:S(2)}, u32[]{:S(2)}) collective-permute-start(bf16[3,2,528,256]{3,2,1,0:T(8,128)(2,1)} %pad_maximum_fusion), channel_id=1, source_target_pairs={{0,1},{1,0},{2,3},{3,2},{4,5},{5,4},{6,7},{7,6},{8,9},{9,8},{10,11... | collective-permute-start | bytes 4866056 | tf_op jit(solution)/shard_map/ppermute | solution.py:24
  47.4 2.7 %collective-permute-start.4 = (bf16[1,528,256]{2,1,0:T(8,128)(2,1)S(1)}, bf16[1,528,256]{2,1,0:T(8,128)(2,1)S(1)}, u32[]{:S(2)}, u32[]{:S(2)}) collective-permute-start(bf16[1,528,256]{2,1,0:T(8,128)(2,1)S(1)} %slice.76), channel_id=1, source_target_pairs={{0,6},{2,0},{4,2},{6,4},{1,7},{3,1},{5,3},{7,5},{8,14},{10,8},{12,... | collective-permute-start | bytes 811016 | tf_op jit(solution)/shard_map/ppermute | solution.py:24
  50.1 6.6 %collective-permute-done.3.xo2 = bf16[1,528,256]{2,1,0:T(8,128)(2,1)S(1)} collective-permute-done((bf16[1,528,256]{2,1,0:T(8,128)(2,1)S(1)}, bf16[1,528,256]{2,1,0:T(8,128)(2,1)S(1)}, u32[]{:S(2)}, u32[]{:S(2)}) %collective-permute-start.3) | collective-permute-done | bytes 270368 | tf_op jit(solution)/shard_map/ppermute | solution.py:24
  56.8 0.7 collective-permute-start.6
  57.7 0.8 pad_maximum_fusion.1
  58.7 0.4 collective-permute-done.7.xp3
  59.1 7.4 %all-gather.5.cloned.1.call-done = bf16[8192,256]{1,0:T(8,128)(2,1)} async-done(((bf16[512,256]{1,0:T(8,128)(2,1)}), bf16[8192,256]{1,0:T(8,128)(2,1)}) %all-gather.5.cloned.1.call-update) | async-done | bytes 4194320 | tf_op jit(solution)/shard_map/all_gather | solution.py:415
  66.5 2.3 %slice.91 = bf16[16,128,256]{2,1,0:T(8,128)(2,1)} slice(bf16[16,512,256]{2,1,0:T(8,128)(2,1)} %bitcast.52), slice={[0:16], [384:512], [0:256]} | slice | bytes 2097152 | tf_op jit(solution)/shard_map/slice | solution.py:426
  68.8 0.8 collective-permute-start.9
  69.6 19.1 %mix.1 = (bf16[528,256]{1,0:T(8,128)(2,1)}, bf16[528,256]{1,0:T(8,128)(2,1)}, f32[3,128,128]{2,1,0:T(8,128)}, f32[3,128,128]{2,1,0:T(8,128)}) custom-call(s32[6]{0:T(128)} %stack.70.idx, bf16[2,528,256]{2,1,0:T(8,128)(2,1)} %bitcast.62, bf16[2,528,256]{2,1,0:T(8,128)(2,1)} %copy-done.5, bf16[1,528,256]{2,1,0:T(8,128)(2,1)} %copy-done.18, ...), custom_call_target="tpu_custom_call" | custom-call | flops 24 | bytes 24 | tf_op jit(solution)/shard_map/mix/pallas_call | solution.py:198
  88.8 1.7 collective-permute-done.8.b_ref
  90.5 0.7 copy-done.10
  91.2 0.4 copy-done.4
  91.6 3.1 %outp.2 = (bf16[1,528,256]{2,1,0:T(8,128)(2,1)}, bf16[1,528,256]{2,1,0:T(8,128)(2,1)}) custom-call(s32[6]{0:T(128)} %stack.70.idx, bf16[528,256]{1,0:T(8,128)(2,1)} %get-tuple-element.46.a_ref, bf16[528,256]{1,0:T(8,128)(2,1)} %copy-done.10, bf16[16,512,256]{2,1,0:T(8,128)(2,1)} %bitcast.54, bf16[16,128,256]{2,1,0:T(8,128)(2,1)} %copy-done.4), custom_call_target="tpu_custom_call" | custom-call | flops 2 | bytes 2 | tf_op jit(solution)/shard_map/outp/pallas_call | solution.py:260
  94.7 1.2 collective-permute-start.10
  96.0 1.5 collective-permute-start.11
  97.5 4.5 %outp.3 = (f32[2,528,256]{2,1,0:T(8,128)}, f32[2,528,256]{2,1,0:T(8,128)}, f32[2,528,256]{2,1,0:T(8,128)}) custom-call(s32[6]{0:T(128)} %stack.70.idx, bf16[528,256]{1,0:T(8,128)(2,1)} %get-tuple-element.46.a_ref, bf16[528,256]{1,0:T(8,128)(2,1)} %copy-done.10, bf16[16,512,256]{2,1,0:T(8,128)(2,1)} %bitcast.55, bf16[16,128,256]{2,1,0:T(8,128)(2,1)} %copy-done.4), custom_call_target="tpu_custom_call" | custom-call | flops 6 | bytes 6 | tf_op jit(solution)/shard_map/outp/pallas_call | solution.py:260
  102.0 2.2 collective-permute-done.10
  104.2 1.3 add_convert_fusion.5
  105.6 0.9 collective-permute-start.12
  106.5 1.9 collective-permute-start.13
  108.5 1.1 collective-permute-start.14
  109.5 9.5 %collective-permute-done.14 = f32[3,128,128]{2,1,0:T(8,128)S(1)} collective-permute-done((f32[3,128,128]{2,1,0:T(8,128)S(1)}, f32[3,128,128]{2,1,0:T(8,128)S(1)}, u32[]{:S(2)}, u32[]{:S(2)}) %collective-permute-start.14) | collective-permute-done | bytes 196640 | tf_op jit(solution)/shard_map/ppermute | solution.py:24
  119.0 0.8 collective-permute-done.12
  120.0 0.4 collective-permute-start.16
  120.4 2.6 %collective-permute-start.15 = (bf16[2,528,256]{2,1,0:T(8,128)(2,1)S(1)}, bf16[2,528,256]{2,1,0:T(8,128)(2,1)S(1)}, u32[]{:S(2)}, u32[]{:S(2)}) collective-permute-start(bf16[2,528,256]{2,1,0:T(8,128)(2,1)S(1)} %add_convert_fusion.3.x0), channel_id=1, source_target_pairs={{0,6},{2,0},{4,2},{6,4},{1,7},{3,1},{5,3},{7,5},{8,14},{10,8},{12,... | collective-permute-start | bytes 1622024 | tf_op jit(solution)/shard_map/ppermute | solution.py:24
  123.0 10.6 %collective-permute-done.16.x4 = bf16[2,528,256]{2,1,0:T(8,128)(2,1)S(1)} collective-permute-done((bf16[2,528,256]{2,1,0:T(8,128)(2,1)S(1)}, bf16[2,528,256]{2,1,0:T(8,128)(2,1)S(1)}, u32[]{:S(2)}, u32[]{:S(2)}) %collective-permute-start.16) | collective-permute-done | bytes 540704 | tf_op jit(solution)/shard_map/ppermute | solution.py:24
  133.6 9.6 %all-gather.7.cloned.1.call-done = bf16[16896,256]{1,0:T(8,128)(2,1)} async-done(((bf16[1056,256]{1,0:T(8,128)(2,1)}), bf16[16896,256]{1,0:T(8,128)(2,1)}) %all-gather.7.cloned.1.call-update) | async-done | bytes 8650768 | tf_op jit(solution)/shard_map/all_gather | solution.py:429
  143.2 0.7 collective-permute-start.19
  143.9 1.3 collective-permute-start.17
  145.1 1.6 collective-permute-start.18
  146.7 6.6 %collective-permute-done.17.x2 = bf16[1,528,256]{2,1,0:T(8,128)(2,1)S(1)} collective-permute-done((bf16[1,528,256]{2,1,0:T(8,128)(2,1)S(1)}, bf16[1,528,256]{2,1,0:T(8,128)(2,1)S(1)}, u32[]{:S(2)}, u32[]{:S(2)}) %collective-permute-start.17) | collective-permute-done | bytes 270368 | tf_op jit(solution)/shard_map/ppermute | solution.py:24
  153.3 4.1 %collective-permute-done.19.h_ref = bf16[16,1056,256]{2,1,0:T(8,128)(2,1)} collective-permute-done((bf16[16,1056,256]{2,1,0:T(8,128)(2,1)}, bf16[16,1056,256]{2,1,0:T(8,128)(2,1)}, u32[]{:S(2)}, u32[]{:S(2)}) %collective-permute-start.19) | collective-permute-done | bytes 8650784 | tf_op jit(solution)/shard_map/ppermute | solution.py:24
  157.4 13.6 %mlp.1 = (bf16[2,528,704]{2,1,0:T(8,128)(2,1)}, bf16[1,528,256]{2,1,0:T(8,128)(2,1)}, bf16[1,528,256]{2,1,0:T(8,128)(2,1)}) custom-call(s32[6]{0:T(128)} %stack.70.idx, bf16[2,528,256]{2,1,0:T(8,128)(2,1)} %copy-done.2, bf16[2,528,256]{2,1,0:T(8,128)(2,1)} %copy-done.9, bf16[1,528,256]{2,1,0:T(8,128)(2,1)} %copy-done.22, bf16[1,528,256]{2,1,0:T(8,128)(2,1)} %copy-done.23, ...), custom_call_target="tpu_custom_call" | custom-call | flops 16 | bytes 16 | tf_op jit(solution)/shard_map/mlp/pallas_call | solution.py:327
  171.0 1.3 collective-permute-start.20
  172.3 1.5 collective-permute-start.21
  173.7 7.6 %down.1 = (f32[2,528,256]{2,1,0:T(8,128)}, f32[2,528,256]{2,1,0:T(8,128)}, f32[2,528,256]{2,1,0:T(8,128)}) custom-call(s32[6]{0:T(128)} %stack.70.idx, bf16[2,528,704]{2,1,0:T(8,128)(2,1)} %get-tuple-element.56.hid, bf16[16,1056,256]{2,1,0:T(8,128)(2,1)} %bitcast.58, bf16[16,1056,256]{2,1,0:T(8,128)(2,1)} %collective-permute-done.19.h_ref), custom_call_target="tpu_custom_call" | custom-call | flops 5 | bytes 5 | tf_op jit(solution)/shard_map/down/pallas_call | solution.py:352
  181.4 1.4 add_convert_fusion.2
  183.0 2.7 %collective-permute-start.23 = (bf16[2,528,256]{2,1,0:T(8,128)(2,1)S(1)}, bf16[2,528,256]{2,1,0:T(8,128)(2,1)S(1)}, u32[]{:S(2)}, u32[]{:S(2)}) collective-permute-start(bf16[2,528,256]{2,1,0:T(8,128)(2,1)S(1)} %add_convert_fusion.1), channel_id=1, source_target_pairs={{0,6},{2,0},{4,2},{6,4},{1,7},{3,1},{5,3},{7,5},{8,14},{10,8},{12,... | collective-permute-start | bytes 1622024 | tf_op jit(solution)/shard_map/ppermute | solution.py:24
  185.8 11.2 %collective-permute-done.22 = bf16[2,528,256]{2,1,0:T(8,128)(2,1)S(1)} collective-permute-done((bf16[2,528,256]{2,1,0:T(8,128)(2,1)S(1)}, bf16[2,528,256]{2,1,0:T(8,128)(2,1)S(1)}, u32[]{:S(2)}, u32[]{:S(2)}) %collective-permute-start.22) | collective-permute-done | bytes 540704 | tf_op jit(solution)/shard_map/ppermute | solution.py:24
  197.0 0.2 add_convert_fusion
  197.3 0.9 pad_maximum_fusion.2
  198.2 5.3 %all-to-all-start.1 = ((bf16[4,528,128]{2,1,0:T(8,128)(2,1)}), bf16[4,528,128]{2,1,0:T(8,128)(2,1)S(1)}, u32[]{:S(2)}, u32[]{:S(2)}) async-start(bf16[4,528,128]{2,1,0:T(8,128)(2,1)} %bitcast.26), calls=%async_computation.1 | async-start | bytes 1081344 | tf_op jit(solution)/shard_map/all_to_all | solution.py:453
  203.5 0.7 fusion.1
  204.2 0.7 fusion
  204.9 6.7 %all-to-all-done.1 = bf16[4,528,128]{2,1,0:T(8,128)(2,1)S(1)} async-done(((bf16[4,528,128]{2,1,0:T(8,128)(2,1)}), bf16[4,528,128]{2,1,0:T(8,128)(2,1)S(1)}, u32[]{:S(2)}, u32[]{:S(2)}) %all-to-all-start.1) | async-done | bytes 540704 | tf_op jit(solution)/shard_map/all_to_all | solution.py:453
  211.6 0.6 copy.41
  212.2 0.8 slice.96
  (103 shorter events, 1.6 us)
Async XLA Ops:
  7.2 2.9 %copy-start.29 = (bf16[4,128]{1,0:T(4,128)(2,1)S(1)}, bf16[4,128]{1,0:T(4,128)(2,1)}, u32[]{:S(2)}) copy-start(bf16[4,128]{1,0:T(4,128)(2,1)} %param.13) | copy-start | bytes 3076
  7.2 3.0 %copy-start.16 = (bf16[2,1024,128]{2,1,0:T(8,128)(2,1)S(1)}, bf16[2,1024,128]{2,1,0:T(8,128)(2,1)}, u32[]{:S(2)}) copy-start(bf16[2,1024,128]{2,1,0:T(8,128)(2,1)} %param.12) | copy-start | bytes 1572868
  7.2 59.3 %all-gather.5.cloned.1.call-start = ((), (), s32[]{:S(2)}) async-start(), calls=%async_computation.2 | async-start | bytes 4456448 | tf_op jit(solution)/shard_map/all_gather | solution.py:415
  10.2 6.0 %copy-start.24 = (f32[4,1,128,128]{3,2,1,0:T(8,128)S(1)}, f32[4,1,128,128]{3,2,1,0:T(8,128)}, u32[]{:S(2)}) copy-start(f32[4,1,128,128]{3,2,1,0:T(8,128)} %param.15) | copy-start | bytes 786436
  10.2 6.0 %copy-start.26 = (f32[128]{0:T(128)S(1)}, f32[128]{0:T(128)}, u32[]{:S(2)}) copy-start(f32[128]{0:T(128)} %param.18) | copy-start | bytes 1540
  10.2 6.1 %copy-start.27 = (f32[128]{0:T(128)S(1)}, f32[128]{0:T(128)}, u32[]{:S(2)}) copy-start(f32[128]{0:T(128)} %param.17) | copy-start | bytes 1540
  11.2 6.5 %copy-start.28 = (s32[2]{0:T(128)S(1)}, s32[2]{0:T(128)}, u32[]{:S(2)}) copy-start(s32[2]{0:T(128)} %param.14) | copy-start | bytes 28
  11.2 13.1 %all-to-all-start = ((bf16[4,528,128]{2,1,0:T(8,128)(2,1)}), bf16[4,528,128]{2,1,0:T(8,128)(2,1)S(1)}, u32[]{:S(2)}, u32[]{:S(2)}) async-start(bf16[4,528,128]{2,1,0:T(8,128)(2,1)} %maximum_maximum_fusion), calls=%async_computation | async-start | bytes 1081344 | tf_op jit(solution)/shard_map/all_to_all | solution.py:405
  16.2 127.0 %all-gather.7.cloned.1.call-start = ((), (), s32[]{:S(2)}) async-start(), calls=%async_computation.3 | async-start | bytes 9191424 | tf_op jit(solution)/shard_map/all_gather | solution.py:429
  16.3 11.0 %collective-permute-start = (f32[258,128]{1,0:T(8,128)S(1)}, f32[258,128]{1,0:T(8,128)S(1)}, u32[]{:S(2)}, u32[]{:S(2)}) collective-permute-start(f32[258,128]{1,0:T(8,128)S(1)} %pad_maximum_fusion.5), channel_id=1, source_target_pairs={{0,8},{8,0},{1,9},{9,1},{2,10},{10,2},{3,11},{11,3},{4,12},{12,4},... | collective-permute-start | bytes 396296 | tf_op jit(solution)/shard_map/ppermute | solution.py:24
  24.5 19.8 %copy-start = (bf16[2,2,66,8,128]{4,3,1,2,0:T(8,128)(2,1)}, bf16[2,2,66,8,128]{4,3,1,2,0:T(8,128)(2,1)S(1)}, u32[]{:S(2)}) copy-start(bf16[2,2,66,8,128]{4,3,1,2,0:T(8,128)(2,1)S(1)} %copy.40) | copy-start | bytes 1622020
  27.3 12.5 %collective-permute-start.1 = (bf16[2,528,256]{2,1,0:T(8,128)(2,1)S(1)}, bf16[2,528,256]{2,1,0:T(8,128)(2,1)S(1)}, u32[]{:S(2)}, u32[]{:S(2)}) collective-permute-start(bf16[2,528,256]{2,1,0:T(8,128)(2,1)S(1)} %bitcast.59), channel_id=1, source_target_pairs={{0,6},{2,0},{4,2},{6,4},{1,7},{3,1},{5,3},{7,5},{8,14},{10,8},{12,... | collective-permute-start | bytes 1622024 | tf_op jit(solution)/shard_map/ppermute | solution.py:24
  30.0 12.9 %collective-permute-start.2 = (bf16[2,528,256]{2,1,0:T(8,128)(2,1)S(1)}, bf16[2,528,256]{2,1,0:T(8,128)(2,1)S(1)}, u32[]{:S(2)}, u32[]{:S(2)}) collective-permute-start(bf16[2,528,256]{2,1,0:T(8,128)(2,1)S(1)} %bitcast.60), channel_id=1, source_target_pairs={{0,2},{2,4},{4,6},{6,0},{1,3},{3,5},{5,7},{7,1},{8,10},{10,12},{12... | collective-permute-start | bytes 1622024 | tf_op jit(solution)/shard_map/ppermute | solution.py:24
  39.8 7.6 %copy-start.5 = (bf16[2,528,256]{2,1,0:T(8,128)(2,1)}, bf16[2,528,256]{2,1,0:T(8,128)(2,1)S(1)}, u32[]{:S(2)}) copy-start(bf16[2,528,256]{2,1,0:T(8,128)(2,1)S(1)} %collective-permute-done.1.xo1) | copy-start | bytes 1622020
  42.9 4.4 %copy-start.6 = (bf16[2,528,256]{2,1,0:T(8,128)(2,1)}, bf16[2,528,256]{2,1,0:T(8,128)(2,1)S(1)}, u32[]{:S(2)}) copy-start(bf16[2,528,256]{2,1,0:T(8,128)(2,1)S(1)} %collective-permute-done.2.xo4) | copy-start | bytes 1622020
  44.3 13.3 %copy-start.15 = (f32[256,704]{0,1:T(8,128)S(1)}, f32[256,704]{0,1:T(8,128)}, u32[]{:S(2)}) copy-start(f32[256,704]{0,1:T(8,128)} %param.21) | copy-start | bytes 2162692
  44.3 13.3 %copy-start.17 = (f32[352,256]{1,0:T(8,128)S(1)}, f32[352,256]{1,0:T(8,128)}, u32[]{:S(2)}) copy-start(f32[352,256]{1,0:T(8,128)} %param.22) | copy-start | bytes 1081348
  44.3 14.8 %collective-permute-start.5 = (bf16[3,2,528,256]{3,2,1,0:T(8,128)(2,1)}, bf16[3,2,528,256]{3,2,1,0:T(8,128)(2,1)S(1)}, u32[]{:S(2)}, u32[]{:S(2)}) collective-permute-start(bf16[3,2,528,256]{3,2,1,0:T(8,128)(2,1)} %pad_maximum_fusion), channel_id=1, source_target_pairs={{0,1},{1,0},{2,3},{3,2},{4,5},{5,4},{6,7},{7,6},{8,9},{9,8},{10,11... | collective-permute-start | bytes 4866056 | tf_op jit(solution)/shard_map/ppermute | solution.py:24
  47.3 9.5 %collective-permute-start.3 = (bf16[1,528,256]{2,1,0:T(8,128)(2,1)S(1)}, bf16[1,528,256]{2,1,0:T(8,128)(2,1)S(1)}, u32[]{:S(2)}, u32[]{:S(2)}) collective-permute-start(bf16[1,528,256]{2,1,0:T(8,128)(2,1)S(1)} %slice.90), channel_id=1, source_target_pairs={{0,2},{2,4},{4,6},{6,0},{1,3},{3,5},{5,7},{7,1},{8,10},{10,12},{12... | collective-permute-start | bytes 811016 | tf_op jit(solution)/shard_map/ppermute | solution.py:24
  47.4 10.1 %collective-permute-start.4 = (bf16[1,528,256]{2,1,0:T(8,128)(2,1)S(1)}, bf16[1,528,256]{2,1,0:T(8,128)(2,1)S(1)}, u32[]{:S(2)}, u32[]{:S(2)}) collective-permute-start(bf16[1,528,256]{2,1,0:T(8,128)(2,1)S(1)} %slice.76), channel_id=1, source_target_pairs={{0,6},{2,0},{4,2},{6,4},{1,7},{3,1},{5,3},{7,5},{8,14},{10,8},{12,... | collective-permute-start | bytes 811016 | tf_op jit(solution)/shard_map/ppermute | solution.py:24
  56.8 1.7 copy-start.18
  56.8 1.9 collective-permute-start.6
  57.5 1.0 copy-start.19
  57.5 1.6 collective-permute-start.7
  58.7 10.2 %copy-start.20 = (bf16[1,528,256]{2,1,0:T(8,128)(2,1)}, bf16[1,528,256]{2,1,0:T(8,128)(2,1)S(1)}, u32[]{:S(2)}) copy-start(bf16[1,528,256]{2,1,0:T(8,128)(2,1)S(1)} %collective-permute-done.6.xp2) | copy-start | bytes 811012
  59.0 9.8 %copy-start.21 = (bf16[1,528,256]{2,1,0:T(8,128)(2,1)}, bf16[1,528,256]{2,1,0:T(8,128)(2,1)S(1)}, u32[]{:S(2)}) copy-start(bf16[1,528,256]{2,1,0:T(8,128)(2,1)S(1)} %collective-permute-done.7.xp3) | copy-start | bytes 811012
  59.0 9.8 %copy-start.7 = (bf16[3,2,528,256]{3,2,1,0:T(8,128)(2,1)}, bf16[3,2,528,256]{3,2,1,0:T(8,128)(2,1)S(1)}, u32[]{:S(2)}) copy-start(bf16[3,2,528,256]{3,2,1,0:T(8,128)(2,1)S(1)} %collective-permute-done.5.xpm) | copy-start | bytes 4866052
  68.8 21.7 %collective-permute-start.9 = (bf16[16,128,256]{2,1,0:T(8,128)(2,1)}, bf16[16,128,256]{2,1,0:T(8,128)(2,1)S(1)}, u32[]{:S(2)}, u32[]{:S(2)}) collective-permute-start(bf16[16,128,256]{2,1,0:T(8,128)(2,1)} %slice.91), channel_id=1, source_target_pairs={{0,1},{1,0},{2,3},{3,2},{4,5},{5,4},{6,7},{7,6},{8,9},{9,8},{10,11... | collective-permute-start | bytes 3145736 | tf_op jit(solution)/shard_map/ppermute | solution.py:24
  88.7 1.8 collective-permute-start.8
  90.5 0.7 copy-start.10
  90.5 1.1 copy-start.4
  94.7 9.4 %collective-permute-start.10 = (bf16[1,528,256]{2,1,0:T(8,128)(2,1)}, bf16[1,528,256]{2,1,0:T(8,128)(2,1)S(1)}, u32[]{:S(2)}, u32[]{:S(2)}) collective-permute-start(bf16[1,528,256]{2,1,0:T(8,128)(2,1)} %get-tuple-element.44), channel_id=1, source_target_pairs={{0,2},{2,4},{4,6},{6,0},{1,3},{3,5},{5,7},{7,1},{8,10},{10,12},{12... | collective-permute-start | bytes 811016 | tf_op jit(solution)/shard_map/ppermute | solution.py:24
  96.0 8.2 %collective-permute-start.11 = (bf16[1,528,256]{2,1,0:T(8,128)(2,1)}, bf16[1,528,256]{2,1,0:T(8,128)(2,1)S(1)}, u32[]{:S(2)}, u32[]{:S(2)}) collective-permute-start(bf16[1,528,256]{2,1,0:T(8,128)(2,1)} %get-tuple-element.45), channel_id=1, source_target_pairs={{0,6},{2,0},{4,2},{6,4},{1,7},{3,1},{5,3},{7,5},{8,14},{10,8},{12,... | collective-permute-start | bytes 811016 | tf_op jit(solution)/shard_map/ppermute | solution.py:24
  102.0 4.5 %copy-start.13 = (f32[2,528,256]{2,1,0:T(8,128)S(1)}, f32[2,528,256]{2,1,0:T(8,128)}, u32[]{:S(2)}) copy-start(f32[2,528,256]{2,1,0:T(8,128)} %get-tuple-element.50) | copy-start | bytes 3244036
  105.5 2.9 %copy-start.30 = (f32[3,128,128]{2,1,0:T(8,128)S(1)}, f32[3,128,128]{2,1,0:T(8,128)}, u32[]{:S(2)}) copy-start(f32[3,128,128]{2,1,0:T(8,128)} %get-tuple-element.52) | copy-start | bytes 589828
  105.5 14.2 %copy-start.1 = (bf16[2,2,66,8,128]{4,3,1,2,0:T(8,128)(2,1)S(1)}, bf16[2,2,66,8,128]{4,3,1,2,0:T(8,128)(2,1)}, u32[]{:S(2)}) copy-start(bf16[2,2,66,8,128]{4,3,1,2,0:T(8,128)(2,1)} %copy-done) | copy-start | bytes 1622020
  105.5 14.2 %copy-start.11 = (f32[2,528,256]{2,1,0:T(8,128)S(1)}, f32[2,528,256]{2,1,0:T(8,128)}, u32[]{:S(2)}) copy-start(f32[2,528,256]{2,1,0:T(8,128)} %get-tuple-element.47) | copy-start | bytes 3244036
  105.6 14.2 %collective-permute-start.12 = (bf16[2,528,256]{2,1,0:T(8,128)(2,1)S(1)}, bf16[2,528,256]{2,1,0:T(8,128)(2,1)S(1)}, u32[]{:S(2)}, u32[]{:S(2)}) collective-permute-start(bf16[2,528,256]{2,1,0:T(8,128)(2,1)S(1)} %add_convert_fusion.5), channel_id=1, source_target_pairs={{0,2},{2,4},{4,6},{6,0},{1,3},{3,5},{5,7},{7,1},{8,10},{10,12},{12... | collective-permute-start | bytes 1622024 | tf_op jit(solution)/shard_map/ppermute | solution.py:24
  106.5 13.2 %collective-permute-start.13 = (bf16[2,528,256]{2,1,0:T(8,128)(2,1)S(1)}, bf16[2,528,256]{2,1,0:T(8,128)(2,1)S(1)}, u32[]{:S(2)}, u32[]{:S(2)}) collective-permute-start(bf16[2,528,256]{2,1,0:T(8,128)(2,1)S(1)} %add_convert_fusion.4), channel_id=1, source_target_pairs={{0,6},{2,0},{4,2},{6,4},{1,7},{3,1},{5,3},{7,5},{8,14},{10,8},{12,... | collective-permute-start | bytes 1622024 | tf_op jit(solution)/shard_map/ppermute | solution.py:24
  108.5 10.6 %collective-permute-start.14 = (f32[3,128,128]{2,1,0:T(8,128)S(1)}, f32[3,128,128]{2,1,0:T(8,128)S(1)}, u32[]{:S(2)}, u32[]{:S(2)}) collective-permute-start(f32[3,128,128]{2,1,0:T(8,128)S(1)} %copy-done.30), channel_id=1, source_target_pairs={{0,8},{8,0},{1,9},{9,1},{2,10},{10,2},{3,11},{11,3},{4,12},{12,4},... | collective-permute-start | bytes 589832 | tf_op jit(solution)/shard_map/ppermute | solution.py:24
  120.0 37.3 %copy-start.2 = (bf16[2,528,256]{2,1,0:T(8,128)(2,1)}, bf16[2,528,256]{2,1,0:T(8,128)(2,1)S(1)}, u32[]{:S(2)}) copy-start(bf16[2,528,256]{2,1,0:T(8,128)(2,1)S(1)} %add_convert_fusion.3.x0) | copy-start | bytes 1622020
  120.0 13.6 %collective-permute-start.16 = (bf16[2,528,256]{2,1,0:T(8,128)(2,1)S(1)}, bf16[2,528,256]{2,1,0:T(8,128)(2,1)S(1)}, u32[]{:S(2)}, u32[]{:S(2)}) collective-permute-start(bf16[2,528,256]{2,1,0:T(8,128)(2,1)S(1)} %add_convert_fusion.3.x0), channel_id=1, source_target_pairs={{0,2},{2,4},{4,6},{6,0},{1,3},{3,5},{5,7},{7,1},{8,10},{10,12},{12... | collective-permute-start | bytes 1622024 | tf_op jit(solution)/shard_map/ppermute | solution.py:24
  120.4 13.2 %collective-permute-start.15 = (bf16[2,528,256]{2,1,0:T(8,128)(2,1)S(1)}, bf16[2,528,256]{2,1,0:T(8,128)(2,1)S(1)}, u32[]{:S(2)}, u32[]{:S(2)}) collective-permute-start(bf16[2,528,256]{2,1,0:T(8,128)(2,1)S(1)} %add_convert_fusion.3.x0), channel_id=1, source_target_pairs={{0,6},{2,0},{4,2},{6,4},{1,7},{3,1},{5,3},{7,5},{8,14},{10,8},{12,... | collective-permute-start | bytes 1622024 | tf_op jit(solution)/shard_map/ppermute | solution.py:24
  133.6 23.7 %copy-start.8 = (bf16[2,528,256]{2,1,0:T(8,128)(2,1)}, bf16[2,528,256]{2,1,0:T(8,128)(2,1)S(1)}, u32[]{:S(2)}) copy-start(bf16[2,528,256]{2,1,0:T(8,128)(2,1)S(1)} %collective-permute-done.16.x4) | copy-start | bytes 1622020
  133.6 23.7 %copy-start.9 = (bf16[2,528,256]{2,1,0:T(8,128)(2,1)}, bf16[2,528,256]{2,1,0:T(8,128)(2,1)S(1)}, u32[]{:S(2)}) copy-start(bf16[2,528,256]{2,1,0:T(8,128)(2,1)S(1)} %collective-permute-done.15.x1) | copy-start | bytes 1622020
  143.2 14.2 %collective-permute-start.19 = (bf16[16,1056,256]{2,1,0:T(8,128)(2,1)}, bf16[16,1056,256]{2,1,0:T(8,128)(2,1)}, u32[]{:S(2)}, u32[]{:S(2)}) collective-permute-start(bf16[16,1056,256]{2,1,0:T(8,128)(2,1)} %bitcast.56), channel_id=1, source_target_pairs={{0,1},{1,0},{2,3},{3,2},{4,5},{5,4},{6,7},{7,6},{8,9},{9,8},{10,11... | collective-permute-start | bytes 25952264 | tf_op jit(solution)/shard_map/ppermute | solution.py:24
  143.9 9.4 %collective-permute-start.17 = (bf16[1,528,256]{2,1,0:T(8,128)(2,1)S(1)}, bf16[1,528,256]{2,1,0:T(8,128)(2,1)S(1)}, u32[]{:S(2)}, u32[]{:S(2)}) collective-permute-start(bf16[1,528,256]{2,1,0:T(8,128)(2,1)S(1)} %slice.92), channel_id=1, source_target_pairs={{0,2},{2,4},{4,6},{6,0},{1,3},{3,5},{5,7},{7,1},{8,10},{10,12},{12... | collective-permute-start | bytes 811016 | tf_op jit(solution)/shard_map/ppermute | solution.py:24
  145.1 8.1 %collective-permute-start.18 = (bf16[1,528,256]{2,1,0:T(8,128)(2,1)S(1)}, bf16[1,528,256]{2,1,0:T(8,128)(2,1)S(1)}, u32[]{:S(2)}, u32[]{:S(2)}) collective-permute-start(bf16[1,528,256]{2,1,0:T(8,128)(2,1)S(1)} %slice.93), channel_id=1, source_target_pairs={{0,6},{2,0},{4,2},{6,4},{1,7},{3,1},{5,3},{7,5},{8,14},{10,8},{12,... | collective-permute-start | bytes 811016 | tf_op jit(solution)/shard_map/ppermute | solution.py:24
  153.3 4.1 %copy-start.22 = (bf16[1,528,256]{2,1,0:T(8,128)(2,1)}, bf16[1,528,256]{2,1,0:T(8,128)(2,1)S(1)}, u32[]{:S(2)}) copy-start(bf16[1,528,256]{2,1,0:T(8,128)(2,1)S(1)} %collective-permute-done.17.x2) | copy-start | bytes 811012
  153.3 4.1 %copy-start.23 = (bf16[1,528,256]{2,1,0:T(8,128)(2,1)}, bf16[1,528,256]{2,1,0:T(8,128)(2,1)S(1)}, u32[]{:S(2)}) copy-start(bf16[1,528,256]{2,1,0:T(8,128)(2,1)S(1)} %collective-permute-done.18.x3) | copy-start | bytes 811012
  171.0 10.4 %collective-permute-start.20 = (bf16[1,528,256]{2,1,0:T(8,128)(2,1)}, bf16[1,528,256]{2,1,0:T(8,128)(2,1)S(1)}, u32[]{:S(2)}, u32[]{:S(2)}) collective-permute-start(bf16[1,528,256]{2,1,0:T(8,128)(2,1)} %get-tuple-element.59), channel_id=1, source_target_pairs={{0,2},{2,4},{4,6},{6,0},{1,3},{3,5},{5,7},{7,1},{8,10},{10,12},{12... | collective-permute-start | bytes 811016 | tf_op jit(solution)/shard_map/ppermute | solution.py:24
  172.3 9.1 %collective-permute-start.21 = (bf16[1,528,256]{2,1,0:T(8,128)(2,1)}, bf16[1,528,256]{2,1,0:T(8,128)(2,1)S(1)}, u32[]{:S(2)}, u32[]{:S(2)}) collective-permute-start(bf16[1,528,256]{2,1,0:T(8,128)(2,1)} %get-tuple-element.60), channel_id=1, source_target_pairs={{0,6},{2,0},{4,2},{6,4},{1,7},{3,1},{5,3},{7,5},{8,14},{10,8},{12,... | collective-permute-start | bytes 811016 | tf_op jit(solution)/shard_map/ppermute | solution.py:24
  181.4 1.6 copy-start.14
  182.8 2.9 %copy-start.25 = (f32[3,128,128]{2,1,0:T(8,128)S(1)}, f32[3,128,128]{2,1,0:T(8,128)}, u32[]{:S(2)}) copy-start(f32[3,128,128]{2,1,0:T(8,128)} %get-tuple-element.65) | copy-start | bytes 589828
  182.8 14.1 %collective-permute-start.22 = (bf16[2,528,256]{2,1,0:T(8,128)(2,1)S(1)}, bf16[2,528,256]{2,1,0:T(8,128)(2,1)S(1)}, u32[]{:S(2)}, u32[]{:S(2)}) collective-permute-start(bf16[2,528,256]{2,1,0:T(8,128)(2,1)S(1)} %add_convert_fusion.2), channel_id=1, source_target_pairs={{0,2},{2,4},{4,6},{6,0},{1,3},{3,5},{5,7},{7,1},{8,10},{10,12},{12... | collective-permute-start | bytes 1622024 | tf_op jit(solution)/shard_map/ppermute | solution.py:24
  182.9 14.0 %copy-start.3 = (bf16[2,528,256]{2,1,0:T(8,128)(2,1)S(1)}, bf16[2,528,256]{2,1,0:T(8,128)(2,1)}, u32[]{:S(2)}) copy-start(bf16[2,528,256]{2,1,0:T(8,128)(2,1)} %copy-done.2) | copy-start | bytes 1622020
  182.9 14.0 %copy-start.12 = (f32[2,528,256]{2,1,0:T(8,128)S(1)}, f32[2,528,256]{2,1,0:T(8,128)}, u32[]{:S(2)}) copy-start(f32[2,528,256]{2,1,0:T(8,128)} %get-tuple-element.57) | copy-start | bytes 3244036
  183.0 13.9 %collective-permute-start.23 = (bf16[2,528,256]{2,1,0:T(8,128)(2,1)S(1)}, bf16[2,528,256]{2,1,0:T(8,128)(2,1)S(1)}, u32[]{:S(2)}, u32[]{:S(2)}) collective-permute-start(bf16[2,528,256]{2,1,0:T(8,128)(2,1)S(1)} %add_convert_fusion.1), channel_id=1, source_target_pairs={{0,6},{2,0},{4,2},{6,4},{1,7},{3,1},{5,3},{7,5},{8,14},{10,8},{12,... | collective-permute-start | bytes 1622024 | tf_op jit(solution)/shard_map/ppermute | solution.py:24
  198.2 13.4 %all-to-all-start.1 = ((bf16[4,528,128]{2,1,0:T(8,128)(2,1)}), bf16[4,528,128]{2,1,0:T(8,128)(2,1)S(1)}, u32[]{:S(2)}, u32[]{:S(2)}) async-start(bf16[4,528,128]{2,1,0:T(8,128)(2,1)} %bitcast.26), calls=%async_computation.1 | async-start | bytes 1081344 | tf_op jit(solution)/shard_map/all_to_all | solution.py:453
Sparse Core Ops, SparseCore 0:
  10.7 55.6 all-gather.4
  68.7 74.4 all-gather.6

commit v4 on v3

--- a/solution.py
+++ b/solution.py
@@ -273,13 +273,13 @@
     )(idx, a, b, u, v)
 
 
-def down_copies(steps, x, refs, wd):
+def down_copies(steps, x, ref, wd):
     out = []
     for slot, s, z, r in blocks_of(steps, x):
         for j in range(2):
-            for cc, ref in enumerate(refs):
+            for cc in range(2):
                 at = cc * 704 + j * 352
-                out.append((ref.at[2 * r + j, 704:1056], wd.at[slot, at : at + 352, :]))
+                out.append((ref.at[2 * r + j, cc, 704:1056], wd.at[slot, at : at + 352, :]))
     return out
 
 
@@ -289,18 +289,18 @@
         put(steps, outs, s, z, total)
 
 
-def mlp_kernel(idx, x0, x1, x2, x3, x4, g_ref, h_ref, gain_ref, hid, q0, q1, xcat, wg, wd, sems):
+def mlp_kernel(idx, x0, x1, x2, x3, x4, w_ref, gain_ref, hid, q0, q1, xcat, wg, wd, sems):
     x = idx[3]
     started = [copy_all(x_copies((x0, x1, x2, x3, x4), xcat, x), sems)]
-    for cc, ref in ((0, g_ref), (1, h_ref)):
+    for cc in range(2):
         copies = []
         for i in range(16):
             for g in range(2):
                 at, r = (i & 1) * 352, i // 2
                 dst = wg.at[cc, g, at : at + 352, r * 256 : (r + 1) * 256]
-                copies.append((ref.at[i, g * 352 : (g + 1) * 352], dst))
+                copies.append((w_ref.at[i, cc, g * 352 : (g + 1) * 352], dst))
         started.append(copy_all(copies, sems.at[8 + cc * 32 : 40 + cc * 32]))
-    last = copy_all(down_copies((2,), x, (g_ref, h_ref), wd), sems.at[72:80])
+    last = copy_all(down_copies((2,), x, w_ref, wd), sems.at[72:80])
     for cp in started[0]:
         cp.wait()
 
@@ -323,11 +323,11 @@
     down_dots((2,), x, hid, wd, (q0, q1))
 
 
-def mlp_call(idx, xs, g, h, gain):
+def mlp_call(idx, xs, w, gain):
     return pl.pallas_call(
         mlp_kernel,
         out_shape=(jax.ShapeDtypeStruct((2, HALF, 704), BF), FAR, FAR),
-        in_specs=[sspec()] + [anyspec()] * 7 + [vspec()],
+        in_specs=[sspec()] + [anyspec()] * 6 + [vspec()],
         out_specs=(vspec(),) * 3,
         scratch_shapes=[
             pltpu.VMEM((HALF, 2048), BF),
@@ -338,21 +338,21 @@
         compiler_params=pltpu.CompilerParams(vmem_limit_bytes=VMEM_LIMIT),
         cost_estimate=cost(16),
         name="mlp",
-    )(idx, *xs, g, h, gain)
-
-
-def down_kernel(steps, idx, hid, g_ref, h_ref, p0, p1, p2, wd, sems):
-    for cp in copy_all(down_copies(steps, idx[3], (g_ref, h_ref), wd), sems):
+    )(idx, *xs, w, gain)
+
+
+def down_kernel(steps, idx, hid, w_ref, p0, p1, p2, wd, sems):
+    for cp in copy_all(down_copies(steps, idx[3], w_ref, wd), sems):
         cp.wait()
     down_dots(steps, idx[3], hid, wd, (p0, p1, p2))
 
 
-def down_call(steps, idx, hid, g, h):
+def down_call(steps, idx, hid, w):
     n = len(steps)
     return pl.pallas_call(
         functools.partial(down_kernel, steps),
         out_shape=shapes_of(steps),
-        in_specs=[sspec(), vspec()] + [anyspec()] * 2,
+        in_specs=[sspec(), vspec(), anyspec()],
         out_specs=(vspec(),) * n,
         scratch_shapes=[
             pltpu.VMEM((2 * n, 1408, 256), BF),
@@ -361,7 +361,7 @@
         compiler_params=pltpu.CompilerParams(vmem_limit_bytes=VMEM_LIMIT),
         cost_estimate=cost(5),
         name="down",
-    )(idx, hid, g, h)
+    )(idx, hid, w)
 
 
 def swap(value, axis):
@@ -426,7 +426,7 @@
     wo2 = swap(early[:, 384:], "c")
     late = jnp.concatenate([w_gu.astype(BF).T, w_down.astype(BF)])
     late = after(late, early, *xp)
-    late = lax.all_gather(late, ("y", "zh", "zl")).reshape(16, 1056, 256)
+    late = lax.all_gather(late, ("y", "zh", "zl", "c")).reshape(16, 2, 1056, 256)
 
     ho, hs, mine, sent = mix_call(idx, xs, xp, early, bias, gain, dst)
     hr = swap(hs, "c")
@@ -445,9 +445,8 @@
     attention = reduce_parts(far, rest, other)
     residual = (x_own.astype(F32) + attention).astype(BF)
     rs = ring_gather(residual, "x")
-    late2 = swap(after(late, rs[1], rs[4]), "c")
-    hid, *far = mlp_call(idx, rs, late, late2, mlp_gain.reshape(1, 2048))
-    down = reduce_parts(far, down_call((1, 3, 0), idx, hid, late, late2))
+    hid, *far = mlp_call(idx, rs, late, mlp_gain.reshape(1, 2048))
+    down = reduce_parts(far, down_call((1, 3, 0), idx, hid, late))
     layer = (residual.astype(F32) + down).astype(BF)
     layer = layer.reshape(2, HALF, 2, 128).transpose(0, 2, 1, 3).reshape(4, HALF, 128)
     back = lax.all_to_all(layer, ("zl", "c"), 0, 0, tiled=True)

time: 220 us -> 208 us (0.945)
  waiting for transfers between devices: 96.2 us -> 85.1 us
    ppermute x24 -> x23, waiting for transfers between devices: 68.2 us -> 61.7 us  [shift(): return lax.ppermute(value, axis, [(i, (i + step) % n) for i in range(n)])]
    all_gather x1, waiting for transfers between devices: 9.55 us -> 4.84 us  [on_device(): lax.all_gather(late, ('y', 'zh', 'zl', 'c')).reshape(16, 2, 1056, 256)]
    ppermute x24 -> x23, starting transfers between devices: 30.2 us -> 29.3 us  [shift(): return lax.ppermute(value, axis, [(i, (i + step) % n) for i in range(n)])]
  transfers between devices with their start and end apart: 28 -> 27, of which waited for: 18 -> 17; matrix products, arithmetic and copies ran while one was open for 5% -> 6% of each run, Pallas kernels for 16% -> 17%
where the time goes in v4:
time: 208 us
  waiting for transfers between devices  85.1 us (41%)
  Pallas kernels  48 us (23%)
  starting transfers between devices  39.4 us (19%)
  between operations  15.7 us (8%)
  other arithmetic  12 us (6%)
  local copies, waits for them, and re-layouts  7.71 us (4%)
    ppermute x23, waiting for transfers between devices, shift(): return lax.ppermute(value, axis, [(i, (i + step) % n) for i in range(n)])  61.7 us
    ppermute x23, starting transfers between devices, shift(): return lax.ppermute(value, axis, [(i, (i + step) % n) for i in range(n)])  29.3 us
    pallas_call x1, Pallas kernels, mix_call(): pl.pallas_call(mix_kernel, out_shape=(jax.ShapeDtypeStruct((HALF, 256), B...  19.1 us
    pallas_call x1, Pallas kernels, mlp_call(): pl.pallas_call(mlp_kernel, out_shape=(jax.ShapeDtypeStruct((2, HALF, 704)...  13.6 us
    pallas_call x2, Pallas kernels, out_call(): pl.pallas_call(functools.partial(out_kernel, steps), out_shape=shapes_of(...  7.67 us
    pallas_call x1, Pallas kernels, down_call(): pl.pallas_call(functools.partial(down_kernel, steps), out_shape=shapes_of...  7.59 us
    all_gather x1, waiting for transfers between devices, on_device(): early = lax.all_gather(early, ('y', 'zh', 'zl')).reshape(16, 512, 256)  7.56 us
    all_to_all x1, waiting for transfers between devices, on_device(): back = lax.all_to_all(layer, ('zl', 'c'), 0, 0, tiled=True)  6.74 us
  transfers between devices with their start and end apart: 27, of which 17 were waited for; matrix products, arithmetic and copies ran while one was open for 6% of the time, Pallas kernels for 17%

profile of v4, /device:TPU:1, one launch (start us, length us, event | category | flops | bytes accessed | tf_op | source)
XLA Modules:
  0.0 207.9 jit_solution(860070086412951530)
XLA Ops:
  7.2 1.2 copy.33
  8.4 0.9 convert_element_type.54
  9.3 0.7 pad_maximum_fusion.4
  10.2 1.0 maximum_maximum_fusion
  11.2 5.0 %all-to-all-start = ((bf16[4,528,128]{2,1,0:T(8,128)(2,1)}), bf16[4,528,128]{2,1,0:T(8,128)(2,1)S(1)}, u32[]{:S(2)}, u32[]{:S(2)}) async-start(bf16[4,528,128]{2,1,0:T(8,128)(2,1)} %maximum_maximum_fusion), calls=%async_computation | async-start | bytes 1081344 | tf_op jit(solution)/shard_map/all_to_all | solution.py:405
  16.3 1.5 collective-permute-start
  17.7 0.6 fusion.4
  19.5 0.7 stack.70.idx
  20.2 4.2 %all-to-all-done = bf16[4,528,128]{2,1,0:T(8,128)(2,1)S(1)} async-done(((bf16[4,528,128]{2,1,0:T(8,128)(2,1)}), bf16[4,528,128]{2,1,0:T(8,128)(2,1)S(1)}, u32[]{:S(2)}, u32[]{:S(2)}) %all-to-all-start) | async-done | bytes 540704 | tf_op jit(solution)/shard_map/all_to_all | solution.py:405
  24.5 2.8 %collective-permute-done = f32[258,128]{1,0:T(8,128)S(1)} collective-permute-done((f32[258,128]{1,0:T(8,128)S(1)}, f32[258,128]{1,0:T(8,128)S(1)}, u32[]{:S(2)}, u32[]{:S(2)}) %collective-permute-start) | collective-permute-done | bytes 132128 | tf_op jit(solution)/shard_map/ppermute | solution.py:24
  27.3 2.7 %collective-permute-start.1 = (bf16[2,528,256]{2,1,0:T(8,128)(2,1)S(1)}, bf16[2,528,256]{2,1,0:T(8,128)(2,1)S(1)}, u32[]{:S(2)}, u32[]{:S(2)}) collective-permute-start(bf16[2,528,256]{2,1,0:T(8,128)(2,1)S(1)} %bitcast.58), channel_id=1, source_target_pairs={{0,6},{2,0},{4,2},{6,4},{1,7},{3,1},{5,3},{7,5},{8,14},{10,8},{12,... | collective-permute-start | bytes 1622024 | tf_op jit(solution)/shard_map/ppermute | solution.py:24
  30.0 0.6 pad_maximum_fusion.6
  30.6 0.7 pad_maximum_fusion.3.dst_ref
  31.3 8.4 %collective-permute-done.1.xo1 = bf16[2,528,256]{2,1,0:T(8,128)(2,1)S(1)} collective-permute-done((bf16[2,528,256]{2,1,0:T(8,128)(2,1)S(1)}, bf16[2,528,256]{2,1,0:T(8,128)(2,1)S(1)}, u32[]{:S(2)}, u32[]{:S(2)}) %collective-permute-start.1) | collective-permute-done | bytes 540704 | tf_op jit(solution)/shard_map/ppermute | solution.py:24
  39.8 3.1 %collective-permute-done.2.xo4 = bf16[2,528,256]{2,1,0:T(8,128)(2,1)S(1)} collective-permute-done((bf16[2,528,256]{2,1,0:T(8,128)(2,1)S(1)}, bf16[2,528,256]{2,1,0:T(8,128)(2,1)S(1)}, u32[]{:S(2)}, u32[]{:S(2)}) %collective-permute-start.2) | collective-permute-done | bytes 540704 | tf_op jit(solution)/shard_map/ppermute | solution.py:24
  42.9 1.4 pad_maximum_fusion
  44.3 3.0 %collective-permute-start.5 = (bf16[3,2,528,256]{3,2,1,0:T(8,128)(2,1)}, bf16[3,2,528,256]{3,2,1,0:T(8,128)(2,1)S(1)}, u32[]{:S(2)}, u32[]{:S(2)}) collective-permute-start(bf16[3,2,528,256]{3,2,1,0:T(8,128)(2,1)} %pad_maximum_fusion), channel_id=1, source_target_pairs={{0,1},{1,0},{2,3},{3,2},{4,5},{5,4},{6,7},{7,6},{8,9},{9,8},{10,11... | collective-permute-start | bytes 4866056 | tf_op jit(solution)/shard_map/ppermute | solution.py:24
  47.6 1.4 collective-permute-start.3
  48.9 6.6 %collective-permute-done.4.xo3 = bf16[1,528,256]{2,1,0:T(8,128)(2,1)S(1)} collective-permute-done((bf16[1,528,256]{2,1,0:T(8,128)(2,1)S(1)}, bf16[1,528,256]{2,1,0:T(8,128)(2,1)S(1)}, u32[]{:S(2)}, u32[]{:S(2)}) %collective-permute-start.4) | collective-permute-done | bytes 270368 | tf_op jit(solution)/shard_map/ppermute | solution.py:24
  55.6 0.7 collective-permute-start.7
  56.3 0.4 collective-permute-done.3.xo2
  56.7 1.0 collective-permute-start.6
  57.8 0.8 pad_maximum_fusion.1
  58.7 0.2 collective-permute-done.6.xp2
  58.9 7.6 %all-gather.5.cloned.1.call-done = bf16[8192,256]{1,0:T(8,128)(2,1)} async-done(((bf16[512,256]{1,0:T(8,128)(2,1)}), bf16[8192,256]{1,0:T(8,128)(2,1)}) %all-gather.5.cloned.1.call-update) | async-done | bytes 4194320 | tf_op jit(solution)/shard_map/all_gather | solution.py:415
  66.5 2.3 %slice.91 = bf16[16,128,256]{2,1,0:T(8,128)(2,1)} slice(bf16[16,512,256]{2,1,0:T(8,128)(2,1)} %bitcast.54), slice={[0:16], [384:512], [0:256]} | slice | bytes 2097152 | tf_op jit(solution)/shard_map/slice | solution.py:426
  68.9 0.8 collective-permute-start.9
  69.6 19.1 %mix.1 = (bf16[528,256]{1,0:T(8,128)(2,1)}, bf16[528,256]{1,0:T(8,128)(2,1)}, f32[3,128,128]{2,1,0:T(8,128)}, f32[3,128,128]{2,1,0:T(8,128)}) custom-call(s32[6]{0:T(128)} %stack.70.idx, bf16[2,528,256]{2,1,0:T(8,128)(2,1)} %bitcast.61, bf16[2,528,256]{2,1,0:T(8,128)(2,1)} %copy-done.5, bf16[1,528,256]{2,1,0:T(8,128)(2,1)} %copy-done.19, ...), custom_call_target="tpu_custom_call" | custom-call | flops 24 | bytes 24 | tf_op jit(solution)/shard_map/mix/pallas_call | solution.py:198
  88.8 1.7 collective-permute-done.8.b_ref
  90.5 0.7 copy-done.10
  91.2 0.3 copy-done.4
  91.6 3.1 %outp.2 = (bf16[1,528,256]{2,1,0:T(8,128)(2,1)}, bf16[1,528,256]{2,1,0:T(8,128)(2,1)}) custom-call(s32[6]{0:T(128)} %stack.70.idx, bf16[528,256]{1,0:T(8,128)(2,1)} %get-tuple-element.45.a_ref, bf16[528,256]{1,0:T(8,128)(2,1)} %copy-done.10, bf16[16,512,256]{2,1,0:T(8,128)(2,1)} %bitcast.56, bf16[16,128,256]{2,1,0:T(8,128)(2,1)} %copy-done.4), custom_call_target="tpu_custom_call" | custom-call | flops 2 | bytes 2 | tf_op jit(solution)/shard_map/outp/pallas_call | solution.py:260
  94.7 1.3 collective-permute-start.10
  96.0 1.5 collective-permute-start.11
  97.5 4.5 %outp.3 = (f32[2,528,256]{2,1,0:T(8,128)}, f32[2,528,256]{2,1,0:T(8,128)}, f32[2,528,256]{2,1,0:T(8,128)}) custom-call(s32[6]{0:T(128)} %stack.70.idx, bf16[528,256]{1,0:T(8,128)(2,1)} %get-tuple-element.45.a_ref, bf16[528,256]{1,0:T(8,128)(2,1)} %copy-done.10, bf16[16,512,256]{2,1,0:T(8,128)(2,1)} %bitcast.57, bf16[16,128,256]{2,1,0:T(8,128)(2,1)} %copy-done.4), custom_call_target="tpu_custom_call" | custom-call | flops 6 | bytes 6 | tf_op jit(solution)/shard_map/outp/pallas_call | solution.py:260
  102.0 2.1 %collective-permute-done.10 = bf16[1,528,256]{2,1,0:T(8,128)(2,1)S(1)} collective-permute-done((bf16[1,528,256]{2,1,0:T(8,128)(2,1)}, bf16[1,528,256]{2,1,0:T(8,128)(2,1)S(1)}, u32[]{:S(2)}, u32[]{:S(2)}) %collective-permute-start.10) | collective-permute-done | bytes 270368 | tf_op jit(solution)/shard_map/ppermute | solution.py:24
  104.1 1.3 add_convert_fusion.5
  105.5 0.9 collective-permute-start.12
  106.5 1.9 collective-permute-start.13
  108.4 1.1 collective-permute-start.14
  109.5 9.5 %collective-permute-done.14 = f32[3,128,128]{2,1,0:T(8,128)S(1)} collective-permute-done((f32[3,128,128]{2,1,0:T(8,128)S(1)}, f32[3,128,128]{2,1,0:T(8,128)S(1)}, u32[]{:S(2)}, u32[]{:S(2)}) %collective-permute-start.14) | collective-permute-done | bytes 196640 | tf_op jit(solution)/shard_map/ppermute | solution.py:24
  119.0 0.7 collective-permute-done.12
  119.7 0.2 add_convert_fusion.3.x0
  120.0 0.4 collective-permute-start.16
  120.4 2.5 %collective-permute-start.15 = (bf16[2,528,256]{2,1,0:T(8,128)(2,1)S(1)}, bf16[2,528,256]{2,1,0:T(8,128)(2,1)S(1)}, u32[]{:S(2)}, u32[]{:S(2)}) collective-permute-start(bf16[2,528,256]{2,1,0:T(8,128)(2,1)S(1)} %add_convert_fusion.3.x0), channel_id=1, source_target_pairs={{0,6},{2,0},{4,2},{6,4},{1,7},{3,1},{5,3},{7,5},{8,14},{10,8},{12,... | collective-permute-start | bytes 1622024 | tf_op jit(solution)/shard_map/ppermute | solution.py:24
  122.9 10.6 %collective-permute-done.16.x4 = bf16[2,528,256]{2,1,0:T(8,128)(2,1)S(1)} collective-permute-done((bf16[2,528,256]{2,1,0:T(8,128)(2,1)S(1)}, bf16[2,528,256]{2,1,0:T(8,128)(2,1)S(1)}, u32[]{:S(2)}, u32[]{:S(2)}) %collective-permute-start.16) | collective-permute-done | bytes 540704 | tf_op jit(solution)/shard_map/ppermute | solution.py:24
  133.7 2.7 %collective-permute-start.18 = (bf16[1,528,256]{2,1,0:T(8,128)(2,1)S(1)}, bf16[1,528,256]{2,1,0:T(8,128)(2,1)S(1)}, u32[]{:S(2)}, u32[]{:S(2)}) collective-permute-start(bf16[1,528,256]{2,1,0:T(8,128)(2,1)S(1)} %slice.93), channel_id=1, source_target_pairs={{0,6},{2,0},{4,2},{6,4},{1,7},{3,1},{5,3},{7,5},{8,14},{10,8},{12,... | collective-permute-start | bytes 811016 | tf_op jit(solution)/shard_map/ppermute | solution.py:24
  136.4 4.0 %collective-permute-done.17.x2 = bf16[1,528,256]{2,1,0:T(8,128)(2,1)S(1)} collective-permute-done((bf16[1,528,256]{2,1,0:T(8,128)(2,1)S(1)}, bf16[1,528,256]{2,1,0:T(8,128)(2,1)S(1)}, u32[]{:S(2)}, u32[]{:S(2)}) %collective-permute-start.17) | collective-permute-done | bytes 270368 | tf_op jit(solution)/shard_map/ppermute | solution.py:24
  140.5 4.8 %all-gather.7.cloned.1.call-done = bf16[33792,256]{1,0:T(8,128)(2,1)} async-done(((bf16[1056,256]{1,0:T(8,128)(2,1)}), bf16[33792,256]{1,0:T(8,128)(2,1)}) %all-gather.7.cloned.1.call-update) | async-done | bytes 17301520 | tf_op jit(solution)/shard_map/all_gather | solution.py:429
  145.3 13.6 %mlp.1 = (bf16[2,528,704]{2,1,0:T(8,128)(2,1)}, bf16[1,528,256]{2,1,0:T(8,128)(2,1)}, bf16[1,528,256]{2,1,0:T(8,128)(2,1)}) custom-call(s32[6]{0:T(128)} %stack.70.idx, bf16[2,528,256]{2,1,0:T(8,128)(2,1)} %copy-done.2, bf16[2,528,256]{2,1,0:T(8,128)(2,1)} %copy-done.9, bf16[1,528,256]{2,1,0:T(8,128)(2,1)} %copy-done.22, bf16[1,528,256]{2,1,0:T(8,128)(2,1)} %copy-done.23, ...), custom_call_target="tpu_custom_call" | custom-call | flops 16 | bytes 16 | tf_op jit(solution)/shard_map/mlp/pallas_call | solution.py:327
  159.0 1.3 collective-permute-start.19
  160.2 1.5 collective-permute-start.20
  161.7 7.6 %down.1 = (f32[2,528,256]{2,1,0:T(8,128)}, f32[2,528,256]{2,1,0:T(8,128)}, f32[2,528,256]{2,1,0:T(8,128)}) custom-call(s32[6]{0:T(128)} %stack.70.idx, bf16[2,528,704]{2,1,0:T(8,128)(2,1)} %get-tuple-element.54.hid, bf16[16,2,1056,256]{3,2,1,0:T(8,128)(2,1)} %bitcast.53), custom_call_target="tpu_custom_call" | custom-call | flops 5 | bytes 5 | tf_op jit(solution)/shard_map/down/pallas_call | solution.py:352
  169.4 1.4 add_convert_fusion.2
  171.0 2.7 %collective-permute-start.22 = (bf16[2,528,256]{2,1,0:T(8,128)(2,1)S(1)}, bf16[2,528,256]{2,1,0:T(8,128)(2,1)S(1)}, u32[]{:S(2)}, u32[]{:S(2)}) collective-permute-start(bf16[2,528,256]{2,1,0:T(8,128)(2,1)S(1)} %add_convert_fusion.1), channel_id=1, source_target_pairs={{0,6},{2,0},{4,2},{6,4},{1,7},{3,1},{5,3},{7,5},{8,14},{10,8},{12,... | collective-permute-start | bytes 1622024 | tf_op jit(solution)/shard_map/ppermute | solution.py:24
  173.8 11.3 %collective-permute-done.21 = bf16[2,528,256]{2,1,0:T(8,128)(2,1)S(1)} collective-permute-done((bf16[2,528,256]{2,1,0:T(8,128)(2,1)S(1)}, bf16[2,528,256]{2,1,0:T(8,128)(2,1)S(1)}, u32[]{:S(2)}, u32[]{:S(2)}) %collective-permute-start.21) | collective-permute-done | bytes 540704 | tf_op jit(solution)/shard_map/ppermute | solution.py:24
  185.1 0.2 add_convert_fusion
  185.4 0.9 pad_maximum_fusion.2
  186.3 5.1 %all-to-all-start.1 = ((bf16[4,528,128]{2,1,0:T(8,128)(2,1)}), bf16[4,528,128]{2,1,0:T(8,128)(2,1)S(1)}, u32[]{:S(2)}, u32[]{:S(2)}) async-start(bf16[4,528,128]{2,1,0:T(8,128)(2,1)} %bitcast.26), calls=%async_computation.1 | async-start | bytes 1081344 | tf_op jit(solution)/shard_map/all_to_all | solution.py:452
  191.5 0.7 fusion.1
  192.1 0.7 fusion
  192.9 6.7 %all-to-all-done.1 = bf16[4,528,128]{2,1,0:T(8,128)(2,1)S(1)} async-done(((bf16[4,528,128]{2,1,0:T(8,128)(2,1)}), bf16[4,528,128]{2,1,0:T(8,128)(2,1)S(1)}, u32[]{:S(2)}, u32[]{:S(2)}) %all-to-all-start.1) | async-done | bytes 540704 | tf_op jit(solution)/shard_map/all_to_all | solution.py:452
  199.6 0.6 copy.41
  200.2 0.8 slice.96
  (101 shorter events, 1.4 us)
Async XLA Ops:
  7.2 2.9 %copy-start.29 = (bf16[4,128]{1,0:T(4,128)(2,1)S(1)}, bf16[4,128]{1,0:T(4,128)(2,1)}, u32[]{:S(2)}) copy-start(bf16[4,128]{1,0:T(4,128)(2,1)} %param.13) | copy-start | bytes 3076
  7.2 3.0 %copy-start.16 = (bf16[2,1024,128]{2,1,0:T(8,128)(2,1)S(1)}, bf16[2,1024,128]{2,1,0:T(8,128)(2,1)}, u32[]{:S(2)}) copy-start(bf16[2,1024,128]{2,1,0:T(8,128)(2,1)} %param.12) | copy-start | bytes 1572868
  7.2 59.3 %all-gather.5.cloned.1.call-start = ((), (), s32[]{:S(2)}) async-start(), calls=%async_computation.2 | async-start | bytes 4456448 | tf_op jit(solution)/shard_map/all_gather | solution.py:415
  10.2 6.0 %copy-start.24 = (f32[4,1,128,128]{3,2,1,0:T(8,128)S(1)}, f32[4,1,128,128]{3,2,1,0:T(8,128)}, u32[]{:S(2)}) copy-start(f32[4,1,128,128]{3,2,1,0:T(8,128)} %param.15) | copy-start | bytes 786436
  10.2 6.0 %copy-start.26 = (f32[128]{0:T(128)S(1)}, f32[128]{0:T(128)}, u32[]{:S(2)}) copy-start(f32[128]{0:T(128)} %param.18) | copy-start | bytes 1540
  10.2 6.1 %copy-start.27 = (f32[128]{0:T(128)S(1)}, f32[128]{0:T(128)}, u32[]{:S(2)}) copy-start(f32[128]{0:T(128)} %param.17) | copy-start | bytes 1540
  11.2 6.5 %copy-start.28 = (s32[2]{0:T(128)S(1)}, s32[2]{0:T(128)}, u32[]{:S(2)}) copy-start(s32[2]{0:T(128)} %param.14) | copy-start | bytes 28
  11.2 13.1 %all-to-all-start = ((bf16[4,528,128]{2,1,0:T(8,128)(2,1)}), bf16[4,528,128]{2,1,0:T(8,128)(2,1)S(1)}, u32[]{:S(2)}, u32[]{:S(2)}) async-start(bf16[4,528,128]{2,1,0:T(8,128)(2,1)} %maximum_maximum_fusion), calls=%async_computation | async-start | bytes 1081344 | tf_op jit(solution)/shard_map/all_to_all | solution.py:405
  16.2 129.1 %all-gather.7.cloned.1.call-start = ((), (), s32[]{:S(2)}) async-start(), calls=%async_computation.3 | async-start | bytes 17842176 | tf_op jit(solution)/shard_map/all_gather | solution.py:429
  16.3 11.0 %collective-permute-start = (f32[258,128]{1,0:T(8,128)S(1)}, f32[258,128]{1,0:T(8,128)S(1)}, u32[]{:S(2)}, u32[]{:S(2)}) collective-permute-start(f32[258,128]{1,0:T(8,128)S(1)} %pad_maximum_fusion.5), channel_id=1, source_target_pairs={{0,8},{8,0},{1,9},{9,1},{2,10},{10,2},{3,11},{11,3},{4,12},{12,4},... | collective-permute-start | bytes 396296 | tf_op jit(solution)/shard_map/ppermute | solution.py:24
  24.5 19.8 %copy-start = (bf16[2,2,66,8,128]{4,3,1,2,0:T(8,128)(2,1)}, bf16[2,2,66,8,128]{4,3,1,2,0:T(8,128)(2,1)S(1)}, u32[]{:S(2)}) copy-start(bf16[2,2,66,8,128]{4,3,1,2,0:T(8,128)(2,1)S(1)} %copy.40) | copy-start | bytes 1622020
  27.3 12.5 %collective-permute-start.1 = (bf16[2,528,256]{2,1,0:T(8,128)(2,1)S(1)}, bf16[2,528,256]{2,1,0:T(8,128)(2,1)S(1)}, u32[]{:S(2)}, u32[]{:S(2)}) collective-permute-start(bf16[2,528,256]{2,1,0:T(8,128)(2,1)S(1)} %bitcast.58), channel_id=1, source_target_pairs={{0,6},{2,0},{4,2},{6,4},{1,7},{3,1},{5,3},{7,5},{8,14},{10,8},{12,... | collective-permute-start | bytes 1622024 | tf_op jit(solution)/shard_map/ppermute | solution.py:24
  30.0 12.9 %collective-permute-start.2 = (bf16[2,528,256]{2,1,0:T(8,128)(2,1)S(1)}, bf16[2,528,256]{2,1,0:T(8,128)(2,1)S(1)}, u32[]{:S(2)}, u32[]{:S(2)}) collective-permute-start(bf16[2,528,256]{2,1,0:T(8,128)(2,1)S(1)} %bitcast.59), channel_id=1, source_target_pairs={{0,2},{2,4},{4,6},{6,0},{1,3},{3,5},{5,7},{7,1},{8,10},{10,12},{12... | collective-permute-start | bytes 1622024 | tf_op jit(solution)/shard_map/ppermute | solution.py:24
  39.8 7.5 %copy-start.5 = (bf16[2,528,256]{2,1,0:T(8,128)(2,1)}, bf16[2,528,256]{2,1,0:T(8,128)(2,1)S(1)}, u32[]{:S(2)}) copy-start(bf16[2,528,256]{2,1,0:T(8,128)(2,1)S(1)} %collective-permute-done.1.xo1) | copy-start | bytes 1622020
  42.9 4.6 %copy-start.6 = (bf16[2,528,256]{2,1,0:T(8,128)(2,1)}, bf16[2,528,256]{2,1,0:T(8,128)(2,1)S(1)}, u32[]{:S(2)}) copy-start(bf16[2,528,256]{2,1,0:T(8,128)(2,1)S(1)} %collective-permute-done.2.xo4) | copy-start | bytes 1622020
  44.3 13.4 %copy-start.15 = (f32[256,704]{0,1:T(8,128)S(1)}, f32[256,704]{0,1:T(8,128)}, u32[]{:S(2)}) copy-start(f32[256,704]{0,1:T(8,128)} %param.21) | copy-start | bytes 2162692
  44.3 13.5 %copy-start.17 = (f32[352,256]{1,0:T(8,128)S(1)}, f32[352,256]{1,0:T(8,128)}, u32[]{:S(2)}) copy-start(f32[352,256]{1,0:T(8,128)} %param.22) | copy-start | bytes 1081348
  44.3 14.6 %collective-permute-start.5 = (bf16[3,2,528,256]{3,2,1,0:T(8,128)(2,1)}, bf16[3,2,528,256]{3,2,1,0:T(8,128)(2,1)S(1)}, u32[]{:S(2)}, u32[]{:S(2)}) collective-permute-start(bf16[3,2,528,256]{3,2,1,0:T(8,128)(2,1)} %pad_maximum_fusion), channel_id=1, source_target_pairs={{0,1},{1,0},{2,3},{3,2},{4,5},{5,4},{6,7},{7,6},{8,9},{9,8},{10,11... | collective-permute-start | bytes 4866056 | tf_op jit(solution)/shard_map/ppermute | solution.py:24
  47.3 8.3 %collective-permute-start.4 = (bf16[1,528,256]{2,1,0:T(8,128)(2,1)S(1)}, bf16[1,528,256]{2,1,0:T(8,128)(2,1)S(1)}, u32[]{:S(2)}, u32[]{:S(2)}) collective-permute-start(bf16[1,528,256]{2,1,0:T(8,128)(2,1)S(1)} %slice.76), channel_id=1, source_target_pairs={{0,6},{2,0},{4,2},{6,4},{1,7},{3,1},{5,3},{7,5},{8,14},{10,8},{12,... | collective-permute-start | bytes 811016 | tf_op jit(solution)/shard_map/ppermute | solution.py:24
  47.6 9.2 %collective-permute-start.3 = (bf16[1,528,256]{2,1,0:T(8,128)(2,1)S(1)}, bf16[1,528,256]{2,1,0:T(8,128)(2,1)S(1)}, u32[]{:S(2)}, u32[]{:S(2)}) collective-permute-start(bf16[1,528,256]{2,1,0:T(8,128)(2,1)S(1)} %slice.90), channel_id=1, source_target_pairs={{0,2},{2,4},{4,6},{6,0},{1,3},{3,5},{5,7},{7,1},{8,10},{10,12},{12... | collective-permute-start | bytes 811016 | tf_op jit(solution)/shard_map/ppermute | solution.py:24
  55.6 3.1 %copy-start.18 = (bf16[1,528,256]{2,1,0:T(8,128)(2,1)}, bf16[1,528,256]{2,1,0:T(8,128)(2,1)S(1)}, u32[]{:S(2)}) copy-start(bf16[1,528,256]{2,1,0:T(8,128)(2,1)S(1)} %collective-permute-done.4.xo3) | copy-start | bytes 811012
  55.6 3.1 %collective-permute-start.7 = (bf16[1,528,256]{2,1,0:T(8,128)(2,1)S(1)}, bf16[1,528,256]{2,1,0:T(8,128)(2,1)S(1)}, u32[]{:S(2)}, u32[]{:S(2)}) collective-permute-start(bf16[1,528,256]{2,1,0:T(8,128)(2,1)S(1)} %collective-permute-done.4.xo3), channel_id=1, source_target_pairs={{0,1},{1,0},{2,3},{3,2},{4,5},{5,4},{6,7},{7,6},{8,9},{9,8},{10,11... | collective-permute-start | bytes 811016 | tf_op jit(solution)/shard_map/ppermute | solution.py:24
  56.7 1.9 copy-start.19
  56.7 2.2 %collective-permute-start.6 = (bf16[1,528,256]{2,1,0:T(8,128)(2,1)S(1)}, bf16[1,528,256]{2,1,0:T(8,128)(2,1)S(1)}, u32[]{:S(2)}, u32[]{:S(2)}) collective-permute-start(bf16[1,528,256]{2,1,0:T(8,128)(2,1)S(1)} %collective-permute-done.3.xo2), channel_id=1, source_target_pairs={{0,1},{1,0},{2,3},{3,2},{4,5},{5,4},{6,7},{7,6},{8,9},{9,8},{10,11... | collective-permute-start | bytes 811016 | tf_op jit(solution)/shard_map/ppermute | solution.py:24
  58.7 10.2 %copy-start.20 = (bf16[1,528,256]{2,1,0:T(8,128)(2,1)}, bf16[1,528,256]{2,1,0:T(8,128)(2,1)S(1)}, u32[]{:S(2)}) copy-start(bf16[1,528,256]{2,1,0:T(8,128)(2,1)S(1)} %collective-permute-done.7.xp3) | copy-start | bytes 811012
  58.9 9.9 %copy-start.21 = (bf16[1,528,256]{2,1,0:T(8,128)(2,1)}, bf16[1,528,256]{2,1,0:T(8,128)(2,1)S(1)}, u32[]{:S(2)}) copy-start(bf16[1,528,256]{2,1,0:T(8,128)(2,1)S(1)} %collective-permute-done.6.xp2) | copy-start | bytes 811012
  58.9 9.9 %copy-start.7 = (bf16[3,2,528,256]{3,2,1,0:T(8,128)(2,1)}, bf16[3,2,528,256]{3,2,1,0:T(8,128)(2,1)S(1)}, u32[]{:S(2)}) copy-start(bf16[3,2,528,256]{3,2,1,0:T(8,128)(2,1)S(1)} %collective-permute-done.5.xpm) | copy-start | bytes 4866052
  68.9 21.7 %collective-permute-start.9 = (bf16[16,128,256]{2,1,0:T(8,128)(2,1)}, bf16[16,128,256]{2,1,0:T(8,128)(2,1)S(1)}, u32[]{:S(2)}, u32[]{:S(2)}) collective-permute-start(bf16[16,128,256]{2,1,0:T(8,128)(2,1)} %slice.91), channel_id=1, source_target_pairs={{0,1},{1,0},{2,3},{3,2},{4,5},{5,4},{6,7},{7,6},{8,9},{9,8},{10,11... | collective-permute-start | bytes 3145736 | tf_op jit(solution)/shard_map/ppermute | solution.py:24
  88.7 1.8 collective-permute-start.8
  90.5 0.7 copy-start.10
  90.5 1.0 copy-start.4
  94.7 9.4 %collective-permute-start.10 = (bf16[1,528,256]{2,1,0:T(8,128)(2,1)}, bf16[1,528,256]{2,1,0:T(8,128)(2,1)S(1)}, u32[]{:S(2)}, u32[]{:S(2)}) collective-permute-start(bf16[1,528,256]{2,1,0:T(8,128)(2,1)} %get-tuple-element.43), channel_id=1, source_target_pairs={{0,2},{2,4},{4,6},{6,0},{1,3},{3,5},{5,7},{7,1},{8,10},{10,12},{12... | collective-permute-start | bytes 811016 | tf_op jit(solution)/shard_map/ppermute | solution.py:24
  96.0 8.2 %collective-permute-start.11 = (bf16[1,528,256]{2,1,0:T(8,128)(2,1)}, bf16[1,528,256]{2,1,0:T(8,128)(2,1)S(1)}, u32[]{:S(2)}, u32[]{:S(2)}) collective-permute-start(bf16[1,528,256]{2,1,0:T(8,128)(2,1)} %get-tuple-element.44), channel_id=1, source_target_pairs={{0,6},{2,0},{4,2},{6,4},{1,7},{3,1},{5,3},{7,5},{8,14},{10,8},{12,... | collective-permute-start | bytes 811016 | tf_op jit(solution)/shard_map/ppermute | solution.py:24
  102.0 4.4 %copy-start.13 = (f32[2,528,256]{2,1,0:T(8,128)S(1)}, f32[2,528,256]{2,1,0:T(8,128)}, u32[]{:S(2)}) copy-start(f32[2,528,256]{2,1,0:T(8,128)} %get-tuple-element.49) | copy-start | bytes 3244036
  105.5 2.9 %copy-start.30 = (f32[3,128,128]{2,1,0:T(8,128)S(1)}, f32[3,128,128]{2,1,0:T(8,128)}, u32[]{:S(2)}) copy-start(f32[3,128,128]{2,1,0:T(8,128)} %get-tuple-element.51) | copy-start | bytes 589828
  105.5 14.2 %copy-start.1 = (bf16[2,2,66,8,128]{4,3,1,2,0:T(8,128)(2,1)S(1)}, bf16[2,2,66,8,128]{4,3,1,2,0:T(8,128)(2,1)}, u32[]{:S(2)}) copy-start(bf16[2,2,66,8,128]{4,3,1,2,0:T(8,128)(2,1)} %copy-done) | copy-start | bytes 1622020
  105.5 14.2 %copy-start.11 = (f32[2,528,256]{2,1,0:T(8,128)S(1)}, f32[2,528,256]{2,1,0:T(8,128)}, u32[]{:S(2)}) copy-start(f32[2,528,256]{2,1,0:T(8,128)} %get-tuple-element.46) | copy-start | bytes 3244036
  105.5 14.2 %collective-permute-start.12 = (bf16[2,528,256]{2,1,0:T(8,128)(2,1)S(1)}, bf16[2,528,256]{2,1,0:T(8,128)(2,1)S(1)}, u32[]{:S(2)}, u32[]{:S(2)}) collective-permute-start(bf16[2,528,256]{2,1,0:T(8,128)(2,1)S(1)} %add_convert_fusion.5), channel_id=1, source_target_pairs={{0,2},{2,4},{4,6},{6,0},{1,3},{3,5},{5,7},{7,1},{8,10},{10,12},{12... | collective-permute-start | bytes 1622024 | tf_op jit(solution)/shard_map/ppermute | solution.py:24
  106.5 13.2 %collective-permute-start.13 = (bf16[2,528,256]{2,1,0:T(8,128)(2,1)S(1)}, bf16[2,528,256]{2,1,0:T(8,128)(2,1)S(1)}, u32[]{:S(2)}, u32[]{:S(2)}) collective-permute-start(bf16[2,528,256]{2,1,0:T(8,128)(2,1)S(1)} %add_convert_fusion.4), channel_id=1, source_target_pairs={{0,6},{2,0},{4,2},{6,4},{1,7},{3,1},{5,3},{7,5},{8,14},{10,8},{12,... | collective-permute-start | bytes 1622024 | tf_op jit(solution)/shard_map/ppermute | solution.py:24
  108.4 10.6 %collective-permute-start.14 = (f32[3,128,128]{2,1,0:T(8,128)S(1)}, f32[3,128,128]{2,1,0:T(8,128)S(1)}, u32[]{:S(2)}, u32[]{:S(2)}) collective-permute-start(f32[3,128,128]{2,1,0:T(8,128)S(1)} %copy-done.30), channel_id=1, source_target_pairs={{0,8},{8,0},{1,9},{9,1},{2,10},{10,2},{3,11},{11,3},{4,12},{12,4},... | collective-permute-start | bytes 589832 | tf_op jit(solution)/shard_map/ppermute | solution.py:24
  120.0 25.3 %copy-start.2 = (bf16[2,528,256]{2,1,0:T(8,128)(2,1)}, bf16[2,528,256]{2,1,0:T(8,128)(2,1)S(1)}, u32[]{:S(2)}) copy-start(bf16[2,528,256]{2,1,0:T(8,128)(2,1)S(1)} %add_convert_fusion.3.x0) | copy-start | bytes 1622020
  120.0 13.6 %collective-permute-start.16 = (bf16[2,528,256]{2,1,0:T(8,128)(2,1)S(1)}, bf16[2,528,256]{2,1,0:T(8,128)(2,1)S(1)}, u32[]{:S(2)}, u32[]{:S(2)}) collective-permute-start(bf16[2,528,256]{2,1,0:T(8,128)(2,1)S(1)} %add_convert_fusion.3.x0), channel_id=1, source_target_pairs={{0,2},{2,4},{4,6},{6,0},{1,3},{3,5},{5,7},{7,1},{8,10},{10,12},{12... | collective-permute-start | bytes 1622024 | tf_op jit(solution)/shard_map/ppermute | solution.py:24
  120.4 13.3 %collective-permute-start.15 = (bf16[2,528,256]{2,1,0:T(8,128)(2,1)S(1)}, bf16[2,528,256]{2,1,0:T(8,128)(2,1)S(1)}, u32[]{:S(2)}, u32[]{:S(2)}) collective-permute-start(bf16[2,528,256]{2,1,0:T(8,128)(2,1)S(1)} %add_convert_fusion.3.x0), channel_id=1, source_target_pairs={{0,6},{2,0},{4,2},{6,4},{1,7},{3,1},{5,3},{7,5},{8,14},{10,8},{12,... | collective-permute-start | bytes 1622024 | tf_op jit(solution)/shard_map/ppermute | solution.py:24
  133.6 11.8 %copy-start.8 = (bf16[2,528,256]{2,1,0:T(8,128)(2,1)}, bf16[2,528,256]{2,1,0:T(8,128)(2,1)S(1)}, u32[]{:S(2)}) copy-start(bf16[2,528,256]{2,1,0:T(8,128)(2,1)S(1)} %collective-permute-done.16.x4) | copy-start | bytes 1622020
  133.6 6.9 %collective-permute-start.17 = (bf16[1,528,256]{2,1,0:T(8,128)(2,1)S(1)}, bf16[1,528,256]{2,1,0:T(8,128)(2,1)S(1)}, u32[]{:S(2)}, u32[]{:S(2)}) collective-permute-start(bf16[1,528,256]{2,1,0:T(8,128)(2,1)S(1)} %slice.92), channel_id=1, source_target_pairs={{0,2},{2,4},{4,6},{6,0},{1,3},{3,5},{5,7},{7,1},{8,10},{10,12},{12... | collective-permute-start | bytes 811016 | tf_op jit(solution)/shard_map/ppermute | solution.py:24
  133.7 11.6 %copy-start.9 = (bf16[2,528,256]{2,1,0:T(8,128)(2,1)}, bf16[2,528,256]{2,1,0:T(8,128)(2,1)S(1)}, u32[]{:S(2)}) copy-start(bf16[2,528,256]{2,1,0:T(8,128)(2,1)S(1)} %collective-permute-done.15.x1) | copy-start | bytes 1622020
  133.7 6.8 %collective-permute-start.18 = (bf16[1,528,256]{2,1,0:T(8,128)(2,1)S(1)}, bf16[1,528,256]{2,1,0:T(8,128)(2,1)S(1)}, u32[]{:S(2)}, u32[]{:S(2)}) collective-permute-start(bf16[1,528,256]{2,1,0:T(8,128)(2,1)S(1)} %slice.93), channel_id=1, source_target_pairs={{0,6},{2,0},{4,2},{6,4},{1,7},{3,1},{5,3},{7,5},{8,14},{10,8},{12,... | collective-permute-start | bytes 811016 | tf_op jit(solution)/shard_map/ppermute | solution.py:24
  140.5 4.9 %copy-start.22 = (bf16[1,528,256]{2,1,0:T(8,128)(2,1)}, bf16[1,528,256]{2,1,0:T(8,128)(2,1)S(1)}, u32[]{:S(2)}) copy-start(bf16[1,528,256]{2,1,0:T(8,128)(2,1)S(1)} %collective-permute-done.17.x2) | copy-start | bytes 811012
  140.5 4.9 %copy-start.23 = (bf16[1,528,256]{2,1,0:T(8,128)(2,1)}, bf16[1,528,256]{2,1,0:T(8,128)(2,1)S(1)}, u32[]{:S(2)}) copy-start(bf16[1,528,256]{2,1,0:T(8,128)(2,1)S(1)} %collective-permute-done.18.x3) | copy-start | bytes 811012
  159.0 10.4 %collective-permute-start.19 = (bf16[1,528,256]{2,1,0:T(8,128)(2,1)}, bf16[1,528,256]{2,1,0:T(8,128)(2,1)S(1)}, u32[]{:S(2)}, u32[]{:S(2)}) collective-permute-start(bf16[1,528,256]{2,1,0:T(8,128)(2,1)} %get-tuple-element.57), channel_id=1, source_target_pairs={{0,2},{2,4},{4,6},{6,0},{1,3},{3,5},{5,7},{7,1},{8,10},{10,12},{12... | collective-permute-start | bytes 811016 | tf_op jit(solution)/shard_map/ppermute | solution.py:24
  160.2 9.1 %collective-permute-start.20 = (bf16[1,528,256]{2,1,0:T(8,128)(2,1)}, bf16[1,528,256]{2,1,0:T(8,128)(2,1)S(1)}, u32[]{:S(2)}, u32[]{:S(2)}) collective-permute-start(bf16[1,528,256]{2,1,0:T(8,128)(2,1)} %get-tuple-element.58), channel_id=1, source_target_pairs={{0,6},{2,0},{4,2},{6,4},{1,7},{3,1},{5,3},{7,5},{8,14},{10,8},{12,... | collective-permute-start | bytes 811016 | tf_op jit(solution)/shard_map/ppermute | solution.py:24
  169.3 1.6 copy-start.14
  170.8 2.9 %copy-start.25 = (f32[3,128,128]{2,1,0:T(8,128)S(1)}, f32[3,128,128]{2,1,0:T(8,128)}, u32[]{:S(2)}) copy-start(f32[3,128,128]{2,1,0:T(8,128)} %get-tuple-element.63) | copy-start | bytes 589828
  170.8 14.3 %collective-permute-start.21 = (bf16[2,528,256]{2,1,0:T(8,128)(2,1)S(1)}, bf16[2,528,256]{2,1,0:T(8,128)(2,1)S(1)}, u32[]{:S(2)}, u32[]{:S(2)}) collective-permute-start(bf16[2,528,256]{2,1,0:T(8,128)(2,1)S(1)} %add_convert_fusion.2), channel_id=1, source_target_pairs={{0,2},{2,4},{4,6},{6,0},{1,3},{3,5},{5,7},{7,1},{8,10},{10,12},{12... | collective-permute-start | bytes 1622024 | tf_op jit(solution)/shard_map/ppermute | solution.py:24
  170.9 14.2 %copy-start.3 = (bf16[2,528,256]{2,1,0:T(8,128)(2,1)S(1)}, bf16[2,528,256]{2,1,0:T(8,128)(2,1)}, u32[]{:S(2)}) copy-start(bf16[2,528,256]{2,1,0:T(8,128)(2,1)} %copy-done.2) | copy-start | bytes 1622020
  170.9 14.2 %copy-start.12 = (f32[2,528,256]{2,1,0:T(8,128)S(1)}, f32[2,528,256]{2,1,0:T(8,128)}, u32[]{:S(2)}) copy-start(f32[2,528,256]{2,1,0:T(8,128)} %get-tuple-element.55) | copy-start | bytes 3244036
  171.0 14.1 %collective-permute-start.22 = (bf16[2,528,256]{2,1,0:T(8,128)(2,1)S(1)}, bf16[2,528,256]{2,1,0:T(8,128)(2,1)S(1)}, u32[]{:S(2)}, u32[]{:S(2)}) collective-permute-start(bf16[2,528,256]{2,1,0:T(8,128)(2,1)S(1)} %add_convert_fusion.1), channel_id=1, source_target_pairs={{0,6},{2,0},{4,2},{6,4},{1,7},{3,1},{5,3},{7,5},{8,14},{10,8},{12,... | collective-permute-start | bytes 1622024 | tf_op jit(solution)/shard_map/ppermute | solution.py:24
  186.3 13.3 %all-to-all-start.1 = ((bf16[4,528,128]{2,1,0:T(8,128)(2,1)}), bf16[4,528,128]{2,1,0:T(8,128)(2,1)S(1)}, u32[]{:S(2)}, u32[]{:S(2)}) async-start(bf16[4,528,128]{2,1,0:T(8,128)(2,1)} %bitcast.26), calls=%async_computation.1 | async-start | bytes 1081344 | tf_op jit(solution)/shard_map/all_to_all | solution.py:452
Sparse Core Ops, SparseCore 0:
  10.7 55.7 all-gather.4
  68.7 76.5 all-gather.6

commit v5 on v4

--- a/solution.py
+++ b/solution.py
@@ -283,8 +283,10 @@
     return out
 
 
-def down_dots(steps, x, hid, wd, outs):
+def down_dots(steps, x, hid, wd, outs, started):
     for slot, s, z, r in blocks_of(steps, x):
+        for cp in started[slot * 4 : slot * 4 + 4]:
+            cp.wait()
         total = dot_nn(hid[0], wd[slot, 0:704, :]) + dot_nn(hid[1], wd[slot, 704:1408, :])
         put(steps, outs, s, z, total)
 
@@ -318,9 +320,7 @@
         gate = dot_nt(xcat[...], wg[cc, 0])
         up = dot_nt(xcat[...], wg[cc, 1])
         hid[cc] = (gate / (1.0 + jnp.exp(-gate)) * up).astype(BF)
-    for cp in last:
-        cp.wait()
-    down_dots((2,), x, hid, wd, (q0, q1))
+    down_dots((2,), x, hid, wd, (q0, q1), last)
 
 
 def mlp_call(idx, xs, w, gain):
@@ -342,9 +342,8 @@
 
 
 def down_kernel(steps, idx, hid, w_ref, p0, p1, p2, wd, sems):
-    for cp in copy_all(down_copies(steps, idx[3], w_ref, wd), sems):
-        cp.wait()
-    down_dots(steps, idx[3], hid, wd, (p0, p1, p2))
+    started = copy_all(down_copies(steps, idx[3], w_ref, wd), sems)
+    down_dots(steps, idx[3], hid, wd, (p0, p1, p2), started)
 
 
 def down_call(steps, idx, hid, w):

time: 208 us -> 211 us (1.014)
  Pallas kernels: 48 us -> 51 us
    pallas_call x1, Pallas kernels: 7.59 us -> 9.77 us  [down_call(): pl.pallas_call(functools.partial(down_kernel, steps), out_shape=shapes_of...]
where the time goes in v5:
time: 211 us
  waiting for transfers between devices  85.1 us (40%)
  Pallas kernels  51 us (24%)
  starting transfers between devices  39.4 us (19%)
  between operations  15.7 us (7%)
  other arithmetic  12 us (6%)
  local copies, waits for them, and re-layouts  7.71 us (4%)
    ppermute x23, waiting for transfers between devices, shift(): return lax.ppermute(value, axis, [(i, (i + step) % n) for i in range(n)])  61.7 us
    ppermute x23, starting transfers between devices, shift(): return lax.ppermute(value, axis, [(i, (i + step) % n) for i in range(n)])  29.3 us
    pallas_call x1, Pallas kernels, mix_call(): pl.pallas_call(mix_kernel, out_shape=(jax.ShapeDtypeStruct((HALF, 256), B...  19.1 us
    pallas_call x1, Pallas kernels, mlp_call(): pl.pallas_call(mlp_kernel, out_shape=(jax.ShapeDtypeStruct((2, HALF, 704)...  14.5 us
    pallas_call x1, Pallas kernels, down_call(): pl.pallas_call(functools.partial(down_kernel, steps), out_shape=shapes_of...  9.77 us
    pallas_call x2, Pallas kernels, out_call(): pl.pallas_call(functools.partial(out_kernel, steps), out_shape=shapes_of(...  7.67 us
    all_gather x1, waiting for transfers between devices, on_device(): early = lax.all_gather(early, ('y', 'zh', 'zl')).reshape(16, 512, 256)  7.56 us
    all_to_all x1, waiting for transfers between devices, on_device(): back = lax.all_to_all(layer, ('zl', 'c'), 0, 0, tiled=True)  6.74 us
  transfers between devices with their start and end apart: 27, of which 17 were waited for; matrix products, arithmetic and copies ran while one was open for 6% of the time, Pallas kernels for 17%

profile of v5, /device:TPU:1, one launch (start us, length us, event | category | flops | bytes accessed | tf_op | source)
XLA Modules:
  0.0 210.9 jit_solution(9113915867623740674)
XLA Ops:
  7.2 1.2 copy.33
  8.4 0.9 convert_element_type.54
  9.3 0.7 pad_maximum_fusion.4
  10.2 1.0 maximum_maximum_fusion
  11.2 5.0 %all-to-all-start = ((bf16[4,528,128]{2,1,0:T(8,128)(2,1)}), bf16[4,528,128]{2,1,0:T(8,128)(2,1)S(1)}, u32[]{:S(2)}, u32[]{:S(2)}) async-start(bf16[4,528,128]{2,1,0:T(8,128)(2,1)} %maximum_maximum_fusion), calls=%async_computation | async-start | bytes 1081344 | tf_op jit(solution)/shard_map/all_to_all | solution.py:404
  16.3 1.5 collective-permute-start
  17.7 0.6 fusion.4
  19.5 0.7 stack.70.idx
  20.2 4.2 %all-to-all-done = bf16[4,528,128]{2,1,0:T(8,128)(2,1)S(1)} async-done(((bf16[4,528,128]{2,1,0:T(8,128)(2,1)}), bf16[4,528,128]{2,1,0:T(8,128)(2,1)S(1)}, u32[]{:S(2)}, u32[]{:S(2)}) %all-to-all-start) | async-done | bytes 540704 | tf_op jit(solution)/shard_map/all_to_all | solution.py:404
  24.5 2.8 %collective-permute-done = f32[258,128]{1,0:T(8,128)S(1)} collective-permute-done((f32[258,128]{1,0:T(8,128)S(1)}, f32[258,128]{1,0:T(8,128)S(1)}, u32[]{:S(2)}, u32[]{:S(2)}) %collective-permute-start) | collective-permute-done | bytes 132128 | tf_op jit(solution)/shard_map/ppermute | solution.py:24
  27.3 2.7 %collective-permute-start.1 = (bf16[2,528,256]{2,1,0:T(8,128)(2,1)S(1)}, bf16[2,528,256]{2,1,0:T(8,128)(2,1)S(1)}, u32[]{:S(2)}, u32[]{:S(2)}) collective-permute-start(bf16[2,528,256]{2,1,0:T(8,128)(2,1)S(1)} %bitcast.58), channel_id=1, source_target_pairs={{0,6},{2,0},{4,2},{6,4},{1,7},{3,1},{5,3},{7,5},{8,14},{10,8},{12,... | collective-permute-start | bytes 1622024 | tf_op jit(solution)/shard_map/ppermute | solution.py:24
  30.0 0.6 pad_maximum_fusion.6
  30.6 0.7 pad_maximum_fusion.3.dst_ref
  31.3 8.4 %collective-permute-done.1.xo1 = bf16[2,528,256]{2,1,0:T(8,128)(2,1)S(1)} collective-permute-done((bf16[2,528,256]{2,1,0:T(8,128)(2,1)S(1)}, bf16[2,528,256]{2,1,0:T(8,128)(2,1)S(1)}, u32[]{:S(2)}, u32[]{:S(2)}) %collective-permute-start.1) | collective-permute-done | bytes 540704 | tf_op jit(solution)/shard_map/ppermute | solution.py:24
  39.8 3.1 %collective-permute-done.2.xo4 = bf16[2,528,256]{2,1,0:T(8,128)(2,1)S(1)} collective-permute-done((bf16[2,528,256]{2,1,0:T(8,128)(2,1)S(1)}, bf16[2,528,256]{2,1,0:T(8,128)(2,1)S(1)}, u32[]{:S(2)}, u32[]{:S(2)}) %collective-permute-start.2) | collective-permute-done | bytes 540704 | tf_op jit(solution)/shard_map/ppermute | solution.py:24
  42.9 1.4 pad_maximum_fusion
  44.3 3.0 %collective-permute-start.5 = (bf16[3,2,528,256]{3,2,1,0:T(8,128)(2,1)}, bf16[3,2,528,256]{3,2,1,0:T(8,128)(2,1)S(1)}, u32[]{:S(2)}, u32[]{:S(2)}) collective-permute-start(bf16[3,2,528,256]{3,2,1,0:T(8,128)(2,1)} %pad_maximum_fusion), channel_id=1, source_target_pairs={{0,1},{1,0},{2,3},{3,2},{4,5},{5,4},{6,7},{7,6},{8,9},{9,8},{10,11... | collective-permute-start | bytes 4866056 | tf_op jit(solution)/shard_map/ppermute | solution.py:24
  47.6 1.4 collective-permute-start.3
  48.9 6.6 %collective-permute-done.4.xo3 = bf16[1,528,256]{2,1,0:T(8,128)(2,1)S(1)} collective-permute-done((bf16[1,528,256]{2,1,0:T(8,128)(2,1)S(1)}, bf16[1,528,256]{2,1,0:T(8,128)(2,1)S(1)}, u32[]{:S(2)}, u32[]{:S(2)}) %collective-permute-start.4) | collective-permute-done | bytes 270368 | tf_op jit(solution)/shard_map/ppermute | solution.py:24
  55.6 0.7 collective-permute-start.7
  56.3 0.4 collective-permute-done.3.xo2
  56.7 1.0 collective-permute-start.6
  57.8 0.8 pad_maximum_fusion.1
  58.7 0.2 collective-permute-done.6.xp2
  58.9 7.6 %all-gather.5.cloned.1.call-done = bf16[8192,256]{1,0:T(8,128)(2,1)} async-done(((bf16[512,256]{1,0:T(8,128)(2,1)}), bf16[8192,256]{1,0:T(8,128)(2,1)}) %all-gather.5.cloned.1.call-update) | async-done | bytes 4194320 | tf_op jit(solution)/shard_map/all_gather | solution.py:414
  66.5 2.3 %slice.91 = bf16[16,128,256]{2,1,0:T(8,128)(2,1)} slice(bf16[16,512,256]{2,1,0:T(8,128)(2,1)} %bitcast.54), slice={[0:16], [384:512], [0:256]} | slice | bytes 2097152 | tf_op jit(solution)/shard_map/slice | solution.py:425
  68.9 0.8 collective-permute-start.9
  69.6 19.1 %mix.1 = (bf16[528,256]{1,0:T(8,128)(2,1)}, bf16[528,256]{1,0:T(8,128)(2,1)}, f32[3,128,128]{2,1,0:T(8,128)}, f32[3,128,128]{2,1,0:T(8,128)}) custom-call(s32[6]{0:T(128)} %stack.70.idx, bf16[2,528,256]{2,1,0:T(8,128)(2,1)} %bitcast.61, bf16[2,528,256]{2,1,0:T(8,128)(2,1)} %copy-done.5, bf16[1,528,256]{2,1,0:T(8,128)(2,1)} %copy-done.19, ...), custom_call_target="tpu_custom_call" | custom-call | flops 24 | bytes 24 | tf_op jit(solution)/shard_map/mix/pallas_call | solution.py:198
  88.8 1.7 collective-permute-done.8.b_ref
  90.5 0.7 copy-done.10
  91.2 0.3 copy-done.4
  91.6 3.1 %outp.2 = (bf16[1,528,256]{2,1,0:T(8,128)(2,1)}, bf16[1,528,256]{2,1,0:T(8,128)(2,1)}) custom-call(s32[6]{0:T(128)} %stack.70.idx, bf16[528,256]{1,0:T(8,128)(2,1)} %get-tuple-element.45.a_ref, bf16[528,256]{1,0:T(8,128)(2,1)} %copy-done.10, bf16[16,512,256]{2,1,0:T(8,128)(2,1)} %bitcast.56, bf16[16,128,256]{2,1,0:T(8,128)(2,1)} %copy-done.4), custom_call_target="tpu_custom_call" | custom-call | flops 2 | bytes 2 | tf_op jit(solution)/shard_map/outp/pallas_call | solution.py:260
  94.7 1.3 collective-permute-start.10
  96.0 1.5 collective-permute-start.11
  97.5 4.5 %outp.3 = (f32[2,528,256]{2,1,0:T(8,128)}, f32[2,528,256]{2,1,0:T(8,128)}, f32[2,528,256]{2,1,0:T(8,128)}) custom-call(s32[6]{0:T(128)} %stack.70.idx, bf16[528,256]{1,0:T(8,128)(2,1)} %get-tuple-element.45.a_ref, bf16[528,256]{1,0:T(8,128)(2,1)} %copy-done.10, bf16[16,512,256]{2,1,0:T(8,128)(2,1)} %bitcast.57, bf16[16,128,256]{2,1,0:T(8,128)(2,1)} %copy-done.4), custom_call_target="tpu_custom_call" | custom-call | flops 6 | bytes 6 | tf_op jit(solution)/shard_map/outp/pallas_call | solution.py:260
  102.0 2.1 %collective-permute-done.10 = bf16[1,528,256]{2,1,0:T(8,128)(2,1)S(1)} collective-permute-done((bf16[1,528,256]{2,1,0:T(8,128)(2,1)}, bf16[1,528,256]{2,1,0:T(8,128)(2,1)S(1)}, u32[]{:S(2)}, u32[]{:S(2)}) %collective-permute-start.10) | collective-permute-done | bytes 270368 | tf_op jit(solution)/shard_map/ppermute | solution.py:24
  104.1 1.3 add_convert_fusion.5
  105.5 0.9 collective-permute-start.12
  106.5 1.9 collective-permute-start.13
  108.4 1.1 collective-permute-start.14
  109.5 9.5 %collective-permute-done.14 = f32[3,128,128]{2,1,0:T(8,128)S(1)} collective-permute-done((f32[3,128,128]{2,1,0:T(8,128)S(1)}, f32[3,128,128]{2,1,0:T(8,128)S(1)}, u32[]{:S(2)}, u32[]{:S(2)}) %collective-permute-start.14) | collective-permute-done | bytes 196640 | tf_op jit(solution)/shard_map/ppermute | solution.py:24
  119.0 0.7 collective-permute-done.12
  119.7 0.2 add_convert_fusion.3.x0
  120.0 0.4 collective-permute-start.16
  120.4 2.5 %collective-permute-start.15 = (bf16[2,528,256]{2,1,0:T(8,128)(2,1)S(1)}, bf16[2,528,256]{2,1,0:T(8,128)(2,1)S(1)}, u32[]{:S(2)}, u32[]{:S(2)}) collective-permute-start(bf16[2,528,256]{2,1,0:T(8,128)(2,1)S(1)} %add_convert_fusion.3.x0), channel_id=1, source_target_pairs={{0,6},{2,0},{4,2},{6,4},{1,7},{3,1},{5,3},{7,5},{8,14},{10,8},{12,... | collective-permute-start | bytes 1622024 | tf_op jit(solution)/shard_map/ppermute | solution.py:24
  122.9 10.6 %collective-permute-done.16.x4 = bf16[2,528,256]{2,1,0:T(8,128)(2,1)S(1)} collective-permute-done((bf16[2,528,256]{2,1,0:T(8,128)(2,1)S(1)}, bf16[2,528,256]{2,1,0:T(8,128)(2,1)S(1)}, u32[]{:S(2)}, u32[]{:S(2)}) %collective-permute-start.16) | collective-permute-done | bytes 540704 | tf_op jit(solution)/shard_map/ppermute | solution.py:24
  133.7 2.7 %collective-permute-start.18 = (bf16[1,528,256]{2,1,0:T(8,128)(2,1)S(1)}, bf16[1,528,256]{2,1,0:T(8,128)(2,1)S(1)}, u32[]{:S(2)}, u32[]{:S(2)}) collective-permute-start(bf16[1,528,256]{2,1,0:T(8,128)(2,1)S(1)} %slice.93), channel_id=1, source_target_pairs={{0,6},{2,0},{4,2},{6,4},{1,7},{3,1},{5,3},{7,5},{8,14},{10,8},{12,... | collective-permute-start | bytes 811016 | tf_op jit(solution)/shard_map/ppermute | solution.py:24
  136.4 4.0 %collective-permute-done.17.x2 = bf16[1,528,256]{2,1,0:T(8,128)(2,1)S(1)} collective-permute-done((bf16[1,528,256]{2,1,0:T(8,128)(2,1)S(1)}, bf16[1,528,256]{2,1,0:T(8,128)(2,1)S(1)}, u32[]{:S(2)}, u32[]{:S(2)}) %collective-permute-start.17) | collective-permute-done | bytes 270368 | tf_op jit(solution)/shard_map/ppermute | solution.py:24
  140.5 4.8 %all-gather.7.cloned.1.call-done = bf16[33792,256]{1,0:T(8,128)(2,1)} async-done(((bf16[1056,256]{1,0:T(8,128)(2,1)}), bf16[33792,256]{1,0:T(8,128)(2,1)}) %all-gather.7.cloned.1.call-update) | async-done | bytes 17301520 | tf_op jit(solution)/shard_map/all_gather | solution.py:428
  145.3 14.5 %mlp.1 = (bf16[2,528,704]{2,1,0:T(8,128)(2,1)}, bf16[1,528,256]{2,1,0:T(8,128)(2,1)}, bf16[1,528,256]{2,1,0:T(8,128)(2,1)}) custom-call(s32[6]{0:T(128)} %stack.70.idx, bf16[2,528,256]{2,1,0:T(8,128)(2,1)} %copy-done.2, bf16[2,528,256]{2,1,0:T(8,128)(2,1)} %copy-done.9, bf16[1,528,256]{2,1,0:T(8,128)(2,1)} %copy-done.22, bf16[1,528,256]{2,1,0:T(8,128)(2,1)} %copy-done.23, ...), custom_call_target="tpu_custom_call" | custom-call | flops 16 | bytes 16 | tf_op jit(solution)/shard_map/mlp/pallas_call | solution.py:327
  159.9 1.3 collective-permute-start.19
  161.1 1.5 collective-permute-start.20
  162.6 9.8 %down.1 = (f32[2,528,256]{2,1,0:T(8,128)}, f32[2,528,256]{2,1,0:T(8,128)}, f32[2,528,256]{2,1,0:T(8,128)}) custom-call(s32[6]{0:T(128)} %stack.70.idx, bf16[2,528,704]{2,1,0:T(8,128)(2,1)} %get-tuple-element.54.hid, bf16[16,2,1056,256]{3,2,1,0:T(8,128)(2,1)} %bitcast.53), custom_call_target="tpu_custom_call" | custom-call | flops 5 | bytes 5 | tf_op jit(solution)/shard_map/down/pallas_call | solution.py:351
  172.4 1.4 add_convert_fusion.2
  174.0 2.7 %collective-permute-start.22 = (bf16[2,528,256]{2,1,0:T(8,128)(2,1)S(1)}, bf16[2,528,256]{2,1,0:T(8,128)(2,1)S(1)}, u32[]{:S(2)}, u32[]{:S(2)}) collective-permute-start(bf16[2,528,256]{2,1,0:T(8,128)(2,1)S(1)} %add_convert_fusion.1), channel_id=1, source_target_pairs={{0,6},{2,0},{4,2},{6,4},{1,7},{3,1},{5,3},{7,5},{8,14},{10,8},{12,... | collective-permute-start | bytes 1622024 | tf_op jit(solution)/shard_map/ppermute | solution.py:24
  176.8 11.3 %collective-permute-done.21 = bf16[2,528,256]{2,1,0:T(8,128)(2,1)S(1)} collective-permute-done((bf16[2,528,256]{2,1,0:T(8,128)(2,1)S(1)}, bf16[2,528,256]{2,1,0:T(8,128)(2,1)S(1)}, u32[]{:S(2)}, u32[]{:S(2)}) %collective-permute-start.21) | collective-permute-done | bytes 540704 | tf_op jit(solution)/shard_map/ppermute | solution.py:24
  188.1 0.2 add_convert_fusion
  188.5 0.9 pad_maximum_fusion.2
  189.4 5.1 %all-to-all-start.1 = ((bf16[4,528,128]{2,1,0:T(8,128)(2,1)}), bf16[4,528,128]{2,1,0:T(8,128)(2,1)S(1)}, u32[]{:S(2)}, u32[]{:S(2)}) async-start(bf16[4,528,128]{2,1,0:T(8,128)(2,1)} %bitcast.26), calls=%async_computation.1 | async-start | bytes 1081344 | tf_op jit(solution)/shard_map/all_to_all | solution.py:451
  194.5 0.7 fusion.1
  195.2 0.7 fusion
  195.9 6.7 %all-to-all-done.1 = bf16[4,528,128]{2,1,0:T(8,128)(2,1)S(1)} async-done(((bf16[4,528,128]{2,1,0:T(8,128)(2,1)}), bf16[4,528,128]{2,1,0:T(8,128)(2,1)S(1)}, u32[]{:S(2)}, u32[]{:S(2)}) %all-to-all-start.1) | async-done | bytes 540704 | tf_op jit(solution)/shard_map/all_to_all | solution.py:451
  202.7 0.6 copy.41
  203.2 0.8 slice.96
  (101 shorter events, 1.4 us)
Async XLA Ops:
  7.2 2.9 %copy-start.29 = (bf16[4,128]{1,0:T(4,128)(2,1)S(1)}, bf16[4,128]{1,0:T(4,128)(2,1)}, u32[]{:S(2)}) copy-start(bf16[4,128]{1,0:T(4,128)(2,1)} %param.13) | copy-start | bytes 3076
  7.2 3.0 %copy-start.16 = (bf16[2,1024,128]{2,1,0:T(8,128)(2,1)S(1)}, bf16[2,1024,128]{2,1,0:T(8,128)(2,1)}, u32[]{:S(2)}) copy-start(bf16[2,1024,128]{2,1,0:T(8,128)(2,1)} %param.12) | copy-start | bytes 1572868
  7.2 59.3 %all-gather.5.cloned.1.call-start = ((), (), s32[]{:S(2)}) async-start(), calls=%async_computation.2 | async-start | bytes 4456448 | tf_op jit(solution)/shard_map/all_gather | solution.py:414
  10.2 6.0 %copy-start.24 = (f32[4,1,128,128]{3,2,1,0:T(8,128)S(1)}, f32[4,1,128,128]{3,2,1,0:T(8,128)}, u32[]{:S(2)}) copy-start(f32[4,1,128,128]{3,2,1,0:T(8,128)} %param.15) | copy-start | bytes 786436
  10.2 6.0 %copy-start.26 = (f32[128]{0:T(128)S(1)}, f32[128]{0:T(128)}, u32[]{:S(2)}) copy-start(f32[128]{0:T(128)} %param.18) | copy-start | bytes 1540
  10.2 6.1 %copy-start.27 = (f32[128]{0:T(128)S(1)}, f32[128]{0:T(128)}, u32[]{:S(2)}) copy-start(f32[128]{0:T(128)} %param.17) | copy-start | bytes 1540
  11.2 6.5 %copy-start.28 = (s32[2]{0:T(128)S(1)}, s32[2]{0:T(128)}, u32[]{:S(2)}) copy-start(s32[2]{0:T(128)} %param.14) | copy-start | bytes 28
  11.2 13.1 %all-to-all-start = ((bf16[4,528,128]{2,1,0:T(8,128)(2,1)}), bf16[4,528,128]{2,1,0:T(8,128)(2,1)S(1)}, u32[]{:S(2)}, u32[]{:S(2)}) async-start(bf16[4,528,128]{2,1,0:T(8,128)(2,1)} %maximum_maximum_fusion), calls=%async_computation | async-start | bytes 1081344 | tf_op jit(solution)/shard_map/all_to_all | solution.py:404
  16.2 129.1 %all-gather.7.cloned.1.call-start = ((), (), s32[]{:S(2)}) async-start(), calls=%async_computation.3 | async-start | bytes 17842176 | tf_op jit(solution)/shard_map/all_gather | solution.py:428
  16.3 11.0 %collective-permute-start = (f32[258,128]{1,0:T(8,128)S(1)}, f32[258,128]{1,0:T(8,128)S(1)}, u32[]{:S(2)}, u32[]{:S(2)}) collective-permute-start(f32[258,128]{1,0:T(8,128)S(1)} %pad_maximum_fusion.5), channel_id=1, source_target_pairs={{0,8},{8,0},{1,9},{9,1},{2,10},{10,2},{3,11},{11,3},{4,12},{12,4},... | collective-permute-start | bytes 396296 | tf_op jit(solution)/shard_map/ppermute | solution.py:24
  24.5 19.8 %copy-start = (bf16[2,2,66,8,128]{4,3,1,2,0:T(8,128)(2,1)}, bf16[2,2,66,8,128]{4,3,1,2,0:T(8,128)(2,1)S(1)}, u32[]{:S(2)}) copy-start(bf16[2,2,66,8,128]{4,3,1,2,0:T(8,128)(2,1)S(1)} %copy.40) | copy-start | bytes 1622020
  27.3 12.5 %collective-permute-start.1 = (bf16[2,528,256]{2,1,0:T(8,128)(2,1)S(1)}, bf16[2,528,256]{2,1,0:T(8,128)(2,1)S(1)}, u32[]{:S(2)}, u32[]{:S(2)}) collective-permute-start(bf16[2,528,256]{2,1,0:T(8,128)(2,1)S(1)} %bitcast.58), channel_id=1, source_target_pairs={{0,6},{2,0},{4,2},{6,4},{1,7},{3,1},{5,3},{7,5},{8,14},{10,8},{12,... | collective-permute-start | bytes 1622024 | tf_op jit(solution)/shard_map/ppermute | solution.py:24
  30.0 12.9 %collective-permute-start.2 = (bf16[2,528,256]{2,1,0:T(8,128)(2,1)S(1)}, bf16[2,528,256]{2,1,0:T(8,128)(2,1)S(1)}, u32[]{:S(2)}, u32[]{:S(2)}) collective-permute-start(bf16[2,528,256]{2,1,0:T(8,128)(2,1)S(1)} %bitcast.59), channel_id=1, source_target_pairs={{0,2},{2,4},{4,6},{6,0},{1,3},{3,5},{5,7},{7,1},{8,10},{10,12},{12... | collective-permute-start | bytes 1622024 | tf_op jit(solution)/shard_map/ppermute | solution.py:24
  39.8 7.5 %copy-start.5 = (bf16[2,528,256]{2,1,0:T(8,128)(2,1)}, bf16[2,528,256]{2,1,0:T(8,128)(2,1)S(1)}, u32[]{:S(2)}) copy-start(bf16[2,528,256]{2,1,0:T(8,128)(2,1)S(1)} %collective-permute-done.1.xo1) | copy-start | bytes 1622020
  42.9 4.6 %copy-start.6 = (bf16[2,528,256]{2,1,0:T(8,128)(2,1)}, bf16[2,528,256]{2,1,0:T(8,128)(2,1)S(1)}, u32[]{:S(2)}) copy-start(bf16[2,528,256]{2,1,0:T(8,128)(2,1)S(1)} %collective-permute-done.2.xo4) | copy-start | bytes 1622020
  44.3 13.4 %copy-start.15 = (f32[256,704]{0,1:T(8,128)S(1)}, f32[256,704]{0,1:T(8,128)}, u32[]{:S(2)}) copy-start(f32[256,704]{0,1:T(8,128)} %param.21) | copy-start | bytes 2162692
  44.3 13.5 %copy-start.17 = (f32[352,256]{1,0:T(8,128)S(1)}, f32[352,256]{1,0:T(8,128)}, u32[]{:S(2)}) copy-start(f32[352,256]{1,0:T(8,128)} %param.22) | copy-start | bytes 1081348
  44.3 14.6 %collective-permute-start.5 = (bf16[3,2,528,256]{3,2,1,0:T(8,128)(2,1)}, bf16[3,2,528,256]{3,2,1,0:T(8,128)(2,1)S(1)}, u32[]{:S(2)}, u32[]{:S(2)}) collective-permute-start(bf16[3,2,528,256]{3,2,1,0:T(8,128)(2,1)} %pad_maximum_fusion), channel_id=1, source_target_pairs={{0,1},{1,0},{2,3},{3,2},{4,5},{5,4},{6,7},{7,6},{8,9},{9,8},{10,11... | collective-permute-start | bytes 4866056 | tf_op jit(solution)/shard_map/ppermute | solution.py:24
  47.3 8.3 %collective-permute-start.4 = (bf16[1,528,256]{2,1,0:T(8,128)(2,1)S(1)}, bf16[1,528,256]{2,1,0:T(8,128)(2,1)S(1)}, u32[]{:S(2)}, u32[]{:S(2)}) collective-permute-start(bf16[1,528,256]{2,1,0:T(8,128)(2,1)S(1)} %slice.76), channel_id=1, source_target_pairs={{0,6},{2,0},{4,2},{6,4},{1,7},{3,1},{5,3},{7,5},{8,14},{10,8},{12,... | collective-permute-start | bytes 811016 | tf_op jit(solution)/shard_map/ppermute | solution.py:24
  47.6 9.2 %collective-permute-start.3 = (bf16[1,528,256]{2,1,0:T(8,128)(2,1)S(1)}, bf16[1,528,256]{2,1,0:T(8,128)(2,1)S(1)}, u32[]{:S(2)}, u32[]{:S(2)}) collective-permute-start(bf16[1,528,256]{2,1,0:T(8,128)(2,1)S(1)} %slice.90), channel_id=1, source_target_pairs={{0,2},{2,4},{4,6},{6,0},{1,3},{3,5},{5,7},{7,1},{8,10},{10,12},{12... | collective-permute-start | bytes 811016 | tf_op jit(solution)/shard_map/ppermute | solution.py:24
  55.6 3.1 %copy-start.18 = (bf16[1,528,256]{2,1,0:T(8,128)(2,1)}, bf16[1,528,256]{2,1,0:T(8,128)(2,1)S(1)}, u32[]{:S(2)}) copy-start(bf16[1,528,256]{2,1,0:T(8,128)(2,1)S(1)} %collective-permute-done.4.xo3) | copy-start | bytes 811012
  55.6 3.1 %collective-permute-start.7 = (bf16[1,528,256]{2,1,0:T(8,128)(2,1)S(1)}, bf16[1,528,256]{2,1,0:T(8,128)(2,1)S(1)}, u32[]{:S(2)}, u32[]{:S(2)}) collective-permute-start(bf16[1,528,256]{2,1,0:T(8,128)(2,1)S(1)} %collective-permute-done.4.xo3), channel_id=1, source_target_pairs={{0,1},{1,0},{2,3},{3,2},{4,5},{5,4},{6,7},{7,6},{8,9},{9,8},{10,11... | collective-permute-start | bytes 811016 | tf_op jit(solution)/shard_map/ppermute | solution.py:24
  56.7 1.9 copy-start.19
  56.7 2.2 %collective-permute-start.6 = (bf16[1,528,256]{2,1,0:T(8,128)(2,1)S(1)}, bf16[1,528,256]{2,1,0:T(8,128)(2,1)S(1)}, u32[]{:S(2)}, u32[]{:S(2)}) collective-permute-start(bf16[1,528,256]{2,1,0:T(8,128)(2,1)S(1)} %collective-permute-done.3.xo2), channel_id=1, source_target_pairs={{0,1},{1,0},{2,3},{3,2},{4,5},{5,4},{6,7},{7,6},{8,9},{9,8},{10,11... | collective-permute-start | bytes 811016 | tf_op jit(solution)/shard_map/ppermute | solution.py:24
  58.7 10.2 %copy-start.20 = (bf16[1,528,256]{2,1,0:T(8,128)(2,1)}, bf16[1,528,256]{2,1,0:T(8,128)(2,1)S(1)}, u32[]{:S(2)}) copy-start(bf16[1,528,256]{2,1,0:T(8,128)(2,1)S(1)} %collective-permute-done.7.xp3) | copy-start | bytes 811012
  58.9 9.9 %copy-start.21 = (bf16[1,528,256]{2,1,0:T(8,128)(2,1)}, bf16[1,528,256]{2,1,0:T(8,128)(2,1)S(1)}, u32[]{:S(2)}) copy-start(bf16[1,528,256]{2,1,0:T(8,128)(2,1)S(1)} %collective-permute-done.6.xp2) | copy-start | bytes 811012
  58.9 9.9 %copy-start.7 = (bf16[3,2,528,256]{3,2,1,0:T(8,128)(2,1)}, bf16[3,2,528,256]{3,2,1,0:T(8,128)(2,1)S(1)}, u32[]{:S(2)}) copy-start(bf16[3,2,528,256]{3,2,1,0:T(8,128)(2,1)S(1)} %collective-permute-done.5.xpm) | copy-start | bytes 4866052
  68.9 21.7 %collective-permute-start.9 = (bf16[16,128,256]{2,1,0:T(8,128)(2,1)}, bf16[16,128,256]{2,1,0:T(8,128)(2,1)S(1)}, u32[]{:S(2)}, u32[]{:S(2)}) collective-permute-start(bf16[16,128,256]{2,1,0:T(8,128)(2,1)} %slice.91), channel_id=1, source_target_pairs={{0,1},{1,0},{2,3},{3,2},{4,5},{5,4},{6,7},{7,6},{8,9},{9,8},{10,11... | collective-permute-start | bytes 3145736 | tf_op jit(solution)/shard_map/ppermute | solution.py:24
  88.7 1.8 collective-permute-start.8
  90.5 0.7 copy-start.10
  90.5 1.0 copy-start.4
  94.7 9.4 %collective-permute-start.10 = (bf16[1,528,256]{2,1,0:T(8,128)(2,1)}, bf16[1,528,256]{2,1,0:T(8,128)(2,1)S(1)}, u32[]{:S(2)}, u32[]{:S(2)}) collective-permute-start(bf16[1,528,256]{2,1,0:T(8,128)(2,1)} %get-tuple-element.43), channel_id=1, source_target_pairs={{0,2},{2,4},{4,6},{6,0},{1,3},{3,5},{5,7},{7,1},{8,10},{10,12},{12... | collective-permute-start | bytes 811016 | tf_op jit(solution)/shard_map/ppermute | solution.py:24
  96.0 8.2 %collective-permute-start.11 = (bf16[1,528,256]{2,1,0:T(8,128)(2,1)}, bf16[1,528,256]{2,1,0:T(8,128)(2,1)S(1)}, u32[]{:S(2)}, u32[]{:S(2)}) collective-permute-start(bf16[1,528,256]{2,1,0:T(8,128)(2,1)} %get-tuple-element.44), channel_id=1, source_target_pairs={{0,6},{2,0},{4,2},{6,4},{1,7},{3,1},{5,3},{7,5},{8,14},{10,8},{12,... | collective-permute-start | bytes 811016 | tf_op jit(solution)/shard_map/ppermute | solution.py:24
  102.0 4.4 %copy-start.13 = (f32[2,528,256]{2,1,0:T(8,128)S(1)}, f32[2,528,256]{2,1,0:T(8,128)}, u32[]{:S(2)}) copy-start(f32[2,528,256]{2,1,0:T(8,128)} %get-tuple-element.49) | copy-start | bytes 3244036
  105.5 2.9 %copy-start.30 = (f32[3,128,128]{2,1,0:T(8,128)S(1)}, f32[3,128,128]{2,1,0:T(8,128)}, u32[]{:S(2)}) copy-start(f32[3,128,128]{2,1,0:T(8,128)} %get-tuple-element.51) | copy-start | bytes 589828
  105.5 14.2 %copy-start.1 = (bf16[2,2,66,8,128]{4,3,1,2,0:T(8,128)(2,1)S(1)}, bf16[2,2,66,8,128]{4,3,1,2,0:T(8,128)(2,1)}, u32[]{:S(2)}) copy-start(bf16[2,2,66,8,128]{4,3,1,2,0:T(8,128)(2,1)} %copy-done) | copy-start | bytes 1622020
  105.5 14.2 %copy-start.11 = (f32[2,528,256]{2,1,0:T(8,128)S(1)}, f32[2,528,256]{2,1,0:T(8,128)}, u32[]{:S(2)}) copy-start(f32[2,528,256]{2,1,0:T(8,128)} %get-tuple-element.46) | copy-start | bytes 3244036
  105.5 14.2 %collective-permute-start.12 = (bf16[2,528,256]{2,1,0:T(8,128)(2,1)S(1)}, bf16[2,528,256]{2,1,0:T(8,128)(2,1)S(1)}, u32[]{:S(2)}, u32[]{:S(2)}) collective-permute-start(bf16[2,528,256]{2,1,0:T(8,128)(2,1)S(1)} %add_convert_fusion.5), channel_id=1, source_target_pairs={{0,2},{2,4},{4,6},{6,0},{1,3},{3,5},{5,7},{7,1},{8,10},{10,12},{12... | collective-permute-start | bytes 1622024 | tf_op jit(solution)/shard_map/ppermute | solution.py:24
  106.5 13.2 %collective-permute-start.13 = (bf16[2,528,256]{2,1,0:T(8,128)(2,1)S(1)}, bf16[2,528,256]{2,1,0:T(8,128)(2,1)S(1)}, u32[]{:S(2)}, u32[]{:S(2)}) collective-permute-start(bf16[2,528,256]{2,1,0:T(8,128)(2,1)S(1)} %add_convert_fusion.4), channel_id=1, source_target_pairs={{0,6},{2,0},{4,2},{6,4},{1,7},{3,1},{5,3},{7,5},{8,14},{10,8},{12,... | collective-permute-start | bytes 1622024 | tf_op jit(solution)/shard_map/ppermute | solution.py:24
  108.4 10.6 %collective-permute-start.14 = (f32[3,128,128]{2,1,0:T(8,128)S(1)}, f32[3,128,128]{2,1,0:T(8,128)S(1)}, u32[]{:S(2)}, u32[]{:S(2)}) collective-permute-start(f32[3,128,128]{2,1,0:T(8,128)S(1)} %copy-done.30), channel_id=1, source_target_pairs={{0,8},{8,0},{1,9},{9,1},{2,10},{10,2},{3,11},{11,3},{4,12},{12,4},... | collective-permute-start | bytes 589832 | tf_op jit(solution)/shard_map/ppermute | solution.py:24
  120.0 25.3 %copy-start.2 = (bf16[2,528,256]{2,1,0:T(8,128)(2,1)}, bf16[2,528,256]{2,1,0:T(8,128)(2,1)S(1)}, u32[]{:S(2)}) copy-start(bf16[2,528,256]{2,1,0:T(8,128)(2,1)S(1)} %add_convert_fusion.3.x0) | copy-start | bytes 1622020
  120.0 13.6 %collective-permute-start.16 = (bf16[2,528,256]{2,1,0:T(8,128)(2,1)S(1)}, bf16[2,528,256]{2,1,0:T(8,128)(2,1)S(1)}, u32[]{:S(2)}, u32[]{:S(2)}) collective-permute-start(bf16[2,528,256]{2,1,0:T(8,128)(2,1)S(1)} %add_convert_fusion.3.x0), channel_id=1, source_target_pairs={{0,2},{2,4},{4,6},{6,0},{1,3},{3,5},{5,7},{7,1},{8,10},{10,12},{12... | collective-permute-start | bytes 1622024 | tf_op jit(solution)/shard_map/ppermute | solution.py:24
  120.4 13.3 %collective-permute-start.15 = (bf16[2,528,256]{2,1,0:T(8,128)(2,1)S(1)}, bf16[2,528,256]{2,1,0:T(8,128)(2,1)S(1)}, u32[]{:S(2)}, u32[]{:S(2)}) collective-permute-start(bf16[2,528,256]{2,1,0:T(8,128)(2,1)S(1)} %add_convert_fusion.3.x0), channel_id=1, source_target_pairs={{0,6},{2,0},{4,2},{6,4},{1,7},{3,1},{5,3},{7,5},{8,14},{10,8},{12,... | collective-permute-start | bytes 1622024 | tf_op jit(solution)/shard_map/ppermute | solution.py:24
  133.6 11.8 %copy-start.8 = (bf16[2,528,256]{2,1,0:T(8,128)(2,1)}, bf16[2,528,256]{2,1,0:T(8,128)(2,1)S(1)}, u32[]{:S(2)}) copy-start(bf16[2,528,256]{2,1,0:T(8,128)(2,1)S(1)} %collective-permute-done.16.x4) | copy-start | bytes 1622020
  133.6 6.9 %collective-permute-start.17 = (bf16[1,528,256]{2,1,0:T(8,128)(2,1)S(1)}, bf16[1,528,256]{2,1,0:T(8,128)(2,1)S(1)}, u32[]{:S(2)}, u32[]{:S(2)}) collective-permute-start(bf16[1,528,256]{2,1,0:T(8,128)(2,1)S(1)} %slice.92), channel_id=1, source_target_pairs={{0,2},{2,4},{4,6},{6,0},{1,3},{3,5},{5,7},{7,1},{8,10},{10,12},{12... | collective-permute-start | bytes 811016 | tf_op jit(solution)/shard_map/ppermute | solution.py:24
  133.7 11.6 %copy-start.9 = (bf16[2,528,256]{2,1,0:T(8,128)(2,1)}, bf16[2,528,256]{2,1,0:T(8,128)(2,1)S(1)}, u32[]{:S(2)}) copy-start(bf16[2,528,256]{2,1,0:T(8,128)(2,1)S(1)} %collective-permute-done.15.x1) | copy-start | bytes 1622020
  133.7 6.8 %collective-permute-start.18 = (bf16[1,528,256]{2,1,0:T(8,128)(2,1)S(1)}, bf16[1,528,256]{2,1,0:T(8,128)(2,1)S(1)}, u32[]{:S(2)}, u32[]{:S(2)}) collective-permute-start(bf16[1,528,256]{2,1,0:T(8,128)(2,1)S(1)} %slice.93), channel_id=1, source_target_pairs={{0,6},{2,0},{4,2},{6,4},{1,7},{3,1},{5,3},{7,5},{8,14},{10,8},{12,... | collective-permute-start | bytes 811016 | tf_op jit(solution)/shard_map/ppermute | solution.py:24
  140.5 4.9 %copy-start.22 = (bf16[1,528,256]{2,1,0:T(8,128)(2,1)}, bf16[1,528,256]{2,1,0:T(8,128)(2,1)S(1)}, u32[]{:S(2)}) copy-start(bf16[1,528,256]{2,1,0:T(8,128)(2,1)S(1)} %collective-permute-done.17.x2) | copy-start | bytes 811012
  140.5 4.9 %copy-start.23 = (bf16[1,528,256]{2,1,0:T(8,128)(2,1)}, bf16[1,528,256]{2,1,0:T(8,128)(2,1)S(1)}, u32[]{:S(2)}) copy-start(bf16[1,528,256]{2,1,0:T(8,128)(2,1)S(1)} %collective-permute-done.18.x3) | copy-start | bytes 811012
  159.9 12.5 %collective-permute-start.19 = (bf16[1,528,256]{2,1,0:T(8,128)(2,1)}, bf16[1,528,256]{2,1,0:T(8,128)(2,1)S(1)}, u32[]{:S(2)}, u32[]{:S(2)}) collective-permute-start(bf16[1,528,256]{2,1,0:T(8,128)(2,1)} %get-tuple-element.57), channel_id=1, source_target_pairs={{0,2},{2,4},{4,6},{6,0},{1,3},{3,5},{5,7},{7,1},{8,10},{10,12},{12... | collective-permute-start | bytes 811016 | tf_op jit(solution)/shard_map/ppermute | solution.py:24
  161.1 11.3 %collective-permute-start.20 = (bf16[1,528,256]{2,1,0:T(8,128)(2,1)}, bf16[1,528,256]{2,1,0:T(8,128)(2,1)S(1)}, u32[]{:S(2)}, u32[]{:S(2)}) collective-permute-start(bf16[1,528,256]{2,1,0:T(8,128)(2,1)} %get-tuple-element.58), channel_id=1, source_target_pairs={{0,6},{2,0},{4,2},{6,4},{1,7},{3,1},{5,3},{7,5},{8,14},{10,8},{12,... | collective-permute-start | bytes 811016 | tf_op jit(solution)/shard_map/ppermute | solution.py:24
  172.4 1.6 copy-start.14
  173.8 2.9 %copy-start.25 = (f32[3,128,128]{2,1,0:T(8,128)S(1)}, f32[3,128,128]{2,1,0:T(8,128)}, u32[]{:S(2)}) copy-start(f32[3,128,128]{2,1,0:T(8,128)} %get-tuple-element.63) | copy-start | bytes 589828
  173.8 14.3 %collective-permute-start.21 = (bf16[2,528,256]{2,1,0:T(8,128)(2,1)S(1)}, bf16[2,528,256]{2,1,0:T(8,128)(2,1)S(1)}, u32[]{:S(2)}, u32[]{:S(2)}) collective-permute-start(bf16[2,528,256]{2,1,0:T(8,128)(2,1)S(1)} %add_convert_fusion.2), channel_id=1, source_target_pairs={{0,2},{2,4},{4,6},{6,0},{1,3},{3,5},{5,7},{7,1},{8,10},{10,12},{12... | collective-permute-start | bytes 1622024 | tf_op jit(solution)/shard_map/ppermute | solution.py:24
  173.9 14.2 %copy-start.3 = (bf16[2,528,256]{2,1,0:T(8,128)(2,1)S(1)}, bf16[2,528,256]{2,1,0:T(8,128)(2,1)}, u32[]{:S(2)}) copy-start(bf16[2,528,256]{2,1,0:T(8,128)(2,1)} %copy-done.2) | copy-start | bytes 1622020
  174.0 14.2 %copy-start.12 = (f32[2,528,256]{2,1,0:T(8,128)S(1)}, f32[2,528,256]{2,1,0:T(8,128)}, u32[]{:S(2)}) copy-start(f32[2,528,256]{2,1,0:T(8,128)} %get-tuple-element.55) | copy-start | bytes 3244036
  174.0 14.1 %collective-permute-start.22 = (bf16[2,528,256]{2,1,0:T(8,128)(2,1)S(1)}, bf16[2,528,256]{2,1,0:T(8,128)(2,1)S(1)}, u32[]{:S(2)}, u32[]{:S(2)}) collective-permute-start(bf16[2,528,256]{2,1,0:T(8,128)(2,1)S(1)} %add_convert_fusion.1), channel_id=1, source_target_pairs={{0,6},{2,0},{4,2},{6,4},{1,7},{3,1},{5,3},{7,5},{8,14},{10,8},{12,... | collective-permute-start | bytes 1622024 | tf_op jit(solution)/shard_map/ppermute | solution.py:24
  189.4 13.3 %all-to-all-start.1 = ((bf16[4,528,128]{2,1,0:T(8,128)(2,1)}), bf16[4,528,128]{2,1,0:T(8,128)(2,1)S(1)}, u32[]{:S(2)}, u32[]{:S(2)}) async-start(bf16[4,528,128]{2,1,0:T(8,128)(2,1)} %bitcast.26), calls=%async_computation.1 | async-start | bytes 1081344 | tf_op jit(solution)/shard_map/all_to_all | solution.py:451
Sparse Core Ops, SparseCore 0:
  10.7 55.7 all-gather.4
  68.7 76.5 all-gather.6
